TPU v7x, 512 devices: a whole 4x4x16 slice. The times are simulated.
512 devices in a mesh: prow: 16 (over y_hi, x, core), pcol: 32 (over y_lo, z).
Axes of the slice: x: 4, y: 4 (y_hi: 2, y_lo: 2; y = y_hi * 2 + y_lo), z: 16, core: 2. Of those that a mesh axis runs over, the one named last changes fastest.
Arguments:
- ancestor_inverse: float32 [8192, 8192], P('prow', 'pcol'), may hold values from -6 to 6
- block_mask: int32 [32, 32], replicated, may hold values 0 or 1
- block_ids: int32 [32], replicated, may hold values from 0 to 31, each once
- row_lists: int32 [4, 16], replicated, may hold values from 0 to 31, as said below
- panels: float32 [8192, 512], P(('prow', 'pcol')), may hold values from -0.109375 to 0.109375
- diag_inverse: float32 [4, 128, 128], replicated, may hold values from -6 to 6
Outputs:
- inverse_panels: float32 [8192, 512], P(('prow', 'pcol'))
- diag_blocks: float32 [4, 128, 128], replicated
Inputs may be any that keep to these rules, and one draw needn't show every extreme that they name: `row_lists`: each row names 16 different ancestor blocks.
All inputs are finite; a program needn't handle non-finite values.
Results may differ from a plain program's by a relative error of at most 0.0003.
Values sent between devices are 32-bit elements; how exact they have to be, the bound alone decides.
No kernel may reach another device: no remote copies, remote signals or barrier semaphores. Data moves between devices by JAX's collectives and lax.ppermute only.
A program may use at most 64 MiB of HBM per device.

v0:
```python
import jax
import jax.numpy as jnp
from jax import lax
from jax.sharding import PartitionSpec as P

BLK = 256
W = 128
S = 4


def from_root(block, axis, source):
    block = jnp.where(lax.axis_index(axis) == source, block, jnp.zeros_like(block))
    return lax.psum(block, axis)


def local(ancestor_inverse, block_mask, block_ids, row_lists, panels, diag_inverse):
    row_devices = lax.axis_size("prow")
    col_devices = lax.axis_size("pcol")
    col_ratio = col_devices // row_devices
    prow_index = lax.axis_index("prow")
    pcol_index = lax.axis_index("pcol")
    row_count = panels.shape[0]
    block_total = block_ids.shape[0]
    row_span = ancestor_inverse.shape[0]
    col_span = ancestor_inverse.shape[1]
    active_blocks = jnp.any(block_ids[:, None, None] == row_lists[None, :, :], axis=2).astype(
        jnp.float32
    )
    flat_index = prow_index * col_devices + pcol_index
    own_rows = flat_index * row_count + jnp.arange(row_count, dtype=jnp.int32)
    picker = (own_rows[:, None] // BLK == jnp.arange(block_total, dtype=jnp.int32)[None, :]).astype(
        jnp.float32
    )
    own_keep = jnp.repeat(
        jnp.dot(picker, active_blocks, preferred_element_type=jnp.float32), W, axis=1
    )
    active_own = panels * own_keep
    rowset = lax.all_gather(active_own, "pcol", axis=0, tiled=True)
    wanted_rows = lax.dynamic_slice_in_dim(rowset, pcol_index % col_ratio * col_span, col_span, 0)
    needed = from_root(wanted_rows, "prow", pcol_index // col_ratio)
    block_rows = row_span // BLK
    block_cols = col_span // BLK
    local_mask = lax.dynamic_slice(
        block_mask, (prow_index * block_rows, pcol_index * block_cols), (block_rows, block_cols)
    ).astype(jnp.float32)
    masked_local = (
        ancestor_inverse.reshape(block_rows, BLK, block_cols, BLK) * local_mask[:, None, :, None]
    ).reshape(row_span, col_span)
    partial_value = jnp.dot(
        masked_local, needed, precision=lax.Precision.HIGHEST, preferred_element_type=jnp.float32
    )
    summed = lax.psum_scatter(partial_value, "pcol", scatter_dimension=0, tiled=True)
    inverse_panels = -(own_keep * summed)
    local_diag = jnp.einsum(
        "isa,isb->sab",
        active_own.reshape(row_count, S, W),
        inverse_panels.reshape(row_count, S, W),
        precision=lax.Precision.HIGHEST,
    )
    diag_total = lax.psum(local_diag, ("prow", "pcol"))
    return (inverse_panels, diag_inverse - diag_total)


def solution(mesh):
    placed = (P("prow", "pcol"), P(), P(), P(), P(("prow", "pcol"), None), P())
    return jax.shard_map(
        local,
        mesh=mesh,
        in_specs=placed,
        out_specs=(P(("prow", "pcol"), None), P()),
        check_vma=False,
    )
```

profile of v0, /device:TPU:1, one launch (start us, length us, event | category | flops | bytes accessed | tf_op | source)
XLA Modules:
  0.0 910.7 jit_solution(8119235764452468029)
XLA Ops:
  7.2 0.0 all-gather.2.cloned.1.call-start
  7.2 0.0 copy-start.5
  7.2 0.0 copy-start.6
  7.3 0.6 copy-done.5
  7.9 0.0 copy-done.6
  7.9 0.1 compare_reduce_fusion
  8.0 0.2 fusion.9
  8.2 0.0 copy-start.4
  8.2 0.1 broadcast_in_dim.4
  8.3 0.7 copy-done.4
  8.9 0.6 bitcast_multiply_fusion.1
  9.6 0.0 all-gather.2.cloned.1.call-update
  9.6 0.0 all-reduce.3.cloned.1.call-start
  9.7 115.5 %all-gather.2.cloned.1.call-done = f32[512,512]{1,0:T(8,128)} async-done(((f32[16,512]{1,0:T(8,128)}), f32[512,512]{1,0:T(8,128)}) %all-gather.2.cloned.1.call-update) | async-done | bytes 1048592 | tf_op jit(solution)/shard_map/all_gather | solution.py:38
  125.2 1.9 dynamic-slice_select_fusion
  127.1 0.0 copy-start
  127.1 0.0 all-reduce.3.cloned.1.call-update
  127.1 0.0 reduce-scatter.2.cloned.1.call-start
  127.2 0.9 convert_reduce_fusion
  128.1 0.1 broadcast_bitcast_fusion
  128.2 170.5 %all-reduce.3.cloned.1.call-done = f32[256,512]{1,0:T(8,128)} async-done(((f32[256,512]{1,0:T(8,128)}), f32[256,512]{1,0:T(8,128)}) %all-reduce.3.cloned.1.call-update) | async-done | bytes 524304 | tf_op jit(solution)/shard_map/psum | solution.py:13
  298.7 0.0 copy-done
  298.7 3.0 fusion
  301.7 0.0 reduce-scatter.2.cloned.1.call-update
  301.8 0.0 copy-start.1
  301.8 0.0 all-reduce.5.cloned.1.call-start
  301.8 115.4 %reduce-scatter.2.cloned.1.call-done = f32[16,512]{1,0:T(8,128)} async-done(((f32[512,512]{1,0:T(8,128)}), f32[16,512]{1,0:T(8,128)}) %reduce-scatter.2.cloned.1.call-update) | async-done | bytes 32784 | tf_op jit(solution)/shard_map/reduce_scatter | solution.py:52
  417.2 0.8 fusion.3
  417.9 0.0 copy-done.1
  417.9 0.0 copy-start.3
  417.9 0.0 copy-start.2
  418.0 1.3 fusion.4
  419.3 0.0 copy-done.3
  419.3 0.0 all-reduce.5.cloned.1.call-update
  419.3 483.2 %all-reduce.5.cloned.1.call-done = f32[4,128,128]{2,1,0:T(8,128)} async-done(((f32[4,128,128]{2,1,0:T(8,128)}), f32[4,128,128]{2,1,0:T(8,128)}) %all-reduce.5.cloned.1.call-update) | async-done | bytes 262160 | tf_op jit(solution)/shard_map/psum | solution.py:60
  902.5 0.0 copy-done.2
  902.5 1.7 sub.13
  (2 shorter events, 0.0 us)
Async XLA Ops:
  7.2 118.1 %all-gather.2.cloned.1.call-start = ((), (), s32[]{:S(2)}) async-start(), calls=%async_computation.1 | async-start | bytes 1081344 | tf_op jit(solution)/shard_map/all_gather | solution.py:38
  7.2 0.7 copy-start.5
  7.2 0.7 copy-start.6
  8.2 0.8 copy-start.4
  9.6 289.1 %all-reduce.3.cloned.1.call-start = ((), (), s32[]{:S(2)}) async-start(), calls=%async_computation.2 | async-start | bytes 1048576 | tf_op jit(solution)/shard_map/psum | solution.py:13
  127.1 171.6 %copy-start = (f32[512,256]{1,0:T(8,128)S(1)}, f32[512,256]{1,0:T(8,128)}, u32[]{:S(2)}) copy-start(f32[512,256]{1,0:T(8,128)} %param.6) | copy-start | bytes 1572868
  127.1 290.0 %reduce-scatter.2.cloned.1.call-start = ((), (), s32[]{:S(2)}) async-start(), calls=%async_computation.3 | async-start | bytes 1081344 | tf_op jit(solution)/shard_map/reduce_scatter | solution.py:52
  301.8 116.2 %copy-start.1 = (f32[16,512]{1,0:T(8,128)S(1)}, f32[16,512]{1,0:T(8,128)}, u32[]{:S(2)}) copy-start(f32[16,512]{1,0:T(8,128)} %bitcast_multiply_fusion.1) | copy-start | bytes 98308
  301.8 600.7 %all-reduce.5.cloned.1.call-start = ((), (), s32[]{:S(2)}) async-start(), calls=%async_computation.4 | async-start | bytes 524288 | tf_op jit(solution)/shard_map/psum | solution.py:60
  417.9 1.3 copy-start.3
  417.9 484.5 %copy-start.2 = (f32[4,128,128]{2,1,0:T(8,128)S(1)}, f32[4,128,128]{2,1,0:T(8,128)}, u32[]{:S(2)}) copy-start(f32[4,128,128]{2,1,0:T(8,128)} %param.11) | copy-start | bytes 786436
Sparse Core Ops, SparseCore 0:
  10.6 114.5 all-gather.1
  128.1 170.5 all-reduce.2
  301.9 115.2 reduce-scatter.1
  423.0 479.3 all-reduce.4
where the time goes:
time: 912 us; the launch traced here: 911 us
  waiting for transfers between devices  885 us (97%)
  between operations  13.9 us (2%)
    psum x1, waiting for transfers between devices, local(): diag_total = lax.psum(local_diag, ('prow', 'pcol'))  483 us
    psum x1, waiting for transfers between devices, from_root(): return lax.psum(block, axis)  171 us
    all_gather x1, waiting for transfers between devices, local(): rowset = lax.all_gather(active_own, 'pcol', axis=0, tiled=True)  116 us
    reduce_scatter x1, waiting for transfers between devices, local(): lax.psum_scatter(partial_value, 'pcol', scatter_dimension=0, tiled=True)  115 us
  transfers between devices with their start and end apart: 4, of which 4 were waited for; matrix products, arithmetic and copies ran while one was open for 0% of the time, Pallas kernels for 0%

commit v1 on v0

v1 whole, which is shorter than its diff:
```python
import jax
import jax.numpy as jnp
from jax import lax
from jax.sharding import Mesh
from jax.sharding import PartitionSpec as P

BLK = 256
W = 128
S = 4
ROW = ("yh", "x", "c")
COL = ("yl", "z")
PLANE = ("yh", "x", "c", "yl")
ALL = ("yh", "x", "c", "yl", "z")


def exchange(value, axis, groups=None):
    return lax.all_to_all(value, axis, 0, 0, tiled=True, axis_index_groups=groups)


def spread(value, axis, count):
    copies = jnp.broadcast_to(value[None], (count,) + value.shape)
    return lax.all_to_all(copies, axis, 0, 0, tiled=True)


def local(ancestor_inverse, block_mask, block_ids, row_lists, panels, diag_inverse):
    rows = lax.axis_size(ROW)
    cols = lax.axis_size(COL)
    depth = lax.axis_size("z")
    halves = lax.axis_size("yl")
    plane = rows * halves
    prow_index = lax.axis_index(ROW)
    pcol_index = lax.axis_index(COL)
    row_count, width = panels.shape
    block_total = block_ids.shape[0]
    row_span, col_span = ancestor_inverse.shape
    active_blocks = jnp.any(
        block_ids[:, None, None] == row_lists[None, :, :], axis=2
    ).astype(jnp.float32)
    own_block = (prow_index * cols + pcol_index) * row_count // BLK
    own_active = lax.dynamic_slice_in_dim(active_blocks, own_block, 1, 0)
    own_keep = jnp.repeat(own_active, W, axis=1)
    active_own = panels * own_keep

    chunks = col_span // row_count
    pairs = [(q * chunks + j, j * cols + q) for q in range(cols) for j in range(chunks)]
    moved = lax.ppermute(active_own, ALL, pairs)
    needed = spread(moved, ROW, rows).reshape(col_span, width)

    block_rows = row_span // BLK
    local_mask = lax.dynamic_slice(
        block_mask, (prow_index * block_rows, pcol_index), (block_rows, 1)
    ).astype(jnp.float32)
    masked = (ancestor_inverse.reshape(block_rows, BLK, col_span) * local_mask[:, :, None]).reshape(
        row_span, col_span
    )
    pair = 2
    deep = depth // pair
    masked = (
        masked.reshape(halves, deep, pair, row_count, col_span)
        .transpose(0, 2, 1, 3, 4)
        .reshape(row_span, col_span)
    )
    partial_value = jnp.dot(
        masked, needed, precision=lax.Precision.HIGHEST, preferred_element_type=jnp.float32
    )
    near = [
        [h * depth + z * pair + m for h in range(halves) for m in range(pair)] for z in range(deep)
    ]
    far = [[z * pair + m for z in range(deep)] for m in range(pair)]
    first = exchange(partial_value, COL, near)
    first = jnp.sum(first.reshape(halves * pair, deep * row_count, width), axis=0)
    second = exchange(first, "z", far)
    summed = jnp.sum(second.reshape(deep, row_count, width), axis=0)
    inverse_panels = -(own_keep * summed)

    local_diag = jnp.einsum(
        "isa,isb->sab",
        active_own.reshape(row_count, S, W),
        inverse_panels.reshape(row_count, S, W),
        precision=lax.Precision.HIGHEST,
    )
    part = S * W // plane
    terms = exchange(local_diag.reshape(S * W, W), PLANE)
    terms = jnp.sum(terms.reshape(plane, part, W), axis=0)
    terms = jnp.sum(spread(terms, "z", depth).reshape(depth, part, W), axis=0)
    diag_total = spread(terms, PLANE, plane).reshape(S, W, W)
    return (inverse_panels, diag_inverse - diag_total)


def solution(mesh):
    fine = Mesh(mesh.devices.reshape(2, 4, 2, 2, 16), ALL)
    placed = (P(ROW, COL), P(), P(), P(), P(ALL, None), P())
    return jax.shard_map(
        local,
        mesh=fine,
        in_specs=placed,
        out_specs=(P(ALL, None), P()),
        check_vma=False,
    )
```

time: 912 us -> 138 us (0.15)
  waiting for transfers between devices: 885 us -> 19.2 us
  blocking collectives: 0 us -> 78.6 us
  starting transfers between devices: 0.16 us -> 31.7 us
  between operations: 13.9 us -> 0.77 us
    psum x2 -> x0, waiting for transfers between devices: 654 us -> none  [the longest x1 483 us: local(): diag_total = lax.psum(local_diag, ('prow', 'pcol'))]
    all_gather x1 -> x0, waiting for transfers between devices: 116 us -> none  [local(): rowset = lax.all_gather(active_own, 'pcol', axis=0, tiled=True)]
    reduce_scatter x1 -> x0, waiting for transfers between devices: 115 us -> none  [local(): lax.psum_scatter(partial_value, 'pcol', scatter_dimension=0, tiled=True)]
    all_to_all x0 -> x4, blocking collectives: none -> 78.6 us  [the longest x3 64.1 us: exchange(): lax.all_to_all(value, axis, 0, 0, tiled=True, axis_index_groups=groups)]
    all_to_all x0 -> x2, starting transfers between devices: none -> 25.5 us  [spread(): return lax.all_to_all(copies, axis, 0, 0, tiled=True)]
    all_to_all x0 -> x2, waiting for transfers between devices: none -> 18.2 us  [spread(): return lax.all_to_all(copies, axis, 0, 0, tiled=True)]
  transfers between devices with their start and end apart: 4 -> 3, of which waited for: 4 -> 3; matrix products, arithmetic and copies ran while one was open for 0% -> 1% of each run, Pallas kernels for 0% -> 0%
where the time goes in v1:
time: 138 us; the launch traced here: 137 us
  blocking collectives  78.6 us (57%)
  starting transfers between devices  31.7 us (23%)
  waiting for transfers between devices  19.2 us (14%)
  other arithmetic  2.62 us (2%)
  local copies, waits for them, and re-layouts  2.55 us (2%)
  matrix products  1.63 us (1%)
    all_to_all x3, blocking collectives, exchange(): lax.all_to_all(value, axis, 0, 0, tiled=True, axis_index_groups=groups)  64.1 us
    all_to_all x2, starting transfers between devices, spread(): return lax.all_to_all(copies, axis, 0, 0, tiled=True)  25.5 us
    all_to_all x2, waiting for transfers between devices, spread(): return lax.all_to_all(copies, axis, 0, 0, tiled=True)  18.2 us
    all_to_all x1, blocking collectives, spread(): return lax.all_to_all(copies, axis, 0, 0, tiled=True)  14.5 us
    ppermute x1, starting transfers between devices, local(): moved = lax.ppermute(active_own, ALL, pairs)  6.27 us
  transfers between devices with their start and end apart: 3, of which 3 were waited for; matrix products, arithmetic and copies ran while one was open for 1% of the time, Pallas kernels for 0%

profile of v1, /device:TPU:1, one launch (start us, length us, event | category | flops | bytes accessed | tf_op | source)
XLA Modules:
  0.0 137.0 jit_solution(10850297035061317475)
XLA Ops:
  0.6 0.0 copy-start.2
  0.7 0.0 copy-start.3
  0.7 0.0 copy-start.4
  0.7 0.7 copy-done.3
  1.3 0.0 copy-done.4
  1.4 0.1 compare_reduce_fusion
  1.5 0.2 dynamic-slice_reduce_fusion
  1.6 0.1 broadcast_bitcast_fusion
  1.7 0.0 copy-done.2
  1.7 6.3 %collective-permute-start = (f32[16,512]{1,0:T(8,128)S(1)}, f32[16,512]{1,0:T(8,128)S(1)}, u32[]{:S(2)}, u32[]{:S(2)}) collective-permute-start(f32[16,512]{1,0:T(8,128)S(1)} %broadcast_multiply_fusion), channel_id=1, source_target_pairs={{0,0},{1,32},{2,64},{3,96},{4,128},{5,160},{6,192},{7,224},{8,256}... | collective-permute-start | bytes 98312 | tf_op jit(solution)/shard_map/ppermute | solution.py:46
  8.0 1.0 collective-permute-done
  9.0 0.8 broadcast_in_dim.12
  9.9 0.0 copy-start
  9.9 18.4 %all-to-all-start = ((f32[16,16,512]{2,1,0:T(8,128)}), f32[16,16,512]{2,1,0:T(8,128)S(1)}, u32[]{:S(2)}, u32[]{:S(2)}) async-start(f32[16,16,512]{2,1,0:T(8,128)} %broadcast_in_dim.12), calls=%async_computation | async-start | bytes 1048576 | tf_op jit(solution)/shard_map/all_to_all | solution.py:22
  28.3 0.9 convert_reduce_fusion
  29.1 0.0 copy-done
  29.1 0.1 multiply_bitcast_fusion
  29.3 9.9 %all-to-all-done = f32[16,16,512]{2,1,0:T(8,128)S(1)} async-done(((f32[16,16,512]{2,1,0:T(8,128)}), f32[16,16,512]{2,1,0:T(8,128)S(1)}, u32[]{:S(2)}, u32[]{:S(2)}) %all-to-all-start) | async-done | bytes 524320 | tf_op jit(solution)/shard_map/all_to_all | solution.py:22
  39.3 1.0 fusion.7
  40.3 14.9 %all_to_all.39 = f32[4,128,512]{2,1,0:T(8,128)S(1)} all-to-all(f32[4,128,512]{2,1,0:T(8,128)S(1)} %fusion.7), channel_id=1, replica_groups={{0,1,16,17},{2,3,18,19},{4,5,20,21},{6,7,22,23},{8,9,24,25},{10,11,26,2..., dimensions={0} | all-to-all | bytes 2097152 | tf_op jit(solution)/shard_map/all_to_all | solution.py:17
  55.2 0.1 reduce_sum.38
  55.3 29.2 %all_to_all.40 = f32[8,16,512]{2,1,0:T(8,128)S(1)} all-to-all(f32[8,16,512]{2,1,0:T(8,128)S(1)} %bitcast.35), channel_id=1, replica_groups={{0,2,4,6,8,10,12,14},{1,3,5,7,9,11,13,15},{16,18,20,22,24,26,28,30},{17..., dimensions={0} | all-to-all | bytes 524288 | tf_op jit(solution)/shard_map/all_to_all | solution.py:17
  84.5 0.6 fusion.1
  85.1 20.0 %all_to_all.41 = f32[32,16,128]{2,1,0:T(8,128)S(1)} all-to-all(f32[32,16,128]{2,1,0:T(8,128)S(1)} %bitcast.36), channel_id=1, replica_groups=mesh['yh'=2,'x'=4,'c'=2,'yl'=2,'z'=16] {'yh','x','c','yl'}, dimensions={0} | all-to-all | bytes 524288 | tf_op jit(solution)/shard_map/all_to_all | solution.py:17
  105.2 14.5 %all_to_all.42 = f32[16,16,128]{2,1,0:T(8,128)S(1)} all-to-all(f32[16,16,128]{2,1,0:T(8,128)S(1)} %broadcast_in_dim.13), channel_id=1, replica_groups=mesh['yh'=2,'x'=4,'c'=2,'yl'=2,'z'=16] {'z'}, dimensions={0} | all-to-all | bytes 262144 | tf_op jit(solution)/shard_map/all_to_all | solution.py:22
  119.7 0.7 broadcast_in_dim.14
  120.4 0.0 copy-start.1
  120.4 7.0 %all-to-all-start.5 = ((f32[32,16,128]{2,1,0:T(8,128)}), f32[32,16,128]{2,1,0:T(8,128)S(1)}, u32[]{:S(2)}, u32[]{:S(2)}) async-start(f32[32,16,128]{2,1,0:T(8,128)} %broadcast_in_dim.14), calls=%async_computation.5 | async-start | bytes 524288 | tf_op jit(solution)/shard_map/all_to_all | solution.py:22
  127.5 0.6 multiply_negate_fusion
  128.1 8.2 %all-to-all-done.5 = f32[32,16,128]{2,1,0:T(8,128)S(1)} async-done(((f32[32,16,128]{2,1,0:T(8,128)}), f32[32,16,128]{2,1,0:T(8,128)S(1)}, u32[]{:S(2)}, u32[]{:S(2)}) %all-to-all-start.5) | async-done | bytes 262176 | tf_op jit(solution)/shard_map/all_to_all | solution.py:22
  136.3 0.0 copy-done.1
  136.3 0.7 bitcast_subtract_fusion
  (7 shorter events, 0.1 us)
Async XLA Ops:
  0.6 1.1 copy-start.2
  0.7 0.7 copy-start.3
  0.7 0.7 copy-start.4
  1.7 7.3 %collective-permute-start = (f32[16,512]{1,0:T(8,128)S(1)}, f32[16,512]{1,0:T(8,128)S(1)}, u32[]{:S(2)}, u32[]{:S(2)}) collective-permute-start(f32[16,512]{1,0:T(8,128)S(1)} %broadcast_multiply_fusion), channel_id=1, source_target_pairs={{0,0},{1,32},{2,64},{3,96},{4,128},{5,160},{6,192},{7,224},{8,256}... | collective-permute-start | bytes 98312 | tf_op jit(solution)/shard_map/ppermute | solution.py:46
  9.9 19.3 %copy-start = (f32[512,256]{1,0:T(8,128)S(1)}, f32[512,256]{1,0:T(8,128)}, u32[]{:S(2)}) copy-start(f32[512,256]{1,0:T(8,128)} %param.6) | copy-start | bytes 1572868
  9.9 29.4 %all-to-all-start = ((f32[16,16,512]{2,1,0:T(8,128)}), f32[16,16,512]{2,1,0:T(8,128)S(1)}, u32[]{:S(2)}, u32[]{:S(2)}) async-start(f32[16,16,512]{2,1,0:T(8,128)} %broadcast_in_dim.12), calls=%async_computation | async-start | bytes 1048576 | tf_op jit(solution)/shard_map/all_to_all | solution.py:22
  120.4 15.9 %copy-start.1 = (f32[4,128,128]{2,1,0:T(8,128)S(1)}, f32[4,128,128]{2,1,0:T(8,128)}, u32[]{:S(2)}) copy-start(f32[4,128,128]{2,1,0:T(8,128)} %param.11) | copy-start | bytes 786436
  120.4 15.9 %all-to-all-start.5 = ((f32[32,16,128]{2,1,0:T(8,128)}), f32[32,16,128]{2,1,0:T(8,128)S(1)}, u32[]{:S(2)}, u32[]{:S(2)}) async-start(f32[32,16,128]{2,1,0:T(8,128)} %broadcast_in_dim.14), calls=%async_computation.5 | async-start | bytes 524288 | tf_op jit(solution)/shard_map/all_to_all | solution.py:22

commit v2 on v1

v2 whole, which is shorter than its diff:
```python
import jax
import jax.numpy as jnp
from jax import lax
from jax.sharding import Mesh
from jax.sharding import PartitionSpec as P


BLK = 256
W = 128
S = 4
SUB = 8
ROW = ("yh", "x", "c")
COL = ("yl", "zh", "zl")
NEAR = ("yl", "zl")
FAR = "zh"
WIDE = ("yh", "x", "c", "yl", "zl")
ALL = ("yh", "x", "c", "yl", "zh", "zl")


def exchange(value, axis):
    return lax.all_to_all(value, axis, 0, 0, tiled=True)


def spread(value, axis):
    copies = jnp.broadcast_to(value[None], (lax.axis_size(axis),) + value.shape)
    return lax.all_to_all(copies, axis, 0, 0, tiled=True)


def local(ancestor_inverse, block_mask, block_ids, row_lists, panels, diag_inverse):
    cols = lax.axis_size(COL)
    near = lax.axis_size(NEAR)
    far = lax.axis_size(FAR)
    wide = lax.axis_size(WIDE)
    halves = lax.axis_size("yl")
    pair = lax.axis_size("zl")
    prow_index = lax.axis_index(ROW)
    pcol_index = lax.axis_index(COL)
    row_count, width = panels.shape
    row_span, col_span = ancestor_inverse.shape
    active_blocks = jnp.any(
        block_ids[:, None, None] == row_lists[None, :, :], axis=2
    ).astype(jnp.float32)
    own_block = (prow_index * cols + pcol_index) * row_count // BLK
    own_active = lax.dynamic_slice_in_dim(active_blocks, own_block, 1, 0)
    own_keep = jnp.repeat(own_active, W, axis=1)
    active_own = panels * own_keep

    chunks = col_span // row_count
    pairs = [(q * chunks + j, j * cols + q) for q in range(cols) for j in range(chunks)]
    moved = lax.ppermute(active_own, ALL, pairs)
    active_far = spread(active_own, FAR).reshape(far * row_count, width)
    needed = spread(moved, ROW).reshape(col_span, width)

    block_rows = row_span // BLK
    local_mask = lax.dynamic_slice(
        block_mask, (prow_index * block_rows, pcol_index), (block_rows, 1)
    ).astype(jnp.float32)
    masked = (
        ancestor_inverse.reshape(block_rows, BLK, col_span) * local_mask[:, :, None]
    ).reshape(row_span, col_span)
    masked = (
        masked.reshape(halves, far, pair, row_count, col_span)
        .transpose(0, 2, 1, 3, 4)
        .reshape(row_span, col_span)
    )
    partial_value = jnp.dot(
        masked, needed, precision=lax.Precision.HIGHEST, preferred_element_type=jnp.float32
    )
    first = exchange(partial_value, NEAR)
    first = jnp.sum(first.reshape(near, far * row_count, width), axis=0)

    local_diag = jnp.einsum(
        "isa,isb->sab",
        active_far.reshape(far * row_count, S, W),
        first.reshape(far * row_count, S, W),
        precision=lax.Precision.HIGHEST,
    )
    part = S * W // wide
    terms = exchange(local_diag.reshape(S * W, W), WIDE)
    terms = jnp.sum(terms.reshape(wide, part, W), axis=0)
    tiles = row_count // SUB * S
    sent = first.reshape(far, row_count // SUB, SUB, S, W).transpose(0, 1, 3, 2, 4)
    sent = sent.reshape(far, tiles * SUB, W)
    copies = jnp.broadcast_to(terms[None], (far,) + terms.shape)
    both = exchange(jnp.concatenate([sent, copies], axis=1), FAR)
    both = jnp.sum(both, axis=0)
    summed = both[: tiles * SUB].reshape(row_count // SUB, S, SUB, W)
    summed = summed.transpose(0, 2, 1, 3).reshape(row_count, width)
    inverse_panels = -(own_keep * summed)
    terms = both[tiles * SUB :]
    diag_total = spread(terms, WIDE).reshape(S, W, W)
    return (inverse_panels, diag_inverse + diag_total)


def solution(mesh):
    fine = Mesh(mesh.devices.reshape(2, 4, 2, 2, 8, 2), ALL)
    placed = (P(ROW, COL), P(), P(), P(), P(ALL, None), P())
    return jax.shard_map(
        local,
        mesh=fine,
        in_specs=placed,
        out_specs=(P(ALL, None), P()),
        check_vma=False,
    )
```

time: 138 us -> 148 us (1.072)
  waiting for transfers between devices: 19.2 us -> 37.7 us
  blocking collectives: 78.6 us -> 72.7 us
  starting transfers between devices: 31.7 us -> 28.6 us
    all_to_all x3 -> x2, blocking collectives: 64.1 us -> 43.6 us  [exchange(): return lax.all_to_all(value, axis, 0, 0, tiled=True)]
    all_to_all x1, blocking collectives: 14.5 us -> 29.1 us  [spread(): return lax.all_to_all(copies, axis, 0, 0, tiled=True)]
    all_to_all x0 -> x1, waiting for transfers between devices: none -> 12.8 us  [exchange(): return lax.all_to_all(value, axis, 0, 0, tiled=True)]
    all_to_all x2, starting transfers between devices: 25.5 us -> 18.7 us  [spread(): return lax.all_to_all(copies, axis, 0, 0, tiled=True)]
    all_to_all x2, waiting for transfers between devices: 18.2 us -> 23.9 us  [spread(): return lax.all_to_all(copies, axis, 0, 0, tiled=True)]
    all_to_all x0 -> x1, starting transfers between devices: none -> 3.66 us  [exchange(): return lax.all_to_all(value, axis, 0, 0, tiled=True)]
  transfers between devices with their start and end apart: 3 -> 4, of which waited for: 3 -> 4; matrix products, arithmetic and copies ran while one was open for 1% -> 3% of each run, Pallas kernels for 0% -> 0%
where the time goes in v2:
time: 148 us
  blocking collectives  72.7 us (49%)
  waiting for transfers between devices  37.7 us (25%)
  starting transfers between devices  28.6 us (19%)
  local copies, waits for them, and re-layouts  2.7 us (2%)
  other arithmetic  2.66 us (2%)
  matrix products  2.6 us (2%)
    all_to_all x2, blocking collectives, exchange(): return lax.all_to_all(value, axis, 0, 0, tiled=True)  43.6 us
    all_to_all x1, blocking collectives, spread(): return lax.all_to_all(copies, axis, 0, 0, tiled=True)  29.1 us
    all_to_all x2, waiting for transfers between devices, spread(): return lax.all_to_all(copies, axis, 0, 0, tiled=True)  23.9 us
    all_to_all x2, starting transfers between devices, spread(): return lax.all_to_all(copies, axis, 0, 0, tiled=True)  18.7 us
    all_to_all x1, waiting for transfers between devices, exchange(): return lax.all_to_all(value, axis, 0, 0, tiled=True)  12.8 us
    ppermute x1, starting transfers between devices, local(): moved = lax.ppermute(active_own, ALL, pairs)  6.27 us
    all_to_all x1, starting transfers between devices, exchange(): return lax.all_to_all(value, axis, 0, 0, tiled=True)  3.66 us
  transfers between devices with their start and end apart: 4, of which 4 were waited for; matrix products, arithmetic and copies ran while one was open for 3% of the time, Pallas kernels for 0%

profile of v2, /device:TPU:1, one launch (start us, length us, event | category | flops | bytes accessed | tf_op | source)
XLA Modules:
  0.0 147.7 jit_solution(12911280721230705822)
XLA Ops:
  0.6 0.0 copy-start.2
  0.7 0.0 copy-start.3
  0.7 0.0 copy-start.4
  0.7 0.7 copy-done.3
  1.4 0.0 copy-done.4
  1.4 0.1 compare_reduce_fusion
  1.5 0.2 dynamic-slice_reduce_fusion
  1.6 0.1 broadcast_bitcast_fusion
  1.7 0.0 copy-done.2
  1.7 6.3 %collective-permute-start = (f32[16,512]{1,0:T(8,128)S(1)}, f32[16,512]{1,0:T(8,128)S(1)}, u32[]{:S(2)}, u32[]{:S(2)}) collective-permute-start(f32[16,512]{1,0:T(8,128)S(1)} %broadcast_multiply_fusion), channel_id=1, source_target_pairs={{0,0},{1,32},{2,64},{3,96},{4,128},{5,160},{6,192},{7,224},{8,256}... | collective-permute-start | bytes 98312 | tf_op jit(solution)/shard_map/ppermute | solution.py:50
  8.0 1.0 collective-permute-done
  9.1 29.1 %all_to_all.35 = f32[16,16,512]{2,1,0:T(8,128)S(1)} all-to-all(f32[16,16,512]{2,1,0:T(8,128)S(1)} %broadcast_in_dim.14), channel_id=1, replica_groups=mesh['yh'=2,'x'=4,'c'=2,'yl'=2,'zh'=8,'zl'=2] {'yh','x','c'}, dimensions={0} | all-to-all | bytes 1048576 | tf_op jit(solution)/shard_map/all_to_all | solution.py:26
  38.1 0.0 copy-start
  38.1 0.7 broadcast_in_dim.15
  38.9 12.3 %all-to-all-start.2 = ((f32[8,16,512]{2,1,0:T(8,128)}), f32[8,16,512]{2,1,0:T(8,128)S(1)}, u32[]{:S(2)}, u32[]{:S(2)}) async-start(f32[8,16,512]{2,1,0:T(8,128)} %broadcast_in_dim.15), calls=%async_computation.2 | async-start | bytes 524288 | tf_op jit(solution)/shard_map/all_to_all | solution.py:26
  51.1 0.9 convert_reduce_fusion
  52.0 0.0 copy-done
  52.0 0.1 multiply_bitcast_fusion
  52.2 2.0 %fusion.2 = f32[4,128,512]{2,1,0:T(8,128)} fusion(f32[4,128,256]{2,1,0:T(8,128)S(1)} %bitcast.29, f32[256,512,1]{1,0,2:T(8,128)S(1)} %bitcast.28), kind=kOutput, calls=%fused_computation.11 | convolution fusion | flops 805306368 | bytes 2097152 | tf_op jit(solution)/shard_map/dot_general | solution.py:66
  54.2 14.5 %all-to-all-done.2 = f32[8,16,512]{2,1,0:T(8,128)S(1)} async-done(((f32[8,16,512]{2,1,0:T(8,128)}), f32[8,16,512]{2,1,0:T(8,128)S(1)}, u32[]{:S(2)}, u32[]{:S(2)}) %all-to-all-start.2) | async-done | bytes 262176 | tf_op jit(solution)/shard_map/all_to_all | solution.py:26
  68.7 3.7 %all-to-all-start.1 = ((f32[4,128,512]{2,1,0:T(8,128)}), f32[4,128,512]{2,1,0:T(8,128)S(1)}, u32[]{:S(2)}, u32[]{:S(2)}) async-start(f32[4,128,512]{2,1,0:T(8,128)} %fusion.2), calls=%async_computation.1 | async-start | bytes 2097152 | tf_op jit(solution)/shard_map/all_to_all | solution.py:21
  72.4 0.1 reshape_reshape.4
  72.5 12.8 %all-to-all-done.1 = f32[4,128,512]{2,1,0:T(8,128)S(1)} async-done(((f32[4,128,512]{2,1,0:T(8,128)}), f32[4,128,512]{2,1,0:T(8,128)S(1)}, u32[]{:S(2)}, u32[]{:S(2)}) %all-to-all-start.1) | async-done | bytes 1048608 | tf_op jit(solution)/shard_map/all_to_all | solution.py:21
  85.3 0.1 reduce_sum.27
  85.4 0.1 copy.22
  85.6 0.6 fusion
  86.2 18.8 %all_to_all.36 = f32[64,8,128]{2,1,0:T(8,128)S(1)} all-to-all(f32[64,8,128]{2,1,0:T(8,128)S(1)} %bitcast.31), channel_id=1, replica_groups=mesh['yh'=2,'x'=4,'c'=2,'yl'=2,'zh'=8,'zl'=2] {'yh','x','c','yl','zl'}, dimensions={0} | all-to-all | bytes 524288 | tf_op jit(solution)/shard_map/all_to_all | solution.py:21
  105.0 0.1 reduce_sum.28
  105.1 24.8 %all_to_all.37 = f32[8,72,128]{2,1,0:T(8,128)S(1)} all-to-all(f32[8,72,128]{2,1,0:T(8,128)S(1)} %pad_maximum_fusion), channel_id=1, replica_groups=mesh['yh'=2,'x'=4,'c'=2,'yl'=2,'zh'=8,'zl'=2] {'zh'}, dimensions={0} | all-to-all | bytes 589824 | tf_op jit(solution)/shard_map/all_to_all | solution.py:21
  129.9 0.7 broadcast_in_dim.17
  130.6 0.0 copy-start.1
  130.6 6.4 %all-to-all-start.5 = ((f32[64,8,128]{2,1,0:T(8,128)}), f32[64,8,128]{2,1,0:T(8,128)S(1)}, u32[]{:S(2)}, u32[]{:S(2)}) async-start(f32[64,8,128]{2,1,0:T(8,128)} %broadcast_in_dim.17), calls=%async_computation.5 | async-start | bytes 524288 | tf_op jit(solution)/shard_map/all_to_all | solution.py:26
  137.1 0.6 multiply_negate_fusion
  137.7 9.3 %all-to-all-done.5 = f32[64,8,128]{2,1,0:T(8,128)S(1)} async-done(((f32[64,8,128]{2,1,0:T(8,128)}), f32[64,8,128]{2,1,0:T(8,128)S(1)}, u32[]{:S(2)}, u32[]{:S(2)}) %all-to-all-start.5) | async-done | bytes 262176 | tf_op jit(solution)/shard_map/all_to_all | solution.py:26
  147.0 0.0 copy-done.1
  147.0 0.7 bitcast_add_fusion
  (9 shorter events, 0.2 us)
Async XLA Ops:
  0.6 1.1 copy-start.2
  0.7 0.7 copy-start.3
  0.7 0.7 copy-start.4
  1.7 7.3 %collective-permute-start = (f32[16,512]{1,0:T(8,128)S(1)}, f32[16,512]{1,0:T(8,128)S(1)}, u32[]{:S(2)}, u32[]{:S(2)}) collective-permute-start(f32[16,512]{1,0:T(8,128)S(1)} %broadcast_multiply_fusion), channel_id=1, source_target_pairs={{0,0},{1,32},{2,64},{3,96},{4,128},{5,160},{6,192},{7,224},{8,256}... | collective-permute-start | bytes 98312 | tf_op jit(solution)/shard_map/ppermute | solution.py:50
  38.1 13.9 %copy-start = (f32[512,256]{1,0:T(8,128)S(1)}, f32[512,256]{1,0:T(8,128)}, u32[]{:S(2)}) copy-start(f32[512,256]{1,0:T(8,128)} %param.6) | copy-start | bytes 1572868
  38.9 29.9 %all-to-all-start.2 = ((f32[8,16,512]{2,1,0:T(8,128)}), f32[8,16,512]{2,1,0:T(8,128)S(1)}, u32[]{:S(2)}, u32[]{:S(2)}) async-start(f32[8,16,512]{2,1,0:T(8,128)} %broadcast_in_dim.15), calls=%async_computation.2 | async-start | bytes 524288 | tf_op jit(solution)/shard_map/all_to_all | solution.py:26
  68.7 16.6 %all-to-all-start.1 = ((f32[4,128,512]{2,1,0:T(8,128)}), f32[4,128,512]{2,1,0:T(8,128)S(1)}, u32[]{:S(2)}, u32[]{:S(2)}) async-start(f32[4,128,512]{2,1,0:T(8,128)} %fusion.2), calls=%async_computation.1 | async-start | bytes 2097152 | tf_op jit(solution)/shard_map/all_to_all | solution.py:21
  130.6 16.4 %copy-start.1 = (f32[4,128,128]{2,1,0:T(8,128)S(1)}, f32[4,128,128]{2,1,0:T(8,128)}, u32[]{:S(2)}) copy-start(f32[4,128,128]{2,1,0:T(8,128)} %param.11) | copy-start | bytes 786436
  130.6 16.4 %all-to-all-start.5 = ((f32[64,8,128]{2,1,0:T(8,128)}), f32[64,8,128]{2,1,0:T(8,128)S(1)}, u32[]{:S(2)}, u32[]{:S(2)}) async-start(f32[64,8,128]{2,1,0:T(8,128)} %broadcast_in_dim.17), calls=%async_computation.5 | async-start | bytes 524288 | tf_op jit(solution)/shard_map/all_to_all | solution.py:26

commit v3 on v1

v3 whole, which is shorter than its diff:
```python
import jax
import jax.numpy as jnp
from jax import lax
from jax.sharding import Mesh
from jax.sharding import PartitionSpec as P


BLK = 256
W = 128
S = 4
ROW = ("yh", "x", "c")
COL = ("yl", "z")
PLANE = ("yh", "x", "c", "yl")
SIDE = ("yh", "x", "yl")
ALL = ("yh", "x", "c", "yl", "z")
SWAP = [(0, 1), (1, 0)]


def spread(value, axis):
    copies = jnp.broadcast_to(value[None], (lax.axis_size(axis),) + value.shape)
    return lax.all_to_all(copies, axis, 0, 0, tiled=True)


def body(ancestor_inverse, block_mask, block_ids, row_lists, panels, diag_inverse):
    cols = lax.axis_size(COL)
    deep = lax.axis_size("z")
    prow_index = lax.axis_index(ROW)
    pcol_index = lax.axis_index(COL)
    core = lax.axis_index("c")
    side = lax.axis_index("yl")
    row_count, width = panels.shape
    half = width // 2
    row_span, col_span = ancestor_inverse.shape
    active_blocks = jnp.any(
        block_ids[:, None, None] == row_lists[None, :, :], axis=2
    ).astype(jnp.float32)
    own_block = (prow_index * cols + pcol_index) * row_count // BLK
    own_active = lax.dynamic_slice_in_dim(active_blocks, own_block, 1, 0)
    own_keep = jnp.repeat(own_active, W, axis=1)
    active_own = panels * own_keep

    chunks = col_span // row_count
    plane = lax.axis_size(PLANE)
    pairs = [
        (q * chunks + j, (q // deep * chunks + j) * deep + q % deep)
        for q in range(cols)
        for j in range(chunks)
    ]
    moved = lax.ppermute(active_own, ALL, pairs)

    by_core = active_own.reshape(row_count, 2, half).transpose(1, 0, 2)
    mine = jnp.where(core == 0, by_core[0], by_core[1])
    theirs = jnp.where(core == 0, by_core[1], by_core[0])
    active_pair = jnp.stack([mine, lax.ppermute(theirs, "c", SWAP)])

    block_rows = row_span // BLK
    local_mask = lax.dynamic_slice(
        block_mask, (prow_index * block_rows, pcol_index), (block_rows, 1)
    ).astype(jnp.float32)
    masked = ancestor_inverse.reshape(block_rows, BLK, col_span) * local_mask[:, :, None]
    kept = jnp.where(side == 0, masked[0], masked[1])
    sent = jnp.where(side == 0, masked[1], masked[0])
    came = lax.ppermute(sent, "yl", SWAP)
    own_rows = jnp.where(
        side == 0,
        jnp.concatenate([kept, came], axis=1),
        jnp.concatenate([came, kept], axis=1),
    )
    other_rows = lax.ppermute(own_rows, "c", SWAP)
    both_rows = jnp.stack(
        [
            own_rows.reshape(deep, row_count, 2 * col_span),
            other_rows.reshape(deep, row_count, 2 * col_span),
        ],
        axis=1,
    ).reshape(row_span, 2 * col_span)

    halves = moved.reshape(row_count, 2, half).transpose(1, 0, 2)
    shape = tuple(lax.axis_size(name) for name in PLANE)
    outgoing = jnp.broadcast_to(
        halves[None, None, :, None], shape + (row_count, half)
    ).reshape(plane, row_count, half)
    needed = lax.all_to_all(outgoing, PLANE, 0, 0, tiled=True).reshape(2 * col_span, half)

    partial_value = jnp.dot(
        both_rows, needed, precision=lax.Precision.HIGHEST, preferred_element_type=jnp.float32
    ).reshape(deep, 2 * row_count, half)
    parts = lax.all_to_all(partial_value, "z", 0, 0, tiled=True)
    summed = jnp.sum(parts, axis=0).reshape(2, row_count, half)

    back = lax.ppermute(summed[1], "c", SWAP)
    full = jnp.where(
        core == 0,
        jnp.concatenate([summed[0], back], axis=1),
        jnp.concatenate([back, summed[0]], axis=1),
    )
    inverse_panels = -(own_keep * full)

    local_diag = jnp.einsum(
        "isa,isb->sab",
        active_pair.reshape(2 * row_count, S // 2, W),
        summed.reshape(2 * row_count, S // 2, W),
        precision=lax.Precision.HIGHEST,
    )
    peers = lax.axis_size(SIDE)
    part = S // 2 * W // peers
    terms = lax.all_to_all(local_diag.reshape(peers, part, W), SIDE, 0, 0, tiled=True)
    terms = jnp.sum(terms, axis=0)
    terms = jnp.sum(spread(terms, "z"), axis=0)
    diag_total = spread(terms, PLANE).reshape(shape + (part, W))
    diag_total = diag_total.transpose(2, 0, 1, 3, 4, 5).reshape(S, W, W)
    return (inverse_panels, diag_inverse + diag_total)


def solution(mesh):
    fine = Mesh(mesh.devices.reshape(2, 4, 2, 2, 16), ALL)
    placed = (P(ROW, COL), P(), P(), P(), P(ALL, None), P())
    return jax.shard_map(
        body,
        mesh=fine,
        in_specs=placed,
        out_specs=(P(ALL, None), P()),
        check_vma=False,
    )
```

time: 138 us -> 144 us (1.043)
  blocking collectives: 78.6 us -> 35 us
  starting transfers between devices: 31.7 us -> 56 us
  waiting for transfers between devices: 19.2 us -> 42.8 us
    all_to_all x3 -> x1, blocking collectives: 64.1 us -> 12.5 us  [body(): lax.all_to_all(local_diag.reshape(peers, part, W), SIDE, 0, 0, tiled=True)]
    all_to_all x0 -> x2, waiting for transfers between devices: none -> 28.5 us  [the longest x1 17.9 us: body(): parts = lax.all_to_all(partial_value, 'z', 0, 0, tiled=True)]
    all_to_all x0 -> x2, starting transfers between devices: none -> 26.8 us  [the longest x1 14.9 us: body(): lax.all_to_all(outgoing, PLANE, 0, 0, tiled=True)]
    all_to_all x2 -> x1, starting transfers between devices: 25.5 us -> 7.98 us  [spread(): return lax.all_to_all(copies, axis, 0, 0, tiled=True)]
    ppermute x1 -> x5, starting transfers between devices: 6.27 us -> 21.2 us  [the longest x1 9.24 us: body(): other_rows = lax.ppermute(own_rows, 'c', SWAP)]
    all_to_all x2 -> x1, waiting for transfers between devices: 18.2 us -> 5.02 us  [spread(): return lax.all_to_all(copies, axis, 0, 0, tiled=True)]
    ppermute x1 -> x5, waiting for transfers between devices: 1 us -> 9.29 us  [the longest x1 4.2 us: body(): moved = lax.ppermute(active_own, ALL, pairs)]
    all_to_all x1, blocking collectives: 14.5 us -> 22.5 us  [spread(): return lax.all_to_all(copies, axis, 0, 0, tiled=True)]
  transfers between devices with their start and end apart: 3 -> 8, of which waited for: 3 -> 7; matrix products, arithmetic and copies ran while one was open for 1% -> 1% of each run, Pallas kernels for 0% -> 0%
where the time goes in v3:
time: 144 us
  starting transfers between devices  56 us (39%)
  waiting for transfers between devices  42.8 us (30%)
  blocking collectives  35 us (24%)
  other arithmetic  3.77 us (3%)
  local copies, waits for them, and re-layouts  2.85 us (2%)
  matrix products  2.16 us (2%)
    all_to_all x1, blocking collectives, spread(): return lax.all_to_all(copies, axis, 0, 0, tiled=True)  22.5 us
    all_to_all x1, waiting for transfers between devices, body(): parts = lax.all_to_all(partial_value, 'z', 0, 0, tiled=True)  17.9 us
    all_to_all x1, starting transfers between devices, body(): lax.all_to_all(outgoing, PLANE, 0, 0, tiled=True)  14.9 us
    all_to_all x1, blocking collectives, body(): lax.all_to_all(local_diag.reshape(peers, part, W), SIDE, 0, 0, tiled=True)  12.5 us
    all_to_all x1, starting transfers between devices, body(): parts = lax.all_to_all(partial_value, 'z', 0, 0, tiled=True)  11.9 us
    all_to_all x1, waiting for transfers between devices, body(): lax.all_to_all(outgoing, PLANE, 0, 0, tiled=True)  10.7 us
    ppermute x1, starting transfers between devices, body(): other_rows = lax.ppermute(own_rows, 'c', SWAP)  9.24 us
    all_to_all x1, starting transfers between devices, spread(): return lax.all_to_all(copies, axis, 0, 0, tiled=True)  7.98 us
  transfers between devices with their start and end apart: 8, of which 7 were waited for; matrix products, arithmetic and copies ran while one was open for 1% of the time, Pallas kernels for 0%

profile of v3, /device:TPU:1, one launch (start us, length us, event | category | flops | bytes accessed | tf_op | source)
XLA Modules:
  0.0 143.6 jit_solution(14456432793586238092)
XLA Ops:
  0.6 0.9 convert_reduce_fusion
  1.5 1.1 broadcast_multiply_fusion
  2.7 0.0 copy-start.2
  2.7 0.0 copy-start.3
  2.7 4.0 %collective-permute-start = (f32[256,256]{1,0:T(8,128)S(1)}, f32[256,256]{1,0:T(8,128)S(1)}, u32[]{:S(2)}, u32[]{:S(2)}) collective-permute-start(f32[256,256]{1,0:T(8,128)S(1)} %get-tuple-element.3), channel_id=1, source_target_pairs={{0,16},{16,0},{1,17},{17,1},{2,18},{18,2},{3,19},{19,3},{4,20},{20... | collective-permute-start | bytes 786440 | tf_op jit(solution)/shard_map/ppermute | solution.py:63
  6.8 0.0 copy-done.2
  6.8 0.0 copy-done.3
  6.8 0.1 compare_reduce_fusion
  6.9 0.2 dynamic-slice_reduce_fusion
  7.1 0.1 broadcast_bitcast_fusion
  7.2 3.3 %collective-permute-done = f32[256,256]{1,0:T(8,128)S(1)} collective-permute-done((f32[256,256]{1,0:T(8,128)S(1)}, f32[256,256]{1,0:T(8,128)S(1)}, u32[]{:S(2)}, u32[]{:S(2)}) %collective-permute-start) | collective-permute-done | bytes 262176 | tf_op jit(solution)/shard_map/ppermute | solution.py:63
  10.5 0.0 copy-start.1
  10.6 9.2 %collective-permute-start.1 = (f32[256,512]{1,0:T(8,128)S(1)}, f32[256,512]{1,0:T(8,128)S(1)}, u32[]{:S(2)}, u32[]{:S(2)}) collective-permute-start(f32[256,512]{1,0:T(8,128)S(1)} %maximum_select_fusion.1), channel_id=1, source_target_pairs={{0,32},{32,0},{1,33},{33,1},{2,34},{34,2},{3,35},{35,3},{4,36},{36... | collective-permute-start | bytes 1572872 | tf_op jit(solution)/shard_map/ppermute | solution.py:69
  19.8 0.0 copy-done.1
  19.8 1.9 %collective-permute-start.2 = (f32[16,512]{1,0:T(8,128)S(1)}, f32[16,512]{1,0:T(8,128)S(1)}, u32[]{:S(2)}, u32[]{:S(2)}) collective-permute-start(f32[16,512]{1,0:T(8,128)S(1)} %broadcast_multiply_fusion.1), channel_id=1, source_target_pairs={{0,0},{1,16},{2,32},{3,48},{4,64},{5,80},{6,96},{7,112},{8,128},{9... | collective-permute-start | bytes 98312 | tf_op jit(solution)/shard_map/ppermute | solution.py:49
  21.8 4.2 %collective-permute-done.2 = f32[16,512]{1,0:T(8,128)S(1)} collective-permute-done((f32[16,512]{1,0:T(8,128)S(1)}, f32[16,512]{1,0:T(8,128)S(1)}, u32[]{:S(2)}, u32[]{:S(2)}) %collective-permute-start.2) | collective-permute-done | bytes 32800 | tf_op jit(solution)/shard_map/ppermute | solution.py:49
  26.0 0.8 broadcast_in_dim.12
  26.9 14.9 %all-to-all-start = ((f32[32,16,256]{2,1,0:T(8,128)}), f32[32,16,256]{2,1,0:T(8,128)S(1)}, u32[]{:S(2)}, u32[]{:S(2)}) async-start(f32[32,16,256]{2,1,0:T(8,128)} %bitcast.9), calls=%async_computation | async-start | bytes 1048576 | tf_op jit(solution)/shard_map/all_to_all | solution.py:83
  41.8 0.0 collective-permute-done.1
  41.9 0.1 pad_maximum_fusion
  41.9 10.7 %all-to-all-done = f32[32,16,256]{2,1,0:T(8,128)S(1)} async-done(((f32[32,16,256]{2,1,0:T(8,128)}), f32[32,16,256]{2,1,0:T(8,128)S(1)}, u32[]{:S(2)}, u32[]{:S(2)}) %all-to-all-start) | async-done | bytes 524320 | tf_op jit(solution)/shard_map/all_to_all | solution.py:83
  52.6 1.8 %fusion.7 = f32[16,32,256]{2,1,0:T(8,128)} fusion(f32[16,32,512]{2,1,0:T(8,128)S(1)} %bitcast.39, f32[512,256,1]{1,0,2:T(8,128)S(1)} %bitcast.42), kind=kOutput, calls=%fused_computation.23 | convolution fusion | flops 805306368 | bytes 2097152 | tf_op jit(solution)/shard_map/dot_general | solution.py:85
  54.4 11.9 %all-to-all-start.1 = ((f32[16,32,256]{2,1,0:T(8,128)}), f32[16,32,256]{2,1,0:T(8,128)S(1)}, u32[]{:S(2)}, u32[]{:S(2)}) async-start(f32[16,32,256]{2,1,0:T(8,128)} %fusion.7), calls=%async_computation.1 | async-start | bytes 1048576 | tf_op jit(solution)/shard_map/all_to_all | solution.py:88
  66.4 3.8 %collective-permute-start.4 = (f32[16,256]{1,0:T(8,128)S(1)}, f32[16,256]{1,0:T(8,128)S(1)}, u32[]{:S(2)}, u32[]{:S(2)}) collective-permute-start(f32[16,256]{1,0:T(8,128)S(1)} %get-tuple-element.5), channel_id=1, source_target_pairs={{0,32},{32,0},{1,33},{33,1},{2,34},{34,2},{3,35},{35,3},{4,36},{36... | collective-permute-start | bytes 49160 | tf_op jit(solution)/shard_map/ppermute | solution.py:54
  70.2 0.8 collective-permute-done.4
  71.1 17.9 %all-to-all-done.1 = f32[16,32,256]{2,1,0:T(8,128)S(1)} async-done(((f32[16,32,256]{2,1,0:T(8,128)}), f32[16,32,256]{2,1,0:T(8,128)S(1)}, u32[]{:S(2)}, u32[]{:S(2)}) %all-to-all-start.1) | async-done | bytes 524320 | tf_op jit(solution)/shard_map/all_to_all | solution.py:88
  88.9 0.4 fusion
  89.3 12.5 %all_to_all.25 = f32[16,16,128]{2,1,0:T(8,128)S(1)} all-to-all(f32[16,16,128]{2,1,0:T(8,128)S(1)} %bitcast.46), channel_id=1, replica_groups=mesh['yh'=2,'x'=4,'c'=2,'yl'=2,'z'=16] {'yh','x','yl'}, dimensions={0} | all-to-all | bytes 262144 | tf_op jit(solution)/shard_map/all_to_all | solution.py:107
  101.9 22.5 %all_to_all.26 = f32[16,16,128]{2,1,0:T(8,128)S(1)} all-to-all(f32[16,16,128]{2,1,0:T(8,128)S(1)} %broadcast_in_dim.13), channel_id=1, replica_groups=mesh['yh'=2,'x'=4,'c'=2,'yl'=2,'z'=16] {'z'}, dimensions={0} | all-to-all | bytes 262144 | tf_op jit(solution)/shard_map/all_to_all | solution.py:21
  124.4 0.7 broadcast_in_dim.14
  125.2 8.0 %all-to-all-start.4 = ((f32[32,16,128]{2,1,0:T(8,128)}), f32[32,16,128]{2,1,0:T(8,128)S(1)}, u32[]{:S(2)}, u32[]{:S(2)}) async-start(f32[32,16,128]{2,1,0:T(8,128)} %broadcast_in_dim.14), calls=%async_computation.4 | async-start | bytes 524288 | tf_op jit(solution)/shard_map/all_to_all | solution.py:21
  133.2 2.1 %collective-permute-start.3 = (f32[16,256]{1,0:T(8,128)S(1)}, f32[16,256]{1,0:T(8,128)S(1)}, u32[]{:S(2)}, u32[]{:S(2)}) collective-permute-start(f32[16,256]{1,0:T(8,128)S(1)} %get-tuple-element.7), channel_id=1, source_target_pairs={{0,32},{32,0},{1,33},{33,1},{2,34},{34,2},{3,35},{35,3},{4,36},{36... | collective-permute-start | bytes 49160 | tf_op jit(solution)/shard_map/ppermute | solution.py:91
  135.3 0.9 collective-permute-done.3
  136.2 0.6 fusion.4
  136.9 5.0 %all-to-all-done.4 = f32[32,16,128]{2,1,0:T(8,128)S(1)} async-done(((f32[32,16,128]{2,1,0:T(8,128)}), f32[32,16,128]{2,1,0:T(8,128)S(1)}, u32[]{:S(2)}, u32[]{:S(2)}) %all-to-all-start.4) | async-done | bytes 262176 | tf_op jit(solution)/shard_map/all_to_all | solution.py:21
  141.9 0.0 copy-start
  141.9 0.9 copy-done
  142.8 0.7 add.32
  (17 shorter events, 0.3 us)
Async XLA Ops:
  2.7 4.1 %copy-start.2 = (s32[4,16]{1,0:T(4,128)S(1)}, s32[4,16]{1,0:T(4,128)}, u32[]{:S(2)}) copy-start(s32[4,16]{1,0:T(4,128)} %param.9) | copy-start | bytes 772
  2.7 4.1 %copy-start.3 = (s32[32]{0:T(128)S(1)}, s32[32]{0:T(128)}, u32[]{:S(2)}) copy-start(s32[32]{0:T(128)} %param.8) | copy-start | bytes 388
  2.7 7.8 %collective-permute-start = (f32[256,256]{1,0:T(8,128)S(1)}, f32[256,256]{1,0:T(8,128)S(1)}, u32[]{:S(2)}, u32[]{:S(2)}) collective-permute-start(f32[256,256]{1,0:T(8,128)S(1)} %get-tuple-element.3), channel_id=1, source_target_pairs={{0,16},{16,0},{1,17},{17,1},{2,18},{18,2},{3,19},{19,3},{4,20},{20... | collective-permute-start | bytes 786440 | tf_op jit(solution)/shard_map/ppermute | solution.py:63
  10.5 9.3 %copy-start.1 = (f32[16,512]{1,0:T(8,128)S(1)}, f32[16,512]{1,0:T(8,128)}, u32[]{:S(2)}) copy-start(f32[16,512]{1,0:T(8,128)} %param.10) | copy-start | bytes 98308
  10.6 31.3 %collective-permute-start.1 = (f32[256,512]{1,0:T(8,128)S(1)}, f32[256,512]{1,0:T(8,128)S(1)}, u32[]{:S(2)}, u32[]{:S(2)}) collective-permute-start(f32[256,512]{1,0:T(8,128)S(1)} %maximum_select_fusion.1), channel_id=1, source_target_pairs={{0,32},{32,0},{1,33},{33,1},{2,34},{34,2},{3,35},{35,3},{4,36},{36... | collective-permute-start | bytes 1572872 | tf_op jit(solution)/shard_map/ppermute | solution.py:69
  19.8 6.1 %collective-permute-start.2 = (f32[16,512]{1,0:T(8,128)S(1)}, f32[16,512]{1,0:T(8,128)S(1)}, u32[]{:S(2)}, u32[]{:S(2)}) collective-permute-start(f32[16,512]{1,0:T(8,128)S(1)} %broadcast_multiply_fusion.1), channel_id=1, source_target_pairs={{0,0},{1,16},{2,32},{3,48},{4,64},{5,80},{6,96},{7,112},{8,128},{9... | collective-permute-start | bytes 98312 | tf_op jit(solution)/shard_map/ppermute | solution.py:49
  26.9 25.8 %all-to-all-start = ((f32[32,16,256]{2,1,0:T(8,128)}), f32[32,16,256]{2,1,0:T(8,128)S(1)}, u32[]{:S(2)}, u32[]{:S(2)}) async-start(f32[32,16,256]{2,1,0:T(8,128)} %bitcast.9), calls=%async_computation | async-start | bytes 1048576 | tf_op jit(solution)/shard_map/all_to_all | solution.py:83
  54.4 34.5 %all-to-all-start.1 = ((f32[16,32,256]{2,1,0:T(8,128)}), f32[16,32,256]{2,1,0:T(8,128)S(1)}, u32[]{:S(2)}, u32[]{:S(2)}) async-start(f32[16,32,256]{2,1,0:T(8,128)} %fusion.7), calls=%async_computation.1 | async-start | bytes 1048576 | tf_op jit(solution)/shard_map/all_to_all | solution.py:88
  66.4 4.7 %collective-permute-start.4 = (f32[16,256]{1,0:T(8,128)S(1)}, f32[16,256]{1,0:T(8,128)S(1)}, u32[]{:S(2)}, u32[]{:S(2)}) collective-permute-start(f32[16,256]{1,0:T(8,128)S(1)} %get-tuple-element.5), channel_id=1, source_target_pairs={{0,32},{32,0},{1,33},{33,1},{2,34},{34,2},{3,35},{35,3},{4,36},{36... | collective-permute-start | bytes 49160 | tf_op jit(solution)/shard_map/ppermute | solution.py:54
  125.2 16.7 %all-to-all-start.4 = ((f32[32,16,128]{2,1,0:T(8,128)}), f32[32,16,128]{2,1,0:T(8,128)S(1)}, u32[]{:S(2)}, u32[]{:S(2)}) async-start(f32[32,16,128]{2,1,0:T(8,128)} %broadcast_in_dim.14), calls=%async_computation.4 | async-start | bytes 524288 | tf_op jit(solution)/shard_map/all_to_all | solution.py:21
  133.2 3.1 %collective-permute-start.3 = (f32[16,256]{1,0:T(8,128)S(1)}, f32[16,256]{1,0:T(8,128)S(1)}, u32[]{:S(2)}, u32[]{:S(2)}) collective-permute-start(f32[16,256]{1,0:T(8,128)S(1)} %get-tuple-element.7), channel_id=1, source_target_pairs={{0,32},{32,0},{1,33},{33,1},{2,34},{34,2},{3,35},{35,3},{4,36},{36... | collective-permute-start | bytes 49160 | tf_op jit(solution)/shard_map/ppermute | solution.py:91
  141.9 1.0 copy-start

commit v4 on v3

--- a/solution.py
+++ b/solution.py
@@ -9,10 +9,12 @@
 W = 128
 S = 4
 ROW = ("yh", "x", "c")
-COL = ("yl", "z")
+COL = ("yl", "zh", "zl")
+DEPTH = ("zh", "zl")
 PLANE = ("yh", "x", "c", "yl")
 SIDE = ("yh", "x", "yl")
-ALL = ("yh", "x", "c", "yl", "z")
+BACK = ("c", "yh", "x", "yl")
+ALL = ("yh", "x", "c", "yl", "zh", "zl")
 SWAP = [(0, 1), (1, 0)]
 
 
@@ -23,11 +25,14 @@
 
 def body(ancestor_inverse, block_mask, block_ids, row_lists, panels, diag_inverse):
     cols = lax.axis_size(COL)
-    deep = lax.axis_size("z")
+    deep = lax.axis_size(DEPTH)
+    far = lax.axis_size("zh")
+    near = lax.axis_size("zl")
     prow_index = lax.axis_index(ROW)
     pcol_index = lax.axis_index(COL)
     core = lax.axis_index("c")
     side = lax.axis_index("yl")
+    odd = lax.axis_index("zl")
     row_count, width = panels.shape
     half = width // 2
     row_span, col_span = ancestor_inverse.shape
@@ -54,12 +59,9 @@
     active_pair = jnp.stack([mine, lax.ppermute(theirs, "c", SWAP)])
 
     block_rows = row_span // BLK
-    local_mask = lax.dynamic_slice(
-        block_mask, (prow_index * block_rows, pcol_index), (block_rows, 1)
-    ).astype(jnp.float32)
-    masked = ancestor_inverse.reshape(block_rows, BLK, col_span) * local_mask[:, :, None]
-    kept = jnp.where(side == 0, masked[0], masked[1])
-    sent = jnp.where(side == 0, masked[1], masked[0])
+    blocks = ancestor_inverse.reshape(block_rows, BLK, col_span)
+    kept = jnp.where(side == 0, blocks[0], blocks[1])
+    sent = jnp.where(side == 0, blocks[1], blocks[0])
     came = lax.ppermute(sent, "yl", SWAP)
     own_rows = jnp.where(
         side == 0,
@@ -67,13 +69,22 @@
         jnp.concatenate([came, kept], axis=1),
     )
     other_rows = lax.ppermute(own_rows, "c", SWAP)
-    both_rows = jnp.stack(
-        [
-            own_rows.reshape(deep, row_count, 2 * col_span),
-            other_rows.reshape(deep, row_count, 2 * col_span),
-        ],
-        axis=1,
-    ).reshape(row_span, 2 * col_span)
+
+    def keep_cols(grid_row):
+        marks = lax.dynamic_slice(block_mask, (grid_row * block_rows + side, 0), (1, cols))
+        marks = marks.reshape(cols // deep, deep)
+        marks = lax.dynamic_slice(marks, (0, lax.axis_index(DEPTH)), (cols // deep, 1))
+        return jnp.repeat(marks.reshape(cols // deep).astype(jnp.float32), col_span)
+
+    def by_depth(rows, grid_row):
+        rows = rows * keep_cols(grid_row)[None, :]
+        return rows.reshape(far, near, row_count, 2 * col_span)
+
+    pieces = jnp.stack(
+        [by_depth(own_rows, prow_index), by_depth(other_rows, prow_index ^ 1)], axis=2
+    )
+    leave = jnp.where(odd == 0, pieces[:, 1], pieces[:, 0]).reshape(-1, 2 * col_span)
+    stay = jnp.where(odd == 0, pieces[:, 0], pieces[:, 1]).reshape(-1, 2 * col_span)
 
     halves = moved.reshape(row_count, 2, half).transpose(1, 0, 2)
     shape = tuple(lax.axis_size(name) for name in PLANE)
@@ -82,10 +93,16 @@
     ).reshape(plane, row_count, half)
     needed = lax.all_to_all(outgoing, PLANE, 0, 0, tiled=True).reshape(2 * col_span, half)
 
-    partial_value = jnp.dot(
-        both_rows, needed, precision=lax.Precision.HIGHEST, preferred_element_type=jnp.float32
-    ).reshape(deep, 2 * row_count, half)
-    parts = lax.all_to_all(partial_value, "z", 0, 0, tiled=True)
+    def product(rows):
+        value = jnp.dot(
+            rows, needed, precision=lax.Precision.HIGHEST, preferred_element_type=jnp.float32
+        )
+        return value.reshape(far, 2 * row_count, half)
+
+    leaving = product(leave)
+    arrived = lax.ppermute(leaving, "zl", SWAP)
+    pair_sum = product(stay) + arrived
+    parts = lax.all_to_all(pair_sum, "zh", 0, 0, tiled=True)
     summed = jnp.sum(parts, axis=0).reshape(2, row_count, half)
 
     back = lax.ppermute(summed[1], "c", SWAP)
@@ -106,14 +123,15 @@
     part = S // 2 * W // peers
     terms = lax.all_to_all(local_diag.reshape(peers, part, W), SIDE, 0, 0, tiled=True)
     terms = jnp.sum(terms, axis=0)
-    terms = jnp.sum(spread(terms, "z"), axis=0)
-    diag_total = spread(terms, PLANE).reshape(shape + (part, W))
-    diag_total = diag_total.transpose(2, 0, 1, 3, 4, 5).reshape(S, W, W)
-    return (inverse_panels, diag_inverse + diag_total)
+    terms = jnp.sum(spread(terms, DEPTH), axis=0)
+    own_part = lax.axis_index(BACK) * part
+    terms = lax.dynamic_slice_in_dim(diag_inverse.reshape(S * W, W), own_part, part, 0) + terms
+    diag_blocks = spread(terms, BACK).reshape(S, W, W)
+    return (inverse_panels, diag_blocks)
 
 
 def solution(mesh):
-    fine = Mesh(mesh.devices.reshape(2, 4, 2, 2, 16), ALL)
+    fine = Mesh(mesh.devices.reshape(2, 4, 2, 2, 8, 2), ALL)
     placed = (P(ROW, COL), P(), P(), P(), P(ALL, None), P())
     return jax.shard_map(
         body,

time: 144 us -> 135 us (0.938)
  blocking collectives: 35 us -> 12.4 us
  starting transfers between devices: 56 us -> 64.1 us
  waiting for transfers between devices: 42.8 us -> 46 us
  local copies, waits for them, and re-layouts: 2.85 us -> 5.11 us
    all_to_all x1 -> x0, blocking collectives: 22.5 us -> none  [spread(): return lax.all_to_all(copies, axis, 0, 0, tiled=True)]
    all_to_all x1 -> x2, waiting for transfers between devices: 5.02 us -> 17.1 us  [spread(): return lax.all_to_all(copies, axis, 0, 0, tiled=True)]
    all_to_all x1 -> x2, starting transfers between devices: 7.98 us -> 15.2 us  [spread(): return lax.all_to_all(copies, axis, 0, 0, tiled=True)]
    all_to_all x1, waiting for transfers between devices: 17.9 us -> 11 us  [body(): parts = lax.all_to_all(pair_sum, 'zh', 0, 0, tiled=True)]
    ppermute x0 -> x1, waiting for transfers between devices: none -> 5.66 us  [body(): arrived = lax.ppermute(leaving, 'zl', SWAP)]
    ppermute x1, starting transfers between devices: 9.24 us -> 4.94 us  [body(): other_rows = lax.ppermute(own_rows, 'c', SWAP)]
    ppermute x1, waiting for transfers between devices: 4.2 us -> 0.01 us  [body(): moved = lax.ppermute(active_own, ALL, pairs)]
    ppermute x1, starting transfers between devices: 1.92 us -> 5.73 us  [body(): moved = lax.ppermute(active_own, ALL, pairs)]
  transfers between devices with their start and end apart: 8 -> 10, of which waited for: 7 -> 7; matrix products, arithmetic and copies ran while one was open for 1% -> 3% of each run, Pallas kernels for 0% -> 0%
where the time goes in v4:
time: 135 us; the launch traced here: 134 us
  starting transfers between devices  64.1 us (47%)
  waiting for transfers between devices  46 us (34%)
  blocking collectives  12.4 us (9%)
  local copies, waits for them, and re-layouts  5.11 us (4%)
  other arithmetic  3.11 us (2%)
  matrix products  2.28 us (2%)
    all_to_all x2, waiting for transfers between devices, spread(): return lax.all_to_all(copies, axis, 0, 0, tiled=True)  17.1 us
    all_to_all x2, starting transfers between devices, spread(): return lax.all_to_all(copies, axis, 0, 0, tiled=True)  15.2 us
    all_to_all x1, starting transfers between devices, body(): lax.all_to_all(outgoing, PLANE, 0, 0, tiled=True)  14.8 us
    all_to_all x1, blocking collectives, body(): lax.all_to_all(local_diag.reshape(peers, part, W), SIDE, 0, 0, tiled=True)  12.4 us
    all_to_all x1, waiting for transfers between devices, body(): parts = lax.all_to_all(pair_sum, 'zh', 0, 0, tiled=True)  11 us
    all_to_all x1, waiting for transfers between devices, body(): lax.all_to_all(outgoing, PLANE, 0, 0, tiled=True)  10.5 us
    all_to_all x1, starting transfers between devices, body(): parts = lax.all_to_all(pair_sum, 'zh', 0, 0, tiled=True)  10.2 us
    ppermute x1, starting transfers between devices, body(): moved = lax.ppermute(active_own, ALL, pairs)  5.73 us
  transfers between devices with their start and end apart: 10, of which 7 were waited for; matrix products, arithmetic and copies ran while one was open for 3% of the time, Pallas kernels for 0%

profile of v4, /device:TPU:1, one launch (start us, length us, event | category | flops | bytes accessed | tf_op | source)
XLA Modules:
  0.0 133.9 jit_solution(10634255354422986724)
XLA Ops:
  0.6 1.1 slice_select_fusion.1
  1.7 4.0 %collective-permute-start = (f32[256,256]{1,0:T(8,128)S(1)}, f32[256,256]{1,0:T(8,128)S(1)}, u32[]{:S(2)}, u32[]{:S(2)}) collective-permute-start(f32[256,256]{1,0:T(8,128)S(1)} %get-tuple-element.7), channel_id=1, source_target_pairs={{0,16},{16,0},{1,17},{17,1},{2,18},{18,2},{3,19},{19,3},{4,20},{20... | collective-permute-start | bytes 786440 | tf_op jit(solution)/shard_map/ppermute | solution.py:65
  5.7 0.0 copy-start
  5.8 0.0 copy-start.1
  5.8 0.0 copy-start.2
  5.8 0.7 copy-done.1
  6.5 0.0 copy-done.2
  6.5 0.1 compare_reduce_fusion
  6.6 0.2 dynamic-slice_reduce_fusion
  6.8 0.1 broadcast_bitcast_fusion
  6.8 0.0 copy-done
  6.8 5.7 %collective-permute-start.2 = (f32[16,512]{1,0:T(8,128)S(1)}, f32[16,512]{1,0:T(8,128)S(1)}, u32[]{:S(2)}, u32[]{:S(2)}) collective-permute-start(f32[16,512]{1,0:T(8,128)S(1)} %broadcast_multiply_fusion.1), channel_id=1, source_target_pairs={{0,0},{1,16},{2,32},{3,48},{4,64},{5,80},{6,96},{7,112},{8,128},{9... | collective-permute-start | bytes 98312 | tf_op jit(solution)/shard_map/ppermute | solution.py:54
  12.6 0.8 fusion.12
  13.4 0.1 reshape.141
  13.5 0.1 reshape.142
  13.5 0.2 fusion.9
  13.8 0.0 collective-permute-done
  13.8 4.9 %collective-permute-start.1 = (f32[256,512]{1,0:T(8,128)S(1)}, f32[256,512]{1,0:T(8,128)S(1)}, u32[]{:S(2)}, u32[]{:S(2)}) collective-permute-start(f32[256,512]{1,0:T(8,128)S(1)} %maximum_select_fusion.1), channel_id=1, source_target_pairs={{0,32},{32,0},{1,33},{33,1},{2,34},{34,2},{3,35},{35,3},{4,36},{36... | collective-permute-start | bytes 1572872 | tf_op jit(solution)/shard_map/ppermute | solution.py:71
  18.8 0.1 broadcast_bitcast_fusion.1
  18.8 0.1 broadcast_bitcast_fusion.2
  18.9 0.0 collective-permute-done.2
  19.0 0.8 broadcast_in_dim.35
  19.8 14.8 %all-to-all-start = ((f32[32,16,256]{2,1,0:T(8,128)}), f32[32,16,256]{2,1,0:T(8,128)S(1)}, u32[]{:S(2)}, u32[]{:S(2)}) async-start(f32[32,16,256]{2,1,0:T(8,128)} %bitcast.6), calls=%async_computation | async-start | bytes 1048576 | tf_op jit(solution)/shard_map/all_to_all | solution.py:94
  34.6 0.1 fusion.1
  34.7 0.0 collective-permute-done.1
  34.7 0.1 broadcast_multiply_fusion
  34.7 0.1 broadcast_select_fusion.1
  34.9 10.5 %all-to-all-done = f32[32,16,256]{2,1,0:T(8,128)S(1)} async-done(((f32[32,16,256]{2,1,0:T(8,128)}), f32[32,16,256]{2,1,0:T(8,128)S(1)}, u32[]{:S(2)}, u32[]{:S(2)}) %all-to-all-start) | async-done | bytes 524320 | tf_op jit(solution)/shard_map/all_to_all | solution.py:94
  45.4 0.6 fusion.15
  46.0 2.4 %collective-permute-start.3 = (f32[8,32,256]{2,1,0:T(8,128)S(1)}, f32[8,32,256]{2,1,0:T(8,128)S(1)}, u32[]{:S(2)}, u32[]{:S(2)}) collective-permute-start(f32[8,32,256]{2,1,0:T(8,128)S(1)} %fusion.15), channel_id=1, source_target_pairs={{0,1},{1,0},{2,3},{3,2},{4,5},{5,4},{6,7},{7,6},{8,9},{9,8},{10,11... | collective-permute-start | bytes 786440 | tf_op jit(solution)/shard_map/ppermute | solution.py:103
  48.4 5.7 %collective-permute-done.3 = f32[8,32,256]{2,1,0:T(8,128)S(1)} collective-permute-done((f32[8,32,256]{2,1,0:T(8,128)S(1)}, f32[8,32,256]{2,1,0:T(8,128)S(1)}, u32[]{:S(2)}, u32[]{:S(2)}) %collective-permute-start.3) | collective-permute-done | bytes 262176 | tf_op jit(solution)/shard_map/ppermute | solution.py:103
  54.1 1.3 convolution_add_fusion
  55.4 10.2 %all-to-all-start.1 = ((f32[8,32,256]{2,1,0:T(8,128)}), f32[8,32,256]{2,1,0:T(8,128)S(1)}, u32[]{:S(2)}, u32[]{:S(2)}) async-start(f32[8,32,256]{2,1,0:T(8,128)} %convolution_add_fusion), calls=%async_computation.1 | async-start | bytes 524288 | tf_op jit(solution)/shard_map/all_to_all | solution.py:105
  65.6 4.7 %collective-permute-start.5 = (f32[16,256]{1,0:T(8,128)S(1)}, f32[16,256]{1,0:T(8,128)S(1)}, u32[]{:S(2)}, u32[]{:S(2)}) collective-permute-start(f32[16,256]{1,0:T(8,128)S(1)} %get-tuple-element.9), channel_id=1, source_target_pairs={{0,32},{32,0},{1,33},{33,1},{2,34},{34,2},{3,35},{35,3},{4,36},{36... | collective-permute-start | bytes 49160 | tf_op jit(solution)/shard_map/ppermute | solution.py:59
  70.3 0.8 collective-permute-done.5
  71.2 11.0 %all-to-all-done.1 = f32[8,32,256]{2,1,0:T(8,128)S(1)} async-done(((f32[8,32,256]{2,1,0:T(8,128)}), f32[8,32,256]{2,1,0:T(8,128)S(1)}, u32[]{:S(2)}, u32[]{:S(2)}) %all-to-all-start.1) | async-done | bytes 262176 | tf_op jit(solution)/shard_map/all_to_all | solution.py:105
  82.2 0.4 fusion.2
  82.6 12.4 %all_to_all.25 = f32[16,16,128]{2,1,0:T(8,128)S(1)} all-to-all(f32[16,16,128]{2,1,0:T(8,128)S(1)} %bitcast.50), channel_id=1, replica_groups=mesh['yh'=2,'x'=4,'c'=2,'yl'=2,'zh'=8,'zl'=2] {'yh','x','yl'}, dimensions={0} | all-to-all | bytes 262144 | tf_op jit(solution)/shard_map/all_to_all | solution.py:124
  95.0 0.7 broadcast_in_dim.36
  95.6 7.1 %all-to-all-start.3 = ((f32[16,16,128]{2,1,0:T(8,128)}), f32[16,16,128]{2,1,0:T(8,128)S(1)}, u32[]{:S(2)}, u32[]{:S(2)}) async-start(f32[16,16,128]{2,1,0:T(8,128)} %broadcast_in_dim.36), calls=%async_computation.3 | async-start | bytes 262144 | tf_op jit(solution)/shard_map/all_to_all | solution.py:23
  102.8 12.0 %all-to-all-done.3 = f32[16,16,128]{2,1,0:T(8,128)S(1)} async-done(((f32[16,16,128]{2,1,0:T(8,128)}), f32[16,16,128]{2,1,0:T(8,128)S(1)}, u32[]{:S(2)}, u32[]{:S(2)}) %all-to-all-start.3) | async-done | bytes 131104 | tf_op jit(solution)/shard_map/all_to_all | solution.py:23
  114.8 0.7 dynamic-slice_add_fusion
  115.5 0.7 broadcast_in_dim.37
  116.2 8.1 %all-to-all-start.4 = ((f32[32,16,128]{2,1,0:T(8,128)}), f32[32,16,128]{2,1,0:T(8,128)S(1)}, u32[]{:S(2)}, u32[]{:S(2)}) async-start(f32[32,16,128]{2,1,0:T(8,128)} %broadcast_in_dim.37), calls=%async_computation.4 | async-start | bytes 524288 | tf_op jit(solution)/shard_map/all_to_all | solution.py:23
  124.3 2.1 %collective-permute-start.4 = (f32[16,256]{1,0:T(8,128)S(1)}, f32[16,256]{1,0:T(8,128)S(1)}, u32[]{:S(2)}, u32[]{:S(2)}) collective-permute-start(f32[16,256]{1,0:T(8,128)S(1)} %get-tuple-element.11), channel_id=1, source_target_pairs={{0,32},{32,0},{1,33},{33,1},{2,34},{34,2},{3,35},{35,3},{4,36},{36... | collective-permute-start | bytes 49160 | tf_op jit(solution)/shard_map/ppermute | solution.py:108
  126.5 0.9 collective-permute-done.4
  127.4 0.6 fusion.6
  128.0 5.2 %all-to-all-done.4 = f32[32,16,128]{2,1,0:T(8,128)S(1)} async-done(((f32[32,16,128]{2,1,0:T(8,128)}), f32[32,16,128]{2,1,0:T(8,128)S(1)}, u32[]{:S(2)}, u32[]{:S(2)}) %all-to-all-start.4) | async-done | bytes 262176 | tf_op jit(solution)/shard_map/all_to_all | solution.py:23
  133.2 0.7 copy.47
  (17 shorter events, 0.3 us)
Async XLA Ops:
  1.7 12.1 %collective-permute-start = (f32[256,256]{1,0:T(8,128)S(1)}, f32[256,256]{1,0:T(8,128)S(1)}, u32[]{:S(2)}, u32[]{:S(2)}) collective-permute-start(f32[256,256]{1,0:T(8,128)S(1)} %get-tuple-element.7), channel_id=1, source_target_pairs={{0,16},{16,0},{1,17},{17,1},{2,18},{18,2},{3,19},{19,3},{4,20},{20... | collective-permute-start | bytes 786440 | tf_op jit(solution)/shard_map/ppermute | solution.py:65
  5.7 1.1 copy-start
  5.8 0.7 copy-start.1
  5.8 0.7 copy-start.2
  6.8 12.1 %collective-permute-start.2 = (f32[16,512]{1,0:T(8,128)S(1)}, f32[16,512]{1,0:T(8,128)S(1)}, u32[]{:S(2)}, u32[]{:S(2)}) collective-permute-start(f32[16,512]{1,0:T(8,128)S(1)} %broadcast_multiply_fusion.1), channel_id=1, source_target_pairs={{0,0},{1,16},{2,32},{3,48},{4,64},{5,80},{6,96},{7,112},{8,128},{9... | collective-permute-start | bytes 98312 | tf_op jit(solution)/shard_map/ppermute | solution.py:54
  13.8 20.8 %collective-permute-start.1 = (f32[256,512]{1,0:T(8,128)S(1)}, f32[256,512]{1,0:T(8,128)S(1)}, u32[]{:S(2)}, u32[]{:S(2)}) collective-permute-start(f32[256,512]{1,0:T(8,128)S(1)} %maximum_select_fusion.1), channel_id=1, source_target_pairs={{0,32},{32,0},{1,33},{33,1},{2,34},{34,2},{3,35},{35,3},{4,36},{36... | collective-permute-start | bytes 1572872 | tf_op jit(solution)/shard_map/ppermute | solution.py:71
  19.8 25.6 %all-to-all-start = ((f32[32,16,256]{2,1,0:T(8,128)}), f32[32,16,256]{2,1,0:T(8,128)S(1)}, u32[]{:S(2)}, u32[]{:S(2)}) async-start(f32[32,16,256]{2,1,0:T(8,128)} %bitcast.6), calls=%async_computation | async-start | bytes 1048576 | tf_op jit(solution)/shard_map/all_to_all | solution.py:94
  46.0 8.1 %collective-permute-start.3 = (f32[8,32,256]{2,1,0:T(8,128)S(1)}, f32[8,32,256]{2,1,0:T(8,128)S(1)}, u32[]{:S(2)}, u32[]{:S(2)}) collective-permute-start(f32[8,32,256]{2,1,0:T(8,128)S(1)} %fusion.15), channel_id=1, source_target_pairs={{0,1},{1,0},{2,3},{3,2},{4,5},{5,4},{6,7},{7,6},{8,9},{9,8},{10,11... | collective-permute-start | bytes 786440 | tf_op jit(solution)/shard_map/ppermute | solution.py:103
  55.4 26.8 %all-to-all-start.1 = ((f32[8,32,256]{2,1,0:T(8,128)}), f32[8,32,256]{2,1,0:T(8,128)S(1)}, u32[]{:S(2)}, u32[]{:S(2)}) async-start(f32[8,32,256]{2,1,0:T(8,128)} %convolution_add_fusion), calls=%async_computation.1 | async-start | bytes 524288 | tf_op jit(solution)/shard_map/all_to_all | solution.py:105
  65.6 5.5 %collective-permute-start.5 = (f32[16,256]{1,0:T(8,128)S(1)}, f32[16,256]{1,0:T(8,128)S(1)}, u32[]{:S(2)}, u32[]{:S(2)}) collective-permute-start(f32[16,256]{1,0:T(8,128)S(1)} %get-tuple-element.9), channel_id=1, source_target_pairs={{0,32},{32,0},{1,33},{33,1},{2,34},{34,2},{3,35},{35,3},{4,36},{36... | collective-permute-start | bytes 49160 | tf_op jit(solution)/shard_map/ppermute | solution.py:59
  95.6 19.1 %all-to-all-start.3 = ((f32[16,16,128]{2,1,0:T(8,128)}), f32[16,16,128]{2,1,0:T(8,128)S(1)}, u32[]{:S(2)}, u32[]{:S(2)}) async-start(f32[16,16,128]{2,1,0:T(8,128)} %broadcast_in_dim.36), calls=%async_computation.3 | async-start | bytes 262144 | tf_op jit(solution)/shard_map/all_to_all | solution.py:23
  116.2 17.0 %all-to-all-start.4 = ((f32[32,16,128]{2,1,0:T(8,128)}), f32[32,16,128]{2,1,0:T(8,128)S(1)}, u32[]{:S(2)}, u32[]{:S(2)}) async-start(f32[32,16,128]{2,1,0:T(8,128)} %broadcast_in_dim.37), calls=%async_computation.4 | async-start | bytes 524288 | tf_op jit(solution)/shard_map/all_to_all | solution.py:23
  124.3 3.1 %collective-permute-start.4 = (f32[16,256]{1,0:T(8,128)S(1)}, f32[16,256]{1,0:T(8,128)S(1)}, u32[]{:S(2)}, u32[]{:S(2)}) collective-permute-start(f32[16,256]{1,0:T(8,128)S(1)} %get-tuple-element.11), channel_id=1, source_target_pairs={{0,32},{32,0},{1,33},{33,1},{2,34},{34,2},{3,35},{35,3},{4,36},{36... | collective-permute-start | bytes 49160 | tf_op jit(solution)/shard_map/ppermute | solution.py:108

commit v5 on v2

v5 whole, which is shorter than its diff:
```python
import jax
import jax.numpy as jnp
from jax import lax
from jax.sharding import Mesh
from jax.sharding import PartitionSpec as P


BLK = 256
W = 128
S = 4
YH, XS, CS, YL, ZH, ZL = 2, 4, 2, 2, 8, 2
ROW = ("yh", "x", "c")
COL = ("yl", "zh", "zl")
SIDE = ("yh", "x", "zl")
BACK = ("c", "yl", "yh", "x", "zl")
ALL = ("yh", "x", "c", "yl", "zh", "zl")
SWAP = [(0, 1), (1, 0)]


def flat_of(yh, x, c, yl, zh, zl):
    return ((((yh * XS + x) * CS + c) * YL + yl) * ZH + zh) * ZL + zl


def place_of(flat):
    out = []
    for size in (ZL, ZH, YL, CS, XS, YH):
        out.append(flat % size)
        flat //= size
    return tuple(reversed(out))


def hops(one, two):
    total = 0
    for a, b, size in (
        (one[1], two[1], XS),
        (one[0] * YL + one[3], two[0] * YL + two[3], YH * YL),
        (one[4] * ZL + one[5], two[4] * ZL + two[5], ZH * ZL),
    ):
        gap = abs(a - b) % size
        total += min(gap, size - gap)
    return total


def assign(sources, targets):
    near = [[hops(place_of(s), place_of(t)) for t in targets] for s in sources]
    owner = {}

    def place(s, limit, seen):
        for t in sorted(range(len(targets)), key=lambda t: near[s][t]):
            if near[s][t] > limit or t in seen:
                continue
            seen.add(t)
            if t not in owner or place(owner[t], limit, seen):
                owner[t] = s
                return True
        return False

    limit = 0
    for s in range(len(sources)):
        while not place(s, limit, set()):
            limit += 1
    return {sources[s]: targets[t] for t, s in owner.items()}


def routes(chunks):
    pairs, groups = [], []
    for zh in range(ZH):
        blocks = [(h * ZH + zh) * ZL + zl for h in range(YL) for zl in range(ZL)]
        where = {}
        for k in range(S):
            sources = [q * chunks + j for q in blocks for j in range(k, chunks, S)]
            targets = [
                flat_of(yh, x, k // YL, k % YL, zh, zl)
                for yh in range(YH)
                for x in range(XS)
                for zl in range(ZL)
            ]
            where.update(assign(sources, targets))
        order = [where[q * chunks + j] for q in blocks for j in range(chunks)]
        pairs += [(q * chunks + j, where[q * chunks + j]) for q in blocks for j in range(chunks)]
        groups.append(order)
    return pairs, groups


def spread(value, axis):
    copies = jnp.broadcast_to(value[None], (lax.axis_size(axis),) + value.shape)
    return lax.all_to_all(copies, axis, 0, 0, tiled=True)


def pick(index, one, two):
    return jnp.where(index == 0, one, two)


def in_order(index, own, other, axis):
    return pick(
        index,
        jnp.concatenate([own, other], axis=axis),
        jnp.concatenate([other, own], axis=axis),
    )


def body(ancestor_inverse, block_mask, block_ids, row_lists, panels, diag_inverse):
    cols = lax.axis_size(COL)
    prow_index = lax.axis_index(ROW)
    pcol_index = lax.axis_index(COL)
    core, side, odd = lax.axis_index("c"), lax.axis_index("yl"), lax.axis_index("zl")
    mine = core * YL + side
    row_count, _ = panels.shape
    row_span, col_span = ancestor_inverse.shape
    chunks = col_span // row_count
    pairs, groups = routes(chunks)
    active_blocks = jnp.any(
        block_ids[:, None, None] == row_lists[None, :, :], axis=2
    ).astype(jnp.float32)
    own_block = (prow_index * cols + pcol_index) * row_count // BLK
    own_active = lax.dynamic_slice_in_dim(active_blocks, own_block, 1, 0)
    own_keep = jnp.repeat(own_active, W, axis=1)
    active_own = panels * own_keep

    moved = lax.ppermute(active_own, ALL, pairs)

    blocks = ancestor_inverse.reshape(YL, ZH, ZL, row_count, col_span)
    kept = pick(odd, blocks[:, :, 0], blocks[:, :, 1]).reshape(-1, col_span)
    sent = pick(odd, blocks[:, :, 1], blocks[:, :, 0]).reshape(-1, col_span)
    came = lax.ppermute(sent, "zl", SWAP)
    two = in_order(odd, kept, came, 1)
    across = lax.ppermute(two, "yl", SWAP)
    four = in_order(side, two, across, 1)
    other = lax.ppermute(four, "c", SWAP)

    def masked(rows, grid_row):
        marks = lax.dynamic_slice(block_mask, (grid_row * YL, 0), (YL, cols)).reshape(YL, YL, ZH, ZL)
        marks = lax.dynamic_slice(
            marks, (0, 0, lax.axis_index("zh"), 0), (YL, YL, 1, ZL)
        ).reshape(YL, YL * ZL)
        marks = jnp.repeat(marks.astype(jnp.float32), col_span, axis=1)
        return rows.reshape(YL, ZH, row_count, -1) * marks[:, None, None, :]

    rows = jnp.stack([masked(four, prow_index), masked(other, prow_index ^ 1)])
    rows = rows.transpose(2, 0, 1, 3, 4).reshape(row_span, YL * ZL * col_span)

    by_node = moved.reshape(row_count, S, W).transpose(1, 0, 2)
    outgoing = jnp.broadcast_to(by_node[None], (chunks, S, row_count, W))
    outgoing = outgoing.reshape(chunks * S, row_count, W)
    needed = lax.all_to_all(outgoing, ALL, 0, 0, tiled=True, axis_index_groups=groups)
    partial_value = jnp.dot(
        rows,
        needed.reshape(-1, W),
        precision=lax.Precision.HIGHEST,
        preferred_element_type=jnp.float32,
    ).reshape(ZH, CS * YL * row_count, W)
    parts = lax.all_to_all(partial_value, "zh", 0, 0, tiled=True)
    summed = jnp.sum(parts, axis=0).reshape(CS, YL, row_count, W)

    shifts = ((0, 1), (1, 0), (1, 1))
    swaps = [
        [(m, m ^ (dc * YL + dy)) for m in range(CS * YL)] for dc, dy in shifts
    ]
    own_nodes = active_own.reshape(row_count, S, W)

    def node(index):
        return lax.dynamic_slice_in_dim(own_nodes, index, 1, 1)[:, 0]

    a01, a10, a11 = [
        lax.ppermute(node(mine ^ (dc * YL + dy)), ("c", "yl"), swap)
        for (dc, dy), swap in zip(shifts, swaps)
    ]
    a00 = node(mine)
    active_group = jnp.concatenate(
        [pick(side, a00, a01), pick(side, a01, a00), pick(side, a10, a11), pick(side, a11, a10)]
    )
    local_diag = jnp.dot(
        active_group.T, summed.reshape(-1, W), precision=lax.Precision.HIGHEST
    )
    peers = lax.axis_size(SIDE)
    part = W // peers
    terms = lax.all_to_all(local_diag.reshape(peers, part, W), SIDE, 0, 0, tiled=True)
    terms = jnp.sum(terms, axis=0)
    terms = jnp.sum(spread(terms, "zh"), axis=0)
    own_part = lax.axis_index(BACK) * part
    terms = lax.dynamic_slice_in_dim(diag_inverse.reshape(S * W, W), own_part, part, 0) + terms
    diag_blocks = spread(terms, BACK).reshape(S, W, W)

    r00 = pick(side, summed[0, 0], summed[0, 1])
    r01, r10, r11 = [
        lax.ppermute(pick(side ^ dy, summed[dc, 0], summed[dc, 1]), ("c", "yl"), swap)
        for (dc, dy), swap in zip(shifts, swaps)
    ]
    columns = []
    for k in range(S):
        which = mine ^ k
        columns.append(
            jnp.where(which < 2, jnp.where(which == 0, r00, r01), jnp.where(which == 2, r10, r11))
        )
    inverse_panels = -(own_keep * jnp.concatenate(columns, axis=1))
    return (inverse_panels, diag_blocks)


def solution(mesh):
    fine = Mesh(mesh.devices.reshape(YH, XS, CS, YL, ZH, ZL), ALL)
    placed = (P(ROW, COL), P(), P(), P(), P(ALL, None), P())
    return jax.shard_map(
        body,
        mesh=fine,
        in_specs=placed,
        out_specs=(P(ALL, None), P()),
        check_vma=False,
    )
```

time: 148 us -> 139 us (0.939)
  blocking collectives: 72.7 us -> 12.6 us
  starting transfers between devices: 28.6 us -> 69.1 us
  waiting for transfers between devices: 37.7 us -> 42.5 us
  local copies, waits for them, and re-layouts: 2.7 us -> 5.14 us
  other arithmetic: 2.66 us -> 5.09 us
    all_to_all x3 -> x1, blocking collectives: 72.7 us -> 12.6 us  [body(): lax.all_to_all(local_diag.reshape(peers, part, W), SIDE, 0, 0, tiled=True)]
    ppermute x1 -> x10, starting transfers between devices: 6.27 us -> 34.8 us  [the longest x3 7.75 us: body(): lax.ppermute(node(mine ^ dc * YL + dy), ('c', 'yl'), swap)]
    ppermute x1 -> x10, waiting for transfers between devices: 1 us -> 20.3 us  [the longest x1 11.7 us: body(): moved = lax.ppermute(active_own, ALL, pairs)]
    all_to_all x1 -> x2, starting transfers between devices: 3.66 us -> 21.5 us  [the longest x1 12.6 us: body(): parts = lax.all_to_all(partial_value, 'zh', 0, 0, tiled=True)]
    all_to_all x2, waiting for transfers between devices: 23.9 us -> 11.9 us  [spread(): return lax.all_to_all(copies, axis, 0, 0, tiled=True)]
    all_to_all x2, starting transfers between devices: 18.7 us -> 12.8 us  [spread(): return lax.all_to_all(copies, axis, 0, 0, tiled=True)]
    all_to_all x1 -> x2, waiting for transfers between devices: 12.8 us -> 10.4 us  [the longest x1 7.56 us: body(): parts = lax.all_to_all(partial_value, 'zh', 0, 0, tiled=True)]
    select_n x0 -> x8, other arithmetic: none -> 2.32 us  [the longest x6 2.3 us: pick(): return jnp.where(index == 0, one, two)]
  transfers between devices with their start and end apart: 4 -> 14, of which waited for: 4 -> 9; matrix products, arithmetic and copies ran while one was open for 3% -> 5% of each run, Pallas kernels for 0% -> 0%
where the time goes in v5:
time: 139 us; the launch traced here: 138 us
  starting transfers between devices  69.1 us (50%)
  waiting for transfers between devices  42.5 us (31%)
  blocking collectives  12.6 us (9%)
  local copies, waits for them, and re-layouts  5.14 us (4%)
  other arithmetic  5.09 us (4%)
  matrix products  2.78 us (2%)
    all_to_all x2, starting transfers between devices, spread(): return lax.all_to_all(copies, axis, 0, 0, tiled=True)  12.8 us
    all_to_all x1, starting transfers between devices, body(): parts = lax.all_to_all(partial_value, 'zh', 0, 0, tiled=True)  12.6 us
    all_to_all x1, blocking collectives, body(): lax.all_to_all(local_diag.reshape(peers, part, W), SIDE, 0, 0, tiled=True)  12.6 us
    all_to_all x2, waiting for transfers between devices, spread(): return lax.all_to_all(copies, axis, 0, 0, tiled=True)  11.9 us
    ppermute x1, waiting for transfers between devices, body(): moved = lax.ppermute(active_own, ALL, pairs)  11.7 us
    all_to_all x1, starting transfers between devices, body(): lax.all_to_all(outgoing, ALL, 0, 0, tiled=True, axis_index_groups=groups)  8.84 us
    ppermute x3, starting transfers between devices, body(): lax.ppermute(node(mine ^ dc * YL + dy), ('c', 'yl'), swap)  7.75 us
    ppermute x3, starting transfers between devices, body(): lax.ppermute(pick(side ^ dy, summed[dc, 0], summed[dc, 1]), ('c', 'yl'),...  7.72 us
  transfers between devices with their start and end apart: 14, of which 9 were waited for; matrix products, arithmetic and copies ran while one was open for 5% of the time, Pallas kernels for 0%

profile of v5, /device:TPU:1, one launch (start us, length us, event | category | flops | bytes accessed | tf_op | source)
XLA Modules:
  0.0 138.2 jit_solution(1989700108242517698)
XLA Ops:
  0.6 0.0 copy-start
  0.6 1.1 slice_select_fusion.1
  1.7 4.4 %collective-permute-start = (f32[256,256]{1,0:T(8,128)S(1)}, f32[256,256]{1,0:T(8,128)S(1)}, u32[]{:S(2)}, u32[]{:S(2)}) collective-permute-start(f32[256,256]{1,0:T(8,128)S(1)} %bitcast.74), channel_id=1, source_target_pairs={{0,1},{1,0},{2,3},{3,2},{4,5},{5,4},{6,7},{7,6},{8,9},{9,8},{10,11... | collective-permute-start | bytes 786440 | tf_op jit(solution)/shard_map/ppermute | solution.py:125
  6.1 0.8 compare_reduce_fusion
  6.9 0.2 fusion.15
  7.1 0.1 broadcast_bitcast_fusion.2
  7.2 2.7 %collective-permute-done = f32[256,256]{1,0:T(8,128)S(1)} collective-permute-done((f32[256,256]{1,0:T(8,128)S(1)}, f32[256,256]{1,0:T(8,128)S(1)}, u32[]{:S(2)}, u32[]{:S(2)}) %collective-permute-start) | collective-permute-done | bytes 262176 | tf_op jit(solution)/shard_map/ppermute | solution.py:125
  9.9 5.4 %collective-permute-start.1 = (f32[256,512]{1,0:T(8,128)S(1)}, f32[256,512]{1,0:T(8,128)S(1)}, u32[]{:S(2)}, u32[]{:S(2)}) collective-permute-start(f32[256,512]{1,0:T(8,128)S(1)} %maximum_select_fusion.3), channel_id=1, source_target_pairs={{0,16},{16,0},{1,17},{17,1},{2,18},{18,2},{3,19},{19,3},{4,20},{20... | collective-permute-start | bytes 1572872 | tf_op jit(solution)/shard_map/ppermute | solution.py:127
  15.3 0.0 copy-done
  15.3 7.3 %collective-permute-start.3 = (f32[16,512]{1,0:T(8,128)S(1)}, f32[16,512]{1,0:T(8,128)S(1)}, u32[]{:S(2)}, u32[]{:S(2)}) collective-permute-start(f32[16,512]{1,0:T(8,128)S(1)} %broadcast_multiply_fusion.1), channel_id=1, source_target_pairs={{0,128},{1,337},{2,481},{3,369},{4,129},{5,145},{6,161},{7,305},{8... | collective-permute-start | bytes 98312 | tf_op jit(solution)/shard_map/ppermute | solution.py:120
  22.6 11.7 %collective-permute-done.3 = f32[16,512]{1,0:T(8,128)S(1)} collective-permute-done((f32[16,512]{1,0:T(8,128)S(1)}, f32[16,512]{1,0:T(8,128)S(1)}, u32[]{:S(2)}, u32[]{:S(2)}) %collective-permute-start.3) | collective-permute-done | bytes 32800 | tf_op jit(solution)/shard_map/ppermute | solution.py:120
  34.4 0.9 broadcast_in_dim.35
  35.3 8.8 %all-to-all-start = ((f32[64,16,128]{2,1,0:T(8,128)}), f32[64,16,128]{2,1,0:T(8,128)S(1)}, u32[]{:S(2)}, u32[]{:S(2)}) async-start(f32[64,16,128]{2,1,0:T(8,128)} %bitcast.12), calls=%async_computation | async-start | bytes 1048576 | tf_op jit(solution)/shard_map/all_to_all | solution.py:145
  44.1 0.0 collective-permute-done.1
  44.1 1.1 maximum_select_fusion.1
  45.3 2.3 %collective-permute-start.2 = (f32[256,1024]{1,0:T(8,128)}, f32[256,1024]{1,0:T(8,128)S(1)}, u32[]{:S(2)}, u32[]{:S(2)}) collective-permute-start(f32[256,1024]{1,0:T(8,128)} %maximum_select_fusion.1), channel_id=1, source_target_pairs={{0,32},{32,0},{1,33},{33,1},{2,34},{34,2},{3,35},{35,3},{4,36},{36... | collective-permute-start | bytes 3145736 | tf_op jit(solution)/shard_map/ppermute | solution.py:129
  47.6 0.8 constant_dynamic-slice_fusion.7
  48.4 0.1 reshape.211
  48.5 0.1 reshape.213
  48.6 0.1 convert_element_type.19
  48.7 0.1 broadcast_bitcast_fusion
  48.8 0.1 convert_element_type.17
  48.8 0.1 broadcast_bitcast_fusion.1
  49.0 0.2 fusion
  49.2 0.9 collective-permute-done.2
  50.1 0.1 broadcast_multiply_fusion
  50.2 0.2 maximum_bitcast_fusion
  50.4 0.2 copy.33
  50.7 2.8 %all-to-all-done = f32[64,16,128]{2,1,0:T(8,128)S(1)} async-done(((f32[64,16,128]{2,1,0:T(8,128)}), f32[64,16,128]{2,1,0:T(8,128)S(1)}, u32[]{:S(2)}, u32[]{:S(2)}) %all-to-all-start) | async-done | bytes 524320 | tf_op jit(solution)/shard_map/all_to_all | solution.py:145
  53.5 2.5 %fusion.21 = f32[8,64,128]{2,1,0:T(8,128)} fusion(f32[8,64,1024]{2,1,0:T(8,128)S(1)} %bitcast.63, f32[1024,128,1]{1,0,2:T(8,128)S(1)} %bitcast.67), kind=kOutput, calls=%fused_computation.58 | convolution fusion | flops 805306368 | bytes 2883584 | tf_op jit(solution)/shard_map/dot_general | solution.py:146
  56.0 12.6 %all-to-all-start.1 = ((f32[8,64,128]{2,1,0:T(8,128)}), f32[8,64,128]{2,1,0:T(8,128)S(1)}, u32[]{:S(2)}, u32[]{:S(2)}) async-start(f32[8,64,128]{2,1,0:T(8,128)} %fusion.21), calls=%async_computation.1 | async-start | bytes 524288 | tf_op jit(solution)/shard_map/all_to_all | solution.py:152
  68.7 0.1 copy.37
  68.8 2.6 %collective-permute-start.8 = (f32[16,128]{0,1:T(8,128)S(1)}, f32[16,128]{0,1:T(8,128)S(1)}, u32[]{:S(2)}, u32[]{:S(2)}) collective-permute-start(f32[16,128]{0,1:T(8,128)S(1)} %bitcast.77), channel_id=1, source_target_pairs={{0,32},{16,48},{32,0},{48,16},{1,33},{17,49},{33,1},{49,17},{2,34}... | collective-permute-start | bytes 24584 | tf_op jit(solution)/shard_map/ppermute | solution.py:165
  71.4 0.1 copy.38
  71.5 1.9 %collective-permute-start.9 = (f32[16,128]{0,1:T(8,128)S(1)}, f32[16,128]{0,1:T(8,128)S(1)}, u32[]{:S(2)}, u32[]{:S(2)}) collective-permute-start(f32[16,128]{0,1:T(8,128)S(1)} %bitcast.78), channel_id=1, source_target_pairs={{0,48},{16,32},{32,16},{48,0},{1,49},{17,33},{33,17},{49,1},{2,50}... | collective-permute-start | bytes 24584 | tf_op jit(solution)/shard_map/ppermute | solution.py:165
  73.4 0.1 copy.36
  73.5 3.3 %collective-permute-start.7 = (f32[16,128]{0,1:T(8,128)S(1)}, f32[16,128]{0,1:T(8,128)S(1)}, u32[]{:S(2)}, u32[]{:S(2)}) collective-permute-start(f32[16,128]{0,1:T(8,128)S(1)} %bitcast.76), channel_id=1, source_target_pairs={{0,16},{16,0},{32,48},{48,32},{1,17},{17,1},{33,49},{49,33},{2,18}... | collective-permute-start | bytes 24584 | tf_op jit(solution)/shard_map/ppermute | solution.py:165
  76.8 0.1 copy.35
  76.9 0.0 collective-permute-done.8
  76.9 0.5 collective-permute-done.9
  77.4 1.5 %collective-permute-done.7 = f32[16,128]{0,1:T(8,128)S(1)} collective-permute-done((f32[16,128]{0,1:T(8,128)S(1)}, f32[16,128]{0,1:T(8,128)S(1)}, u32[]{:S(2)}, u32[]{:S(2)}) %collective-permute-start.7) | collective-permute-done | bytes 8224 | tf_op jit(solution)/shard_map/ppermute | solution.py:165
  79.0 7.6 %all-to-all-done.1 = f32[8,64,128]{2,1,0:T(8,128)S(1)} async-done(((f32[8,64,128]{2,1,0:T(8,128)}), f32[8,64,128]{2,1,0:T(8,128)S(1)}, u32[]{:S(2)}, u32[]{:S(2)}) %all-to-all-start.1) | async-done | bytes 262176 | tf_op jit(solution)/shard_map/all_to_all | solution.py:152
  86.5 0.3 fusion.2
  86.8 12.6 %all_to_all.25 = f32[16,8,128]{2,1,0:T(8,128)S(1)} all-to-all(f32[16,8,128]{2,1,0:T(8,128)S(1)} %fusion.2), channel_id=1, replica_groups=mesh['yh'=2,'x'=4,'c'=2,'yl'=2,'zh'=8,'zl'=2] {'yh','x','zl'}, dimensions={0} | all-to-all | bytes 131072 | tf_op jit(solution)/shard_map/all_to_all | solution.py:177
  99.4 0.6 broadcast_in_dim.36
  100.0 5.1 %all-to-all-start.3 = ((f32[8,8,128]{2,1,0:T(8,128)}), f32[8,8,128]{2,1,0:T(8,128)S(1)}, u32[]{:S(2)}, u32[]{:S(2)}) async-start(f32[8,8,128]{2,1,0:T(8,128)} %broadcast_in_dim.36), calls=%async_computation.3 | async-start | bytes 65536 | tf_op jit(solution)/shard_map/all_to_all | solution.py:87
  105.1 11.9 %all-to-all-done.3 = f32[8,8,128]{2,1,0:T(8,128)S(1)} async-done(((f32[8,8,128]{2,1,0:T(8,128)}), f32[8,8,128]{2,1,0:T(8,128)S(1)}, u32[]{:S(2)}, u32[]{:S(2)}) %all-to-all-start.3) | async-done | bytes 32800 | tf_op jit(solution)/shard_map/all_to_all | solution.py:87
  117.0 0.7 dynamic-slice_add_fusion
  117.7 0.7 broadcast_in_dim.37
  118.4 7.7 %all-to-all-start.4 = ((f32[64,8,128]{2,1,0:T(8,128)}), f32[64,8,128]{2,1,0:T(8,128)S(1)}, u32[]{:S(2)}, u32[]{:S(2)}) async-start(f32[64,8,128]{2,1,0:T(8,128)} %broadcast_in_dim.37), calls=%async_computation.4 | async-start | bytes 524288 | tf_op jit(solution)/shard_map/all_to_all | solution.py:87
  126.1 3.4 %collective-permute-start.4 = (f32[16,128]{1,0:T(8,128)S(1)}, f32[16,128]{1,0:T(8,128)S(1)}, u32[]{:S(2)}, u32[]{:S(2)}) collective-permute-start(f32[16,128]{1,0:T(8,128)S(1)} %get-tuple-element.19), channel_id=1, source_target_pairs={{0,16},{16,0},{32,48},{48,32},{1,17},{17,1},{33,49},{49,33},{2,18}... | collective-permute-start | bytes 24584 | tf_op jit(solution)/shard_map/ppermute | solution.py:186
  129.5 2.4 %collective-permute-start.5 = (f32[16,128]{1,0:T(8,128)S(1)}, f32[16,128]{1,0:T(8,128)S(1)}, u32[]{:S(2)}, u32[]{:S(2)}) collective-permute-start(f32[16,128]{1,0:T(8,128)S(1)} %get-tuple-element.18), channel_id=1, source_target_pairs={{0,32},{16,48},{32,0},{48,16},{1,33},{17,49},{33,1},{49,17},{2,34}... | collective-permute-start | bytes 24584 | tf_op jit(solution)/shard_map/ppermute | solution.py:186
  131.9 2.0 %collective-permute-start.6 = (f32[16,128]{1,0:T(8,128)S(1)}, f32[16,128]{1,0:T(8,128)S(1)}, u32[]{:S(2)}, u32[]{:S(2)}) collective-permute-start(f32[16,128]{1,0:T(8,128)S(1)} %get-tuple-element.17), channel_id=1, source_target_pairs={{0,48},{16,32},{32,16},{48,0},{1,49},{17,33},{33,17},{49,1},{2,50}... | collective-permute-start | bytes 24584 | tf_op jit(solution)/shard_map/ppermute | solution.py:186
  133.9 0.0 collective-permute-done.4
  133.9 0.0 collective-permute-done.5
  133.9 2.9 %collective-permute-done.6 = f32[16,128]{1,0:T(8,128)S(1)} collective-permute-done((f32[16,128]{1,0:T(8,128)S(1)}, f32[16,128]{1,0:T(8,128)S(1)}, u32[]{:S(2)}, u32[]{:S(2)}) %collective-permute-start.6) | collective-permute-done | bytes 8224 | tf_op jit(solution)/shard_map/ppermute | solution.py:186
  136.9 0.6 fusion.9
  137.5 0.0 all-to-all-done.4
  137.5 0.7 copy.42
  (19 shorter events, 0.3 us)
Async XLA Ops:
  0.6 14.6 %copy-start = (f32[16,512]{1,0:T(8,128)S(1)}, f32[16,512]{1,0:T(8,128)}, u32[]{:S(2)}) copy-start(f32[16,512]{1,0:T(8,128)} %param.10) | copy-start | bytes 98308
  1.7 8.1 %collective-permute-start = (f32[256,256]{1,0:T(8,128)S(1)}, f32[256,256]{1,0:T(8,128)S(1)}, u32[]{:S(2)}, u32[]{:S(2)}) collective-permute-start(f32[256,256]{1,0:T(8,128)S(1)} %bitcast.74), channel_id=1, source_target_pairs={{0,1},{1,0},{2,3},{3,2},{4,5},{5,4},{6,7},{7,6},{8,9},{9,8},{10,11... | collective-permute-start | bytes 786440 | tf_op jit(solution)/shard_map/ppermute | solution.py:125
  9.9 34.2 %collective-permute-start.1 = (f32[256,512]{1,0:T(8,128)S(1)}, f32[256,512]{1,0:T(8,128)S(1)}, u32[]{:S(2)}, u32[]{:S(2)}) collective-permute-start(f32[256,512]{1,0:T(8,128)S(1)} %maximum_select_fusion.3), channel_id=1, source_target_pairs={{0,16},{16,0},{1,17},{17,1},{2,18},{18,2},{3,19},{19,3},{4,20},{20... | collective-permute-start | bytes 1572872 | tf_op jit(solution)/shard_map/ppermute | solution.py:127
  15.3 19.1 %collective-permute-start.3 = (f32[16,512]{1,0:T(8,128)S(1)}, f32[16,512]{1,0:T(8,128)S(1)}, u32[]{:S(2)}, u32[]{:S(2)}) collective-permute-start(f32[16,512]{1,0:T(8,128)S(1)} %broadcast_multiply_fusion.1), channel_id=1, source_target_pairs={{0,128},{1,337},{2,481},{3,369},{4,129},{5,145},{6,161},{7,305},{8... | collective-permute-start | bytes 98312 | tf_op jit(solution)/shard_map/ppermute | solution.py:120
  35.3 18.2 %all-to-all-start = ((f32[64,16,128]{2,1,0:T(8,128)}), f32[64,16,128]{2,1,0:T(8,128)S(1)}, u32[]{:S(2)}, u32[]{:S(2)}) async-start(f32[64,16,128]{2,1,0:T(8,128)} %bitcast.12), calls=%async_computation | async-start | bytes 1048576 | tf_op jit(solution)/shard_map/all_to_all | solution.py:145
  45.3 4.8 %collective-permute-start.2 = (f32[256,1024]{1,0:T(8,128)}, f32[256,1024]{1,0:T(8,128)S(1)}, u32[]{:S(2)}, u32[]{:S(2)}) collective-permute-start(f32[256,1024]{1,0:T(8,128)} %maximum_select_fusion.1), channel_id=1, source_target_pairs={{0,32},{32,0},{1,33},{33,1},{2,34},{34,2},{3,35},{35,3},{4,36},{36... | collective-permute-start | bytes 3145736 | tf_op jit(solution)/shard_map/ppermute | solution.py:129
  56.0 30.5 %all-to-all-start.1 = ((f32[8,64,128]{2,1,0:T(8,128)}), f32[8,64,128]{2,1,0:T(8,128)S(1)}, u32[]{:S(2)}, u32[]{:S(2)}) async-start(f32[8,64,128]{2,1,0:T(8,128)} %fusion.21), calls=%async_computation.1 | async-start | bytes 524288 | tf_op jit(solution)/shard_map/all_to_all | solution.py:152
  68.8 8.1 %collective-permute-start.8 = (f32[16,128]{0,1:T(8,128)S(1)}, f32[16,128]{0,1:T(8,128)S(1)}, u32[]{:S(2)}, u32[]{:S(2)}) collective-permute-start(f32[16,128]{0,1:T(8,128)S(1)} %bitcast.77), channel_id=1, source_target_pairs={{0,32},{16,48},{32,0},{48,16},{1,33},{17,49},{33,1},{49,17},{2,34}... | collective-permute-start | bytes 24584 | tf_op jit(solution)/shard_map/ppermute | solution.py:165
  71.5 5.9 %collective-permute-start.9 = (f32[16,128]{0,1:T(8,128)S(1)}, f32[16,128]{0,1:T(8,128)S(1)}, u32[]{:S(2)}, u32[]{:S(2)}) collective-permute-start(f32[16,128]{0,1:T(8,128)S(1)} %bitcast.78), channel_id=1, source_target_pairs={{0,48},{16,32},{32,16},{48,0},{1,49},{17,33},{33,17},{49,1},{2,50}... | collective-permute-start | bytes 24584 | tf_op jit(solution)/shard_map/ppermute | solution.py:165
  73.5 5.4 %collective-permute-start.7 = (f32[16,128]{0,1:T(8,128)S(1)}, f32[16,128]{0,1:T(8,128)S(1)}, u32[]{:S(2)}, u32[]{:S(2)}) collective-permute-start(f32[16,128]{0,1:T(8,128)S(1)} %bitcast.76), channel_id=1, source_target_pairs={{0,16},{16,0},{32,48},{48,32},{1,17},{17,1},{33,49},{49,33},{2,18}... | collective-permute-start | bytes 24584 | tf_op jit(solution)/shard_map/ppermute | solution.py:165
  100.0 16.9 %all-to-all-start.3 = ((f32[8,8,128]{2,1,0:T(8,128)}), f32[8,8,128]{2,1,0:T(8,128)S(1)}, u32[]{:S(2)}, u32[]{:S(2)}) async-start(f32[8,8,128]{2,1,0:T(8,128)} %broadcast_in_dim.36), calls=%async_computation.3 | async-start | bytes 65536 | tf_op jit(solution)/shard_map/all_to_all | solution.py:87
  118.4 19.1 %all-to-all-start.4 = ((f32[64,8,128]{2,1,0:T(8,128)}), f32[64,8,128]{2,1,0:T(8,128)S(1)}, u32[]{:S(2)}, u32[]{:S(2)}) async-start(f32[64,8,128]{2,1,0:T(8,128)} %broadcast_in_dim.37), calls=%async_computation.4 | async-start | bytes 524288 | tf_op jit(solution)/shard_map/all_to_all | solution.py:87
  126.1 7.8 %collective-permute-start.4 = (f32[16,128]{1,0:T(8,128)S(1)}, f32[16,128]{1,0:T(8,128)S(1)}, u32[]{:S(2)}, u32[]{:S(2)}) collective-permute-start(f32[16,128]{1,0:T(8,128)S(1)} %get-tuple-element.19), channel_id=1, source_target_pairs={{0,16},{16,0},{32,48},{48,32},{1,17},{17,1},{33,49},{49,33},{2,18}... | collective-permute-start | bytes 24584 | tf_op jit(solution)/shard_map/ppermute | solution.py:186
  129.5 4.4 %collective-permute-start.5 = (f32[16,128]{1,0:T(8,128)S(1)}, f32[16,128]{1,0:T(8,128)S(1)}, u32[]{:S(2)}, u32[]{:S(2)}) collective-permute-start(f32[16,128]{1,0:T(8,128)S(1)} %get-tuple-element.18), channel_id=1, source_target_pairs={{0,32},{16,48},{32,0},{48,16},{1,33},{17,49},{33,1},{49,17},{2,34}... | collective-permute-start | bytes 24584 | tf_op jit(solution)/shard_map/ppermute | solution.py:186
  131.9 5.0 %collective-permute-start.6 = (f32[16,128]{1,0:T(8,128)S(1)}, f32[16,128]{1,0:T(8,128)S(1)}, u32[]{:S(2)}, u32[]{:S(2)}) collective-permute-start(f32[16,128]{1,0:T(8,128)S(1)} %get-tuple-element.17), channel_id=1, source_target_pairs={{0,48},{16,32},{32,16},{48,0},{1,49},{17,33},{33,17},{49,1},{2,50}... | collective-permute-start | bytes 24584 | tf_op jit(solution)/shard_map/ppermute | solution.py:186

commit v6 on v5

--- a/solution.py
+++ b/solution.py
@@ -104,8 +104,7 @@
     prow_index = lax.axis_index(ROW)
     pcol_index = lax.axis_index(COL)
     core, side, odd = lax.axis_index("c"), lax.axis_index("yl"), lax.axis_index("zl")
-    mine = core * YL + side
-    row_count, _ = panels.shape
+    row_count, width = panels.shape
     row_span, col_span = ancestor_inverse.shape
     chunks = col_span // row_count
     pairs, groups = routes(chunks)
@@ -118,6 +117,12 @@
     active_own = panels * own_keep
 
     moved = lax.ppermute(active_own, ALL, pairs)
+
+    own_nodes = active_own.reshape(row_count, S, W).transpose(1, 0, 2)
+    copies = jnp.broadcast_to(own_nodes[:, None], (S, ZH, row_count, W))
+    active_group = lax.all_to_all(
+        copies.reshape(S * ZH, row_count, W), ("c", "yl", "zh"), 0, 0, tiled=True
+    )
 
     blocks = ancestor_inverse.reshape(YL, ZH, ZL, row_count, col_span)
     kept = pick(odd, blocks[:, :, 0], blocks[:, :, 1]).reshape(-1, col_span)
@@ -136,7 +141,7 @@
         marks = jnp.repeat(marks.astype(jnp.float32), col_span, axis=1)
         return rows.reshape(YL, ZH, row_count, -1) * marks[:, None, None, :]
 
-    rows = jnp.stack([masked(four, prow_index), masked(other, prow_index ^ 1)])
+    rows = in_order(core, masked(four, prow_index)[None], masked(other, prow_index ^ 1)[None], 0)
     rows = rows.transpose(2, 0, 1, 3, 4).reshape(row_span, YL * ZL * col_span)
 
     by_node = moved.reshape(row_count, S, W).transpose(1, 0, 2)
@@ -148,51 +153,34 @@
         needed.reshape(-1, W),
         precision=lax.Precision.HIGHEST,
         preferred_element_type=jnp.float32,
-    ).reshape(ZH, CS * YL * row_count, W)
-    parts = lax.all_to_all(partial_value, "zh", 0, 0, tiled=True)
-    summed = jnp.sum(parts, axis=0).reshape(CS, YL, row_count, W)
-
-    shifts = ((0, 1), (1, 0), (1, 1))
-    swaps = [
-        [(m, m ^ (dc * YL + dy)) for m in range(CS * YL)] for dc, dy in shifts
-    ]
-    own_nodes = active_own.reshape(row_count, S, W)
-
-    def node(index):
-        return lax.dynamic_slice_in_dim(own_nodes, index, 1, 1)[:, 0]
-
-    a01, a10, a11 = [
-        lax.ppermute(node(mine ^ (dc * YL + dy)), ("c", "yl"), swap)
-        for (dc, dy), swap in zip(shifts, swaps)
-    ]
-    a00 = node(mine)
-    active_group = jnp.concatenate(
-        [pick(side, a00, a01), pick(side, a01, a00), pick(side, a10, a11), pick(side, a11, a10)]
-    )
-    local_diag = jnp.dot(
-        active_group.T, summed.reshape(-1, W), precision=lax.Precision.HIGHEST
+    ).reshape(ZH, CS * YL, row_count, W)
+    local_diag = lax.dot_general(
+        active_group.reshape(-1, W),
+        partial_value.transpose(1, 0, 2, 3).reshape(-1, W),
+        (((0,), (0,)), ((), ())),
+        precision=lax.Precision.HIGHEST,
     )
     peers = lax.axis_size(SIDE)
     part = W // peers
     terms = lax.all_to_all(local_diag.reshape(peers, part, W), SIDE, 0, 0, tiled=True)
     terms = jnp.sum(terms, axis=0)
-    terms = jnp.sum(spread(terms, "zh"), axis=0)
+    members = CS * YL
+    copies = jnp.broadcast_to(terms[None], (ZH, part, W))
+    both = jnp.concatenate(
+        [partial_value.reshape(ZH, members * row_count, W), copies], axis=1
+    )
+    both = jnp.sum(lax.all_to_all(both, "zh", 0, 0, tiled=True), axis=0)
+    summed = both[: members * row_count].reshape(CS, YL, row_count, W)
     own_part = lax.axis_index(BACK) * part
-    terms = lax.dynamic_slice_in_dim(diag_inverse.reshape(S * W, W), own_part, part, 0) + terms
-    diag_blocks = spread(terms, BACK).reshape(S, W, W)
+    own_diag = lax.dynamic_slice_in_dim(diag_inverse.reshape(S * W, W), own_part, part, 0)
+    diag_blocks = spread(own_diag + both[members * row_count :], BACK).reshape(S, W, W)
 
-    r00 = pick(side, summed[0, 0], summed[0, 1])
-    r01, r10, r11 = [
-        lax.ppermute(pick(side ^ dy, summed[dc, 0], summed[dc, 1]), ("c", "yl"), swap)
-        for (dc, dy), swap in zip(shifts, swaps)
-    ]
-    columns = []
-    for k in range(S):
-        which = mine ^ k
-        columns.append(
-            jnp.where(which < 2, jnp.where(which == 0, r00, r01), jnp.where(which == 2, r10, r11))
-        )
-    inverse_panels = -(own_keep * jnp.concatenate(columns, axis=1))
+    from_core = lax.ppermute(pick(core, summed[1], summed[0]), "c", SWAP)
+    held = in_order(core, pick(core, summed[0], summed[1])[None], from_core[None], 0)
+    from_side = lax.ppermute(pick(side, held[:, 1], held[:, 0]), "yl", SWAP)
+    nodes = in_order(side, pick(side, held[:, 0], held[:, 1])[:, None], from_side[:, None], 1)
+    full = nodes.reshape(S, row_count, W).transpose(1, 0, 2).reshape(row_count, width)
+    inverse_panels = -(own_keep * full)
     return (inverse_panels, diag_blocks)
 
 

time: 139 us -> 144 us (1.036)
  waiting for transfers between devices: 42.5 us -> 48.2 us
  other arithmetic: 5.09 us -> 7.91 us
  starting transfers between devices: 69.1 us -> 66.7 us
    all_to_all x1 -> x2, starting transfers between devices: 12.6 us -> 26.9 us  [the longest x1 17.8 us: body(): lax.all_to_all(copies.reshape(S * ZH, row_count, W), ('c', 'yl', 'zh'), 0...]
    ppermute x1, waiting for transfers between devices: 2.66 us -> 14.9 us  [body(): came = lax.ppermute(sent, 'zl', SWAP)]
    all_to_all x1 -> x2, waiting for transfers between devices: 7.56 us -> 18.9 us  [the longest x1 18.9 us: body(): both = jnp.sum(lax.all_to_all(both, 'zh', 0, 0, tiled=True), axis=0)]
    all_to_all x2 -> x1, waiting for transfers between devices: 11.9 us -> 1.16 us  [spread(): return lax.all_to_all(copies, axis, 0, 0, tiled=True)]
    ppermute x6 -> x2, starting transfers between devices: 15.5 us -> 5.62 us  [the longest x1 3.36 us: body(): from_side = lax.ppermute(pick(side, held[:, 1], held[:, 0]), 'yl', SWAP)]
    all_to_all x2 -> x1, starting transfers between devices: 12.8 us -> 8.8 us  [spread(): return lax.all_to_all(copies, axis, 0, 0, tiled=True)]
    ppermute x1, waiting for transfers between devices: 11.7 us -> 8.58 us  [body(): moved = lax.ppermute(active_own, ALL, pairs)]
    all_to_all x1, starting transfers between devices: 8.84 us -> 11.7 us  [body(): lax.all_to_all(outgoing, ALL, 0, 0, tiled=True, axis_index_groups=groups)]
  transfers between devices with their start and end apart: 14 -> 10, of which waited for: 9 -> 8; matrix products, arithmetic and copies ran while one was open for 5% -> 5% of each run, Pallas kernels for 0% -> 0%
where the time goes in v6:
time: 144 us; the launch traced here: 143 us
  starting transfers between devices  66.7 us (46%)
  waiting for transfers between devices  48.2 us (33%)
  blocking collectives  12.4 us (9%)
  other arithmetic  7.91 us (5%)
  local copies, waits for them, and re-layouts  4.84 us (3%)
  matrix products  2.18 us (2%)
    all_to_all x1, waiting for transfers between devices, body(): both = jnp.sum(lax.all_to_all(both, 'zh', 0, 0, tiled=True), axis=0)  18.9 us
    all_to_all x1, starting transfers between devices, body(): lax.all_to_all(copies.reshape(S * ZH, row_count, W), ('c', 'yl', 'zh'), 0...  17.8 us
    ppermute x1, waiting for transfers between devices, body(): came = lax.ppermute(sent, 'zl', SWAP)  14.9 us
    all_to_all x1, blocking collectives, body(): lax.all_to_all(local_diag.reshape(peers, part, W), SIDE, 0, 0, tiled=True)  12.4 us
    all_to_all x1, starting transfers between devices, body(): lax.all_to_all(outgoing, ALL, 0, 0, tiled=True, axis_index_groups=groups)  11.7 us
    all_to_all x1, starting transfers between devices, body(): both = jnp.sum(lax.all_to_all(both, 'zh', 0, 0, tiled=True), axis=0)  9.19 us
    all_to_all x1, starting transfers between devices, spread(): return lax.all_to_all(copies, axis, 0, 0, tiled=True)  8.8 us
    ppermute x1, waiting for transfers between devices, body(): moved = lax.ppermute(active_own, ALL, pairs)  8.58 us
  transfers between devices with their start and end apart: 10, of which 8 were waited for; matrix products, arithmetic and copies ran while one was open for 5% of the time, Pallas kernels for 0%

profile of v6, /device:TPU:1, one launch (start us, length us, event | category | flops | bytes accessed | tf_op | source)
XLA Modules:
  0.0 143.2 jit_solution(11089740182810663113)
XLA Ops:
  0.7 0.8 compare_reduce_fusion
  1.5 0.2 dynamic-slice_reduce_fusion
  1.6 0.1 broadcast_bitcast_fusion.2
  1.7 0.8 broadcast_multiply_fusion.1
  2.5 0.7 broadcast_in_dim.25
  3.2 17.8 %all-to-all-start.1 = ((f32[32,16,128]{2,1,0:T(8,128)}), f32[32,16,128]{2,1,0:T(8,128)S(1)}, u32[]{:S(2)}, u32[]{:S(2)}) async-start(f32[32,16,128]{2,1,0:T(8,128)} %bitcast.16), calls=%async_computation.1 | async-start | bytes 524288 | tf_op jit(solution)/shard_map/all_to_all | solution.py:123
  21.0 1.1 slice_select_fusion.1
  22.1 2.6 %collective-permute-start = (f32[256,256]{1,0:T(8,128)S(1)}, f32[256,256]{1,0:T(8,128)S(1)}, u32[]{:S(2)}, u32[]{:S(2)}) collective-permute-start(f32[256,256]{1,0:T(8,128)S(1)} %bitcast.74), channel_id=1, source_target_pairs={{0,1},{1,0},{2,3},{3,2},{4,5},{5,4},{6,7},{7,6},{8,9},{9,8},{10,11... | collective-permute-start | bytes 786440 | tf_op jit(solution)/shard_map/ppermute | solution.py:130
  24.7 14.9 %collective-permute-done = f32[256,256]{1,0:T(8,128)S(1)} collective-permute-done((f32[256,256]{1,0:T(8,128)S(1)}, f32[256,256]{1,0:T(8,128)S(1)}, u32[]{:S(2)}, u32[]{:S(2)}) %collective-permute-start) | collective-permute-done | bytes 262176 | tf_op jit(solution)/shard_map/ppermute | solution.py:130
  39.7 3.0 %collective-permute-start.1 = (f32[256,512]{1,0:T(8,128)S(1)}, f32[256,512]{1,0:T(8,128)S(1)}, u32[]{:S(2)}, u32[]{:S(2)}) collective-permute-start(f32[256,512]{1,0:T(8,128)S(1)} %maximum_select_fusion.4), channel_id=1, source_target_pairs={{0,16},{16,0},{1,17},{17,1},{2,18},{18,2},{3,19},{19,3},{4,20},{20... | collective-permute-start | bytes 1572872 | tf_op jit(solution)/shard_map/ppermute | solution.py:132
  42.8 5.7 %collective-permute-start.3 = (f32[16,512]{1,0:T(8,128)S(1)}, f32[16,512]{1,0:T(8,128)S(1)}, u32[]{:S(2)}, u32[]{:S(2)}) collective-permute-start(f32[16,512]{1,0:T(8,128)S(1)} %broadcast_multiply_fusion.1), channel_id=1, source_target_pairs={{0,128},{1,337},{2,481},{3,369},{4,129},{5,145},{6,161},{7,305},{8... | collective-permute-start | bytes 98312 | tf_op jit(solution)/shard_map/ppermute | solution.py:119
  48.5 8.6 %collective-permute-done.3 = f32[16,512]{1,0:T(8,128)S(1)} collective-permute-done((f32[16,512]{1,0:T(8,128)S(1)}, f32[16,512]{1,0:T(8,128)S(1)}, u32[]{:S(2)}, u32[]{:S(2)}) %collective-permute-start.3) | collective-permute-done | bytes 32800 | tf_op jit(solution)/shard_map/ppermute | solution.py:119
  57.1 0.0 all-to-all-done.1
  57.1 0.8 broadcast_in_dim.24
  57.9 11.7 %all-to-all-start = ((f32[64,16,128]{2,1,0:T(8,128)}), f32[64,16,128]{2,1,0:T(8,128)S(1)}, u32[]{:S(2)}, u32[]{:S(2)}) async-start(f32[64,16,128]{2,1,0:T(8,128)} %bitcast.12), calls=%async_computation | async-start | bytes 1048576 | tf_op jit(solution)/shard_map/all_to_all | solution.py:150
  69.6 0.0 collective-permute-done.1
  69.7 1.2 maximum_select_fusion.2
  70.8 2.3 %collective-permute-start.2 = (f32[256,1024]{1,0:T(8,128)}, f32[256,1024]{1,0:T(8,128)}, u32[]{:S(2)}, u32[]{:S(2)}) collective-permute-start(f32[256,1024]{1,0:T(8,128)} %maximum_select_fusion.2), channel_id=1, source_target_pairs={{0,32},{32,0},{1,33},{33,1},{2,34},{34,2},{3,35},{35,3},{4,36},{36... | collective-permute-start | bytes 3145736 | tf_op jit(solution)/shard_map/ppermute | solution.py:134
  73.1 0.8 constant_dynamic-slice_fusion.1
  73.9 0.1 reshape.248
  74.0 0.1 reshape.250
  74.1 0.1 convert_element_type.19
  74.2 0.1 broadcast_bitcast_fusion
  74.3 0.1 convert_element_type.17
  74.4 0.1 broadcast_bitcast_fusion.1
  74.5 0.2 fusion.1
  74.7 0.1 copy.48
  74.8 0.9 collective-permute-done.2
  75.7 1.3 broadcast_multiply_fusion
  77.1 0.2 fusion
  77.3 0.1 copy.45
  77.5 1.5 %all-to-all-done = f32[64,16,128]{2,1,0:T(8,128)S(1)} async-done(((f32[64,16,128]{2,1,0:T(8,128)}), f32[64,16,128]{2,1,0:T(8,128)S(1)}, u32[]{:S(2)}, u32[]{:S(2)}) %all-to-all-start) | async-done | bytes 524320 | tf_op jit(solution)/shard_map/all_to_all | solution.py:150
  79.0 1.8 %fusion.7 = f32[512,128]{1,0:T(8,128)S(1)} fusion(f32[512,1024]{1,0:T(8,128)S(1)} %bitcast.62, f32[1024,128]{1,0:T(8,128)S(1)} %bitcast.68), kind=kOutput, calls=%fused_computation.34 | convolution fusion | flops 805306368 | bytes 2883584 | tf_op jit(solution)/shard_map/dot_general | solution.py:151
  80.8 0.4 fusion.3
  81.2 12.4 %all_to_all.25 = f32[16,8,128]{2,1,0:T(8,128)S(1)} all-to-all(f32[16,8,128]{2,1,0:T(8,128)S(1)} %fusion.3), channel_id=1, replica_groups=mesh['yh'=2,'x'=4,'c'=2,'yl'=2,'zh'=8,'zl'=2] {'yh','x','zl'}, dimensions={0} | all-to-all | bytes 131072 | tf_op jit(solution)/shard_map/all_to_all | solution.py:165
  93.6 0.7 pad_maximum_fusion
  94.4 9.2 %all-to-all-start.3 = ((f32[8,72,128]{2,1,0:T(8,128)}), f32[8,72,128]{2,1,0:T(8,128)S(1)}, u32[]{:S(2)}, u32[]{:S(2)}) async-start(f32[8,72,128]{2,1,0:T(8,128)} %pad_maximum_fusion), calls=%async_computation.3 | async-start | bytes 589824 | tf_op jit(solution)/shard_map/all_to_all | solution.py:172
  103.5 18.9 %all-to-all-done.3 = f32[8,72,128]{2,1,0:T(8,128)S(1)} async-done(((f32[8,72,128]{2,1,0:T(8,128)}), f32[8,72,128]{2,1,0:T(8,128)S(1)}, u32[]{:S(2)}, u32[]{:S(2)}) %all-to-all-start.3) | async-done | bytes 294944 | tf_op jit(solution)/shard_map/all_to_all | solution.py:172
  122.4 0.7 slice_add_fusion
  123.1 0.7 broadcast_in_dim.56
  123.9 8.8 %all-to-all-start.4 = ((f32[64,8,128]{2,1,0:T(8,128)}), f32[64,8,128]{2,1,0:T(8,128)S(1)}, u32[]{:S(2)}, u32[]{:S(2)}) async-start(f32[64,8,128]{2,1,0:T(8,128)} %broadcast_in_dim.56), calls=%async_computation.4 | async-start | bytes 524288 | tf_op jit(solution)/shard_map/all_to_all | solution.py:87
  132.7 2.3 %collective-permute-start.4 = (f32[2,16,128]{2,1,0:T(8,128)S(1)}, f32[2,16,128]{2,1,0:T(8,128)S(1)}, u32[]{:S(2)}, u32[]{:S(2)}) collective-permute-start(f32[2,16,128]{2,1,0:T(8,128)S(1)} %bitcast.85), channel_id=1, source_target_pairs={{0,32},{32,0},{1,33},{33,1},{2,34},{34,2},{3,35},{35,3},{4,36},{36... | collective-permute-start | bytes 49160 | tf_op jit(solution)/shard_map/ppermute | solution.py:178
  134.9 0.8 collective-permute-done.4
  135.8 0.1 maximum_select_fusion.5
  135.8 3.4 %collective-permute-start.5 = (f32[2,16,128]{2,0,1:T(2,128)S(1)}, f32[2,16,128]{2,0,1:T(2,128)S(1)}, u32[]{:S(2)}, u32[]{:S(2)}) collective-permute-start(f32[2,16,128]{2,0,1:T(2,128)S(1)} %get-tuple-element.7), channel_id=1, source_target_pairs={{0,16},{16,0},{1,17},{17,1},{2,18},{18,2},{3,19},{19,3},{4,20},{20... | collective-permute-start | bytes 49160 | tf_op jit(solution)/shard_map/ppermute | solution.py:180
  139.2 1.4 collective-permute-done.5
  140.6 0.1 maximum_select_fusion.6
  140.7 0.6 fusion.5
  141.3 1.2 all-to-all-done.4
  142.5 0.7 copy.60
  (17 shorter events, 0.3 us)
Async XLA Ops:
  3.2 53.8 %all-to-all-start.1 = ((f32[32,16,128]{2,1,0:T(8,128)}), f32[32,16,128]{2,1,0:T(8,128)S(1)}, u32[]{:S(2)}, u32[]{:S(2)}) async-start(f32[32,16,128]{2,1,0:T(8,128)} %bitcast.16), calls=%async_computation.1 | async-start | bytes 524288 | tf_op jit(solution)/shard_map/all_to_all | solution.py:123
  22.1 17.6 %collective-permute-start = (f32[256,256]{1,0:T(8,128)S(1)}, f32[256,256]{1,0:T(8,128)S(1)}, u32[]{:S(2)}, u32[]{:S(2)}) collective-permute-start(f32[256,256]{1,0:T(8,128)S(1)} %bitcast.74), channel_id=1, source_target_pairs={{0,1},{1,0},{2,3},{3,2},{4,5},{5,4},{6,7},{7,6},{8,9},{9,8},{10,11... | collective-permute-start | bytes 786440 | tf_op jit(solution)/shard_map/ppermute | solution.py:130
  39.7 29.9 %collective-permute-start.1 = (f32[256,512]{1,0:T(8,128)S(1)}, f32[256,512]{1,0:T(8,128)S(1)}, u32[]{:S(2)}, u32[]{:S(2)}) collective-permute-start(f32[256,512]{1,0:T(8,128)S(1)} %maximum_select_fusion.4), channel_id=1, source_target_pairs={{0,16},{16,0},{1,17},{17,1},{2,18},{18,2},{3,19},{19,3},{4,20},{20... | collective-permute-start | bytes 1572872 | tf_op jit(solution)/shard_map/ppermute | solution.py:132
  42.8 14.3 %collective-permute-start.3 = (f32[16,512]{1,0:T(8,128)S(1)}, f32[16,512]{1,0:T(8,128)S(1)}, u32[]{:S(2)}, u32[]{:S(2)}) collective-permute-start(f32[16,512]{1,0:T(8,128)S(1)} %broadcast_multiply_fusion.1), channel_id=1, source_target_pairs={{0,128},{1,337},{2,481},{3,369},{4,129},{5,145},{6,161},{7,305},{8... | collective-permute-start | bytes 98312 | tf_op jit(solution)/shard_map/ppermute | solution.py:119
  57.9 21.1 %all-to-all-start = ((f32[64,16,128]{2,1,0:T(8,128)}), f32[64,16,128]{2,1,0:T(8,128)S(1)}, u32[]{:S(2)}, u32[]{:S(2)}) async-start(f32[64,16,128]{2,1,0:T(8,128)} %bitcast.12), calls=%async_computation | async-start | bytes 1048576 | tf_op jit(solution)/shard_map/all_to_all | solution.py:150
  70.8 4.9 %collective-permute-start.2 = (f32[256,1024]{1,0:T(8,128)}, f32[256,1024]{1,0:T(8,128)}, u32[]{:S(2)}, u32[]{:S(2)}) collective-permute-start(f32[256,1024]{1,0:T(8,128)} %maximum_select_fusion.2), channel_id=1, source_target_pairs={{0,32},{32,0},{1,33},{33,1},{2,34},{34,2},{3,35},{35,3},{4,36},{36... | collective-permute-start | bytes 3145736 | tf_op jit(solution)/shard_map/ppermute | solution.py:134
  94.4 28.1 %all-to-all-start.3 = ((f32[8,72,128]{2,1,0:T(8,128)}), f32[8,72,128]{2,1,0:T(8,128)S(1)}, u32[]{:S(2)}, u32[]{:S(2)}) async-start(f32[8,72,128]{2,1,0:T(8,128)} %pad_maximum_fusion), calls=%async_computation.3 | async-start | bytes 589824 | tf_op jit(solution)/shard_map/all_to_all | solution.py:172
  123.9 18.6 %all-to-all-start.4 = ((f32[64,8,128]{2,1,0:T(8,128)}), f32[64,8,128]{2,1,0:T(8,128)S(1)}, u32[]{:S(2)}, u32[]{:S(2)}) async-start(f32[64,8,128]{2,1,0:T(8,128)} %broadcast_in_dim.56), calls=%async_computation.4 | async-start | bytes 524288 | tf_op jit(solution)/shard_map/all_to_all | solution.py:87
  132.7 3.1 %collective-permute-start.4 = (f32[2,16,128]{2,1,0:T(8,128)S(1)}, f32[2,16,128]{2,1,0:T(8,128)S(1)}, u32[]{:S(2)}, u32[]{:S(2)}) collective-permute-start(f32[2,16,128]{2,1,0:T(8,128)S(1)} %bitcast.85), channel_id=1, source_target_pairs={{0,32},{32,0},{1,33},{33,1},{2,34},{34,2},{3,35},{35,3},{4,36},{36... | collective-permute-start | bytes 49160 | tf_op jit(solution)/shard_map/ppermute | solution.py:178
  135.8 4.8 %collective-permute-start.5 = (f32[2,16,128]{2,0,1:T(2,128)S(1)}, f32[2,16,128]{2,0,1:T(2,128)S(1)}, u32[]{:S(2)}, u32[]{:S(2)}) collective-permute-start(f32[2,16,128]{2,0,1:T(2,128)S(1)} %get-tuple-element.7), channel_id=1, source_target_pairs={{0,16},{16,0},{1,17},{17,1},{2,18},{18,2},{3,19},{19,3},{4,20},{20... | collective-permute-start | bytes 49160 | tf_op jit(solution)/shard_map/ppermute | solution.py:180

commit v7 on v4

--- a/solution.py
+++ b/solution.py
@@ -8,14 +8,79 @@
 BLK = 256
 W = 128
 S = 4
+YH, XS, CS, YL, ZH, ZL = 2, 4, 2, 2, 8, 2
 ROW = ("yh", "x", "c")
 COL = ("yl", "zh", "zl")
 DEPTH = ("zh", "zl")
-PLANE = ("yh", "x", "c", "yl")
-SIDE = ("yh", "x", "yl")
-BACK = ("c", "yh", "x", "yl")
+SIDE = ("yh", "x", "yl", "zl")
+BACK = ("c", "yh", "x", "yl", "zl")
 ALL = ("yh", "x", "c", "yl", "zh", "zl")
 SWAP = [(0, 1), (1, 0)]
+
+
+def flat_of(yh, x, c, yl, zh, zl):
+    return ((((yh * XS + x) * CS + c) * YL + yl) * ZH + zh) * ZL + zl
+
+
+def place_of(flat):
+    out = []
+    for size in (ZL, ZH, YL, CS, XS, YH):
+        out.append(flat % size)
+        flat //= size
+    return tuple(reversed(out))
+
+
+def hops(one, two):
+    total = 0
+    for a, b, size in (
+        (one[1], two[1], XS),
+        (one[0] * YL + one[3], two[0] * YL + two[3], YH * YL),
+        (one[4] * ZL + one[5], two[4] * ZL + two[5], ZH * ZL),
+    ):
+        gap = abs(a - b) % size
+        total += min(gap, size - gap)
+    return total
+
+
+def assign(sources, targets):
+    near = [[hops(place_of(s), place_of(t)) for t in targets] for s in sources]
+    owner = {}
+
+    def place(s, limit, seen):
+        for t in sorted(range(len(targets)), key=lambda t: near[s][t]):
+            if near[s][t] > limit or t in seen:
+                continue
+            seen.add(t)
+            if t not in owner or place(owner[t], limit, seen):
+                owner[t] = s
+                return True
+        return False
+
+    limit = 0
+    for s in range(len(sources)):
+        while not place(s, limit, set()):
+            limit += 1
+    return {sources[s]: targets[t] for t, s in owner.items()}
+
+
+def routes(chunks):
+    pairs, groups = [], []
+    for z in range(ZH * ZL):
+        blocks = [h * ZH * ZL + z for h in range(YL)]
+        where = {}
+        for c in range(CS):
+            sources = [q * chunks + j for q in blocks for j in range(c, chunks, CS)]
+            targets = [
+                flat_of(yh, x, c, yl, z // ZL, z % ZL)
+                for yh in range(YH)
+                for x in range(XS)
+                for yl in range(YL)
+            ]
+            where.update(assign(sources, targets))
+        order = [q * chunks + j for q in blocks for j in range(chunks)]
+        pairs += [(source, where[source]) for source in order]
+        groups.append([where[source] for source in order])
+    return pairs, groups
 
 
 def spread(value, axis):
@@ -45,12 +110,7 @@
     active_own = panels * own_keep
 
     chunks = col_span // row_count
-    plane = lax.axis_size(PLANE)
-    pairs = [
-        (q * chunks + j, (q // deep * chunks + j) * deep + q % deep)
-        for q in range(cols)
-        for j in range(chunks)
-    ]
+    pairs, groups = routes(chunks)
     moved = lax.ppermute(active_own, ALL, pairs)
 
     by_core = active_own.reshape(row_count, 2, half).transpose(1, 0, 2)
@@ -86,12 +146,12 @@
     leave = jnp.where(odd == 0, pieces[:, 1], pieces[:, 0]).reshape(-1, 2 * col_span)
     stay = jnp.where(odd == 0, pieces[:, 0], pieces[:, 1]).reshape(-1, 2 * col_span)
 
-    halves = moved.reshape(row_count, 2, half).transpose(1, 0, 2)
-    shape = tuple(lax.axis_size(name) for name in PLANE)
-    outgoing = jnp.broadcast_to(
-        halves[None, None, :, None], shape + (row_count, half)
-    ).reshape(plane, row_count, half)
-    needed = lax.all_to_all(outgoing, PLANE, 0, 0, tiled=True).reshape(2 * col_span, half)
+    halves = moved.reshape(row_count, CS, half).transpose(1, 0, 2)
+    outgoing = jnp.broadcast_to(halves[None], (chunks * YL // CS, CS, row_count, half))
+    outgoing = outgoing.reshape(chunks * YL, row_count, half)
+    needed = lax.all_to_all(
+        outgoing, ALL, 0, 0, tiled=True, axis_index_groups=groups
+    ).reshape(2 * col_span, half)
 
     def product(rows):
         value = jnp.dot(
@@ -102,6 +162,11 @@
     leaving = product(leave)
     arrived = lax.ppermute(leaving, "zl", SWAP)
     pair_sum = product(stay) + arrived
+    part = S // 2 * W // lax.axis_size(SIDE)
+    own_diag = lax.dynamic_slice_in_dim(
+        diag_inverse.reshape(S * W, W), lax.axis_index(BACK) * part, part, 0
+    )
+    pair_sum, own_diag = lax.optimization_barrier((pair_sum, own_diag))
     parts = lax.all_to_all(pair_sum, "zh", 0, 0, tiled=True)
     summed = jnp.sum(parts, axis=0).reshape(2, row_count, half)
 
@@ -120,18 +185,15 @@
         precision=lax.Precision.HIGHEST,
     )
     peers = lax.axis_size(SIDE)
-    part = S // 2 * W // peers
     terms = lax.all_to_all(local_diag.reshape(peers, part, W), SIDE, 0, 0, tiled=True)
     terms = jnp.sum(terms, axis=0)
-    terms = jnp.sum(spread(terms, DEPTH), axis=0)
-    own_part = lax.axis_index(BACK) * part
-    terms = lax.dynamic_slice_in_dim(diag_inverse.reshape(S * W, W), own_part, part, 0) + terms
+    terms = own_diag + jnp.sum(spread(terms, "zh"), axis=0)
     diag_blocks = spread(terms, BACK).reshape(S, W, W)
     return (inverse_panels, diag_blocks)
 
 
 def solution(mesh):
-    fine = Mesh(mesh.devices.reshape(2, 4, 2, 2, 8, 2), ALL)
+    fine = Mesh(mesh.devices.reshape(YH, XS, CS, YL, ZH, ZL), ALL)
     placed = (P(ROW, COL), P(), P(), P(), P(ALL, None), P())
     return jax.shard_map(
         body,

time: 135 us -> 135 us (level)
  blocking collectives: 12.4 us -> 30.5 us
  waiting for transfers between devices: 46 us -> 36.6 us
  starting transfers between devices: 64.1 us -> 56.6 us
    all_to_all x0 -> x1, blocking collectives: none -> 15.3 us  [spread(): return lax.all_to_all(copies, axis, 0, 0, tiled=True)]
    all_to_all x2 -> x1, waiting for transfers between devices: 17.1 us -> 5.75 us  [spread(): return lax.all_to_all(copies, axis, 0, 0, tiled=True)]
    all_to_all x2 -> x1, starting transfers between devices: 15.2 us -> 7.56 us  [spread(): return lax.all_to_all(copies, axis, 0, 0, tiled=True)]
    ppermute x1, starting transfers between devices: 5.73 us -> 9.81 us  [body(): moved = lax.ppermute(active_own, ALL, pairs)]
    all_to_all x1, waiting for transfers between devices: 10.5 us -> 6.77 us  [body(): lax.all_to_all(outgoing, ALL, 0, 0, tiled=True, axis_index_groups=groups)]
    ppermute x1, starting transfers between devices: 4.94 us -> 1.92 us  [body(): other_rows = lax.ppermute(own_rows, 'c', SWAP)]
    all_to_all x1, blocking collectives: 12.4 us -> 15.2 us  [body(): lax.all_to_all(local_diag.reshape(peers, part, W), SIDE, 0, 0, tiled=True)]
    all_to_all x1, waiting for transfers between devices: 11 us -> 13.3 us  [body(): parts = lax.all_to_all(pair_sum, 'zh', 0, 0, tiled=True)]
  transfers between devices with their start and end apart: 10 -> 9, of which waited for: 7 -> 7; matrix products, arithmetic and copies ran while one was open for 3% -> 3% of each run, Pallas kernels for 0% -> 0%
where the time goes in v7:
time: 135 us; the launch traced here: 134 us
  starting transfers between devices  56.6 us (42%)
  waiting for transfers between devices  36.6 us (27%)
  blocking collectives  30.5 us (23%)
  local copies, waits for them, and re-layouts  4.47 us (3%)
  other arithmetic  2.45 us (2%)
  matrix products  2.28 us (2%)
    all_to_all x1, blocking collectives, spread(): return lax.all_to_all(copies, axis, 0, 0, tiled=True)  15.3 us
    all_to_all x1, blocking collectives, body(): lax.all_to_all(local_diag.reshape(peers, part, W), SIDE, 0, 0, tiled=True)  15.2 us
    all_to_all x1, starting transfers between devices, body(): lax.all_to_all(outgoing, ALL, 0, 0, tiled=True, axis_index_groups=groups)  13.7 us
    all_to_all x1, waiting for transfers between devices, body(): parts = lax.all_to_all(pair_sum, 'zh', 0, 0, tiled=True)  13.3 us
    all_to_all x1, starting transfers between devices, body(): parts = lax.all_to_all(pair_sum, 'zh', 0, 0, tiled=True)  11.9 us
    ppermute x1, starting transfers between devices, body(): moved = lax.ppermute(active_own, ALL, pairs)  9.81 us
    all_to_all x1, starting transfers between devices, spread(): return lax.all_to_all(copies, axis, 0, 0, tiled=True)  7.56 us
    ppermute x1, waiting for transfers between devices, body(): arrived = lax.ppermute(leaving, 'zl', SWAP)  7.34 us
  transfers between devices with their start and end apart: 9, of which 7 were waited for; matrix products, arithmetic and copies ran while one was open for 3% of the time, Pallas kernels for 0%

profile of v7, /device:TPU:1, one launch (start us, length us, event | category | flops | bytes accessed | tf_op | source)
XLA Modules:
  0.0 133.8 jit_solution(9079177084269817742)
XLA Ops:
  0.6 0.0 copy-start
  0.7 1.1 slice_select_fusion.1
  1.8 4.0 %collective-permute-start = (f32[256,256]{1,0:T(8,128)S(1)}, f32[256,256]{1,0:T(8,128)S(1)}, u32[]{:S(2)}, u32[]{:S(2)}) collective-permute-start(f32[256,256]{1,0:T(8,128)S(1)} %get-tuple-element.11), channel_id=1, source_target_pairs={{0,16},{16,0},{1,17},{17,1},{2,18},{18,2},{3,19},{19,3},{4,20},{20... | collective-permute-start | bytes 786440 | tf_op jit(solution)/shard_map/ppermute | solution.py:125
  5.8 0.0 copy-start.1
  5.8 0.0 copy-start.2
  5.9 0.0 copy-start.3
  5.9 0.7 copy-done.2
  6.5 0.0 copy-done.3
  6.5 0.1 compare_reduce_fusion
  6.6 0.2 dynamic-slice_reduce_fusion
  6.8 0.1 broadcast_bitcast_fusion
  6.9 0.0 copy-done.1
  6.9 9.8 %collective-permute-start.2 = (f32[16,512]{1,0:T(8,128)S(1)}, f32[16,512]{1,0:T(8,128)S(1)}, u32[]{:S(2)}, u32[]{:S(2)}) collective-permute-start(f32[16,512]{1,0:T(8,128)S(1)} %broadcast_multiply_fusion.1), channel_id=1, source_target_pairs={{0,384},{1,416},{2,400},{3,432},{4,144},{5,176},{6,192},{7,96},{8,... | collective-permute-start | bytes 98312 | tf_op jit(solution)/shard_map/ppermute | solution.py:114
  16.7 0.8 fusion.12
  17.5 0.1 reshape.141
  17.6 0.1 reshape.142
  17.7 0.2 fusion.9
  17.9 0.0 collective-permute-done
  18.0 1.9 %collective-permute-start.1 = (f32[256,512]{1,0:T(8,128)S(1)}, f32[256,512]{1,0:T(8,128)S(1)}, u32[]{:S(2)}, u32[]{:S(2)}) collective-permute-start(f32[256,512]{1,0:T(8,128)S(1)} %maximum_select_fusion.1), channel_id=1, source_target_pairs={{0,32},{32,0},{1,33},{33,1},{2,34},{34,2},{3,35},{35,3},{4,36},{36... | collective-permute-start | bytes 1572872 | tf_op jit(solution)/shard_map/ppermute | solution.py:131
  19.9 0.1 broadcast_bitcast_fusion.1
  20.0 0.1 broadcast_bitcast_fusion.2
  20.0 1.8 %collective-permute-done.2 = f32[16,512]{1,0:T(8,128)S(1)} collective-permute-done((f32[16,512]{1,0:T(8,128)S(1)}, f32[16,512]{1,0:T(8,128)S(1)}, u32[]{:S(2)}, u32[]{:S(2)}) %collective-permute-start.2) | collective-permute-done | bytes 32800 | tf_op jit(solution)/shard_map/ppermute | solution.py:114
  21.9 0.8 broadcast_in_dim.35
  22.7 13.7 %all-to-all-start = ((f32[32,16,256]{2,1,0:T(8,128)}), f32[32,16,256]{2,1,0:T(8,128)S(1)}, u32[]{:S(2)}, u32[]{:S(2)}) async-start(f32[32,16,256]{2,1,0:T(8,128)} %bitcast.6), calls=%async_computation | async-start | bytes 1048576 | tf_op jit(solution)/shard_map/all_to_all | solution.py:152
  36.4 0.1 fusion.1
  36.5 0.0 collective-permute-done.1
  36.5 0.1 broadcast_multiply_fusion
  36.6 0.1 broadcast_select_fusion.1
  36.8 6.8 %all-to-all-done = f32[32,16,256]{2,1,0:T(8,128)S(1)} async-done(((f32[32,16,256]{2,1,0:T(8,128)}), f32[32,16,256]{2,1,0:T(8,128)S(1)}, u32[]{:S(2)}, u32[]{:S(2)}) %all-to-all-start) | async-done | bytes 524320 | tf_op jit(solution)/shard_map/all_to_all | solution.py:152
  43.6 0.6 fusion.15
  44.2 1.9 %collective-permute-start.3 = (f32[8,32,256]{2,1,0:T(8,128)S(1)}, f32[8,32,256]{2,1,0:T(8,128)S(1)}, u32[]{:S(2)}, u32[]{:S(2)}) collective-permute-start(f32[8,32,256]{2,1,0:T(8,128)S(1)} %fusion.15), channel_id=1, source_target_pairs={{0,1},{1,0},{2,3},{3,2},{4,5},{5,4},{6,7},{7,6},{8,9},{9,8},{10,11... | collective-permute-start | bytes 786440 | tf_op jit(solution)/shard_map/ppermute | solution.py:163
  46.1 0.0 copy-done
  46.2 7.3 %collective-permute-done.3 = f32[8,32,256]{2,1,0:T(8,128)S(1)} collective-permute-done((f32[8,32,256]{2,1,0:T(8,128)S(1)}, f32[8,32,256]{2,1,0:T(8,128)S(1)}, u32[]{:S(2)}, u32[]{:S(2)}) %collective-permute-start.3) | collective-permute-done | bytes 262176 | tf_op jit(solution)/shard_map/ppermute | solution.py:163
  53.5 1.3 convolution_add_fusion
  54.8 11.9 %all-to-all-start.1 = ((f32[8,32,256]{2,1,0:T(8,128)}), f32[8,32,256]{2,1,0:T(8,128)S(1)}, u32[]{:S(2)}, u32[]{:S(2)}) async-start(f32[8,32,256]{2,1,0:T(8,128)} %convolution_add_fusion), calls=%async_computation.1 | async-start | bytes 524288 | tf_op jit(solution)/shard_map/all_to_all | solution.py:170
  66.8 3.5 %collective-permute-start.5 = (f32[16,256]{1,0:T(8,128)S(1)}, f32[16,256]{1,0:T(8,128)S(1)}, u32[]{:S(2)}, u32[]{:S(2)}) collective-permute-start(f32[16,256]{1,0:T(8,128)S(1)} %get-tuple-element.13), channel_id=1, source_target_pairs={{0,32},{32,0},{1,33},{33,1},{2,34},{34,2},{3,35},{35,3},{4,36},{36... | collective-permute-start | bytes 49160 | tf_op jit(solution)/shard_map/ppermute | solution.py:119
  70.3 0.8 collective-permute-done.5
  71.1 13.3 %all-to-all-done.1 = f32[8,32,256]{2,1,0:T(8,128)S(1)} async-done(((f32[8,32,256]{2,1,0:T(8,128)}), f32[8,32,256]{2,1,0:T(8,128)S(1)}, u32[]{:S(2)}, u32[]{:S(2)}) %all-to-all-start.1) | async-done | bytes 262176 | tf_op jit(solution)/shard_map/all_to_all | solution.py:170
  84.5 0.4 fusion.2
  84.8 15.2 %all_to_all.25 = f32[32,8,128]{2,1,0:T(8,128)S(1)} all-to-all(f32[32,8,128]{2,1,0:T(8,128)S(1)} %bitcast.51), channel_id=1, replica_groups=mesh['yh'=2,'x'=4,'c'=2,'yl'=2,'zh'=8,'zl'=2] {'yh','x','yl','zl'}, dimensions={0} | all-to-all | bytes 262144 | tf_op jit(solution)/shard_map/all_to_all | solution.py:188
  100.1 15.3 %all_to_all.26 = f32[8,8,128]{2,1,0:T(8,128)S(1)} all-to-all(f32[8,8,128]{2,1,0:T(8,128)S(1)} %broadcast_in_dim.36), channel_id=1, replica_groups=mesh['yh'=2,'x'=4,'c'=2,'yl'=2,'zh'=8,'zl'=2] {'zh'}, dimensions={0} | all-to-all | bytes 65536 | tf_op jit(solution)/shard_map/all_to_all | solution.py:88
  115.4 0.7 broadcast_in_dim.37
  116.1 7.6 %all-to-all-start.4 = ((f32[64,8,128]{2,1,0:T(8,128)}), f32[64,8,128]{2,1,0:T(8,128)S(1)}, u32[]{:S(2)}, u32[]{:S(2)}) async-start(f32[64,8,128]{2,1,0:T(8,128)} %broadcast_in_dim.37), calls=%async_computation.4 | async-start | bytes 524288 | tf_op jit(solution)/shard_map/all_to_all | solution.py:88
  123.7 2.3 %collective-permute-start.4 = (f32[16,256]{1,0:T(8,128)S(1)}, f32[16,256]{1,0:T(8,128)S(1)}, u32[]{:S(2)}, u32[]{:S(2)}) collective-permute-start(f32[16,256]{1,0:T(8,128)S(1)} %get-tuple-element.15), channel_id=1, source_target_pairs={{0,32},{32,0},{1,33},{33,1},{2,34},{34,2},{3,35},{35,3},{4,36},{36... | collective-permute-start | bytes 49160 | tf_op jit(solution)/shard_map/ppermute | solution.py:173
  125.9 0.8 collective-permute-done.4
  126.8 0.6 fusion.6
  127.4 5.7 %all-to-all-done.4 = f32[64,8,128]{2,1,0:T(8,128)S(1)} async-done(((f32[64,8,128]{2,1,0:T(8,128)}), f32[64,8,128]{2,1,0:T(8,128)S(1)}, u32[]{:S(2)}, u32[]{:S(2)}) %all-to-all-start.4) | async-done | bytes 262176 | tf_op jit(solution)/shard_map/all_to_all | solution.py:88
  133.1 0.7 copy.47
  (20 shorter events, 0.3 us)
Async XLA Ops:
  0.6 45.5 %copy-start = (f32[4,128,128]{2,1,0:T(8,128)S(1)}, f32[4,128,128]{2,1,0:T(8,128)}, u32[]{:S(2)}) copy-start(f32[4,128,128]{2,1,0:T(8,128)} %param.11) | copy-start | bytes 786436
  1.8 16.1 %collective-permute-start = (f32[256,256]{1,0:T(8,128)S(1)}, f32[256,256]{1,0:T(8,128)S(1)}, u32[]{:S(2)}, u32[]{:S(2)}) collective-permute-start(f32[256,256]{1,0:T(8,128)S(1)} %get-tuple-element.11), channel_id=1, source_target_pairs={{0,16},{16,0},{1,17},{17,1},{2,18},{18,2},{3,19},{19,3},{4,20},{20... | collective-permute-start | bytes 786440 | tf_op jit(solution)/shard_map/ppermute | solution.py:125
  5.8 1.1 copy-start.1
  5.8 0.7 copy-start.2
  5.9 0.7 copy-start.3
  6.9 14.9 %collective-permute-start.2 = (f32[16,512]{1,0:T(8,128)S(1)}, f32[16,512]{1,0:T(8,128)S(1)}, u32[]{:S(2)}, u32[]{:S(2)}) collective-permute-start(f32[16,512]{1,0:T(8,128)S(1)} %broadcast_multiply_fusion.1), channel_id=1, source_target_pairs={{0,384},{1,416},{2,400},{3,432},{4,144},{5,176},{6,192},{7,96},{8,... | collective-permute-start | bytes 98312 | tf_op jit(solution)/shard_map/ppermute | solution.py:114
  18.0 18.6 %collective-permute-start.1 = (f32[256,512]{1,0:T(8,128)S(1)}, f32[256,512]{1,0:T(8,128)S(1)}, u32[]{:S(2)}, u32[]{:S(2)}) collective-permute-start(f32[256,512]{1,0:T(8,128)S(1)} %maximum_select_fusion.1), channel_id=1, source_target_pairs={{0,32},{32,0},{1,33},{33,1},{2,34},{34,2},{3,35},{35,3},{4,36},{36... | collective-permute-start | bytes 1572872 | tf_op jit(solution)/shard_map/ppermute | solution.py:131
  22.7 20.9 %all-to-all-start = ((f32[32,16,256]{2,1,0:T(8,128)}), f32[32,16,256]{2,1,0:T(8,128)S(1)}, u32[]{:S(2)}, u32[]{:S(2)}) async-start(f32[32,16,256]{2,1,0:T(8,128)} %bitcast.6), calls=%async_computation | async-start | bytes 1048576 | tf_op jit(solution)/shard_map/all_to_all | solution.py:152
  44.2 9.4 %collective-permute-start.3 = (f32[8,32,256]{2,1,0:T(8,128)S(1)}, f32[8,32,256]{2,1,0:T(8,128)S(1)}, u32[]{:S(2)}, u32[]{:S(2)}) collective-permute-start(f32[8,32,256]{2,1,0:T(8,128)S(1)} %fusion.15), channel_id=1, source_target_pairs={{0,1},{1,0},{2,3},{3,2},{4,5},{5,4},{6,7},{7,6},{8,9},{9,8},{10,11... | collective-permute-start | bytes 786440 | tf_op jit(solution)/shard_map/ppermute | solution.py:163
  54.8 29.6 %all-to-all-start.1 = ((f32[8,32,256]{2,1,0:T(8,128)}), f32[8,32,256]{2,1,0:T(8,128)S(1)}, u32[]{:S(2)}, u32[]{:S(2)}) async-start(f32[8,32,256]{2,1,0:T(8,128)} %convolution_add_fusion), calls=%async_computation.1 | async-start | bytes 524288 | tf_op jit(solution)/shard_map/all_to_all | solution.py:170
  66.8 4.4 %collective-permute-start.5 = (f32[16,256]{1,0:T(8,128)S(1)}, f32[16,256]{1,0:T(8,128)S(1)}, u32[]{:S(2)}, u32[]{:S(2)}) collective-permute-start(f32[16,256]{1,0:T(8,128)S(1)} %get-tuple-element.13), channel_id=1, source_target_pairs={{0,32},{32,0},{1,33},{33,1},{2,34},{34,2},{3,35},{35,3},{4,36},{36... | collective-permute-start | bytes 49160 | tf_op jit(solution)/shard_map/ppermute | solution.py:119
  116.1 17.0 %all-to-all-start.4 = ((f32[64,8,128]{2,1,0:T(8,128)}), f32[64,8,128]{2,1,0:T(8,128)S(1)}, u32[]{:S(2)}, u32[]{:S(2)}) async-start(f32[64,8,128]{2,1,0:T(8,128)} %broadcast_in_dim.37), calls=%async_computation.4 | async-start | bytes 524288 | tf_op jit(solution)/shard_map/all_to_all | solution.py:88
  123.7 3.1 %collective-permute-start.4 = (f32[16,256]{1,0:T(8,128)S(1)}, f32[16,256]{1,0:T(8,128)S(1)}, u32[]{:S(2)}, u32[]{:S(2)}) collective-permute-start(f32[16,256]{1,0:T(8,128)S(1)} %get-tuple-element.15), channel_id=1, source_target_pairs={{0,32},{32,0},{1,33},{33,1},{2,34},{34,2},{3,35},{35,3},{4,36},{36... | collective-permute-start | bytes 49160 | tf_op jit(solution)/shard_map/ppermute | solution.py:173

commit v8 on v7

--- a/solution.py
+++ b/solution.py
@@ -111,7 +111,9 @@
 
     chunks = col_span // row_count
     pairs, groups = routes(chunks)
-    moved = lax.ppermute(active_own, ALL, pairs)
+    moved = lax.ppermute(panels, ALL, pairs)
+
+    moved, active_own = lax.optimization_barrier((moved, active_own))
 
     by_core = active_own.reshape(row_count, 2, half).transpose(1, 0, 2)
     mine = jnp.where(core == 0, by_core[0], by_core[1])
@@ -146,7 +148,12 @@
     leave = jnp.where(odd == 0, pieces[:, 1], pieces[:, 0]).reshape(-1, 2 * col_span)
     stay = jnp.where(odd == 0, pieces[:, 0], pieces[:, 1]).reshape(-1, 2 * col_span)
 
-    halves = moved.reshape(row_count, CS, half).transpose(1, 0, 2)
+    blocks_at = [0] * len(pairs)
+    for source, target in pairs:
+        blocks_at[target] = source // chunks
+    held = jnp.asarray(blocks_at, jnp.int32)[prow_index * cols + pcol_index]
+    held_keep = jnp.repeat(lax.dynamic_slice_in_dim(active_blocks, held, 1, 0), W, axis=1)
+    halves = (moved * held_keep).reshape(row_count, CS, half).transpose(1, 0, 2)
     outgoing = jnp.broadcast_to(halves[None], (chunks * YL // CS, CS, row_count, half))
     outgoing = outgoing.reshape(chunks * YL, row_count, half)
     needed = lax.all_to_all(
@@ -161,7 +168,9 @@
 
     leaving = product(leave)
     arrived = lax.ppermute(leaving, "zl", SWAP)
-    pair_sum = product(stay) + arrived
+    staying = product(stay)
+    staying, arrived = lax.optimization_barrier((staying, arrived))
+    pair_sum = staying + arrived
     part = S // 2 * W // lax.axis_size(SIDE)
     own_diag = lax.dynamic_slice_in_dim(
         diag_inverse.reshape(S * W, W), lax.axis_index(BACK) * part, part, 0

time: 135 us -> 133 us (0.985)
  starting transfers between devices: 56.6 us -> 54.1 us
  waiting for transfers between devices: 36.6 us -> 34.2 us
  between operations: 0.96 us -> 2.88 us
    all_to_all x1, starting transfers between devices: 11.9 us -> 7.54 us  [body(): parts = lax.all_to_all(pair_sum, 'zh', 0, 0, tiled=True)]
    all_to_all x1, starting transfers between devices: 13.7 us -> 15.5 us  [body(): lax.all_to_all(outgoing, ALL, 0, 0, tiled=True, axis_index_groups=groups)]
    ppermute x1, waiting for transfers between devices: 1.8 us -> 0.01 us  [body(): moved = lax.ppermute(panels, ALL, pairs)]
  transfers between devices with their start and end apart: 9 -> 9, of which waited for: 7 -> 6; matrix products, arithmetic and copies ran while one was open for 3% -> 4% of each run, Pallas kernels for 0% -> 0%
where the time goes in v8:
time: 133 us; the launch traced here: 132 us
  starting transfers between devices  54.1 us (41%)
  waiting for transfers between devices  34.2 us (26%)
  blocking collectives  30.4 us (23%)
  local copies, waits for them, and re-layouts  5.8 us (4%)
  other arithmetic  3.21 us (2%)
  between operations  2.88 us (2%)
  matrix products  1.57 us (1%)
    all_to_all x1, starting transfers between devices, body(): lax.all_to_all(outgoing, ALL, 0, 0, tiled=True, axis_index_groups=groups)  15.5 us
    all_to_all x1, blocking collectives, spread(): return lax.all_to_all(copies, axis, 0, 0, tiled=True)  15.3 us
    all_to_all x1, blocking collectives, body(): lax.all_to_all(local_diag.reshape(peers, part, W), SIDE, 0, 0, tiled=True)  15.2 us
    all_to_all x1, waiting for transfers between devices, body(): parts = lax.all_to_all(pair_sum, 'zh', 0, 0, tiled=True)  13.3 us
    ppermute x1, starting transfers between devices, body(): moved = lax.ppermute(panels, ALL, pairs)  9.82 us
    all_to_all x1, starting transfers between devices, spread(): return lax.all_to_all(copies, axis, 0, 0, tiled=True)  7.56 us
    all_to_all x1, starting transfers between devices, body(): parts = lax.all_to_all(pair_sum, 'zh', 0, 0, tiled=True)  7.54 us
    all_to_all x1, waiting for transfers between devices, body(): lax.all_to_all(outgoing, ALL, 0, 0, tiled=True, axis_index_groups=groups)  6.77 us
  transfers between devices with their start and end apart: 9, of which 6 were waited for; matrix products, arithmetic and copies ran while one was open for 4% of the time, Pallas kernels for 0%

profile of v8, /device:TPU:1, one launch (start us, length us, event | category | flops | bytes accessed | tf_op | source)
XLA Modules:
  0.0 132.2 jit_solution(8013903572487121301)
XLA Ops:
  0.6 0.0 copy-start
  0.7 0.0 copy-start.1
  0.7 1.1 slice_select_fusion.1
  1.8 4.0 %collective-permute-start = (f32[256,256]{1,0:T(8,128)S(1)}, f32[256,256]{1,0:T(8,128)S(1)}, u32[]{:S(2)}, u32[]{:S(2)}) collective-permute-start(f32[256,256]{1,0:T(8,128)S(1)} %get-tuple-element.21), channel_id=1, source_target_pairs={{0,16},{16,0},{1,17},{17,1},{2,18},{18,2},{3,19},{19,3},{4,20},{20... | collective-permute-start | bytes 786440 | tf_op jit(solution)/shard_map/ppermute | solution.py:127
  5.8 0.0 copy-done.1
  5.8 9.8 %collective-permute-start.2 = (f32[16,512]{1,0:T(8,128)S(1)}, f32[16,512]{1,0:T(8,128)S(1)}, u32[]{:S(2)}, u32[]{:S(2)}) collective-permute-start(f32[16,512]{1,0:T(8,128)S(1)} %copy-done.1), channel_id=1, source_target_pairs={{0,384},{1,416},{2,400},{3,432},{4,144},{5,176},{6,192},{7,96},{8,... | collective-permute-start | bytes 98312 | tf_op jit(solution)/shard_map/ppermute | solution.py:114
  15.7 1.3 dynamic_slice.34
  18.3 0.8 fusion.12
  19.0 0.1 reshape.146
  19.1 0.1 reshape.147
  19.2 0.2 fusion.9
  19.4 0.1 broadcast_bitcast_fusion.2
  19.5 0.0 copy-start.2
  19.5 0.0 copy-start.3
  19.5 0.1 broadcast_bitcast_fusion.3
  19.6 0.6 copy-done.2
  20.2 0.0 copy-done.3
  20.2 0.1 compare_reduce_fusion
  21.0 0.2 dynamic-slice_reduce_fusion
  21.2 0.1 broadcast_bitcast_fusion.1
  21.3 0.0 collective-permute-done
  21.3 1.9 %collective-permute-start.1 = (f32[256,512]{1,0:T(8,128)S(1)}, f32[256,512]{1,0:T(8,128)S(1)}, u32[]{:S(2)}, u32[]{:S(2)}) collective-permute-start(f32[256,512]{1,0:T(8,128)S(1)} %maximum_select_fusion.1), channel_id=1, source_target_pairs={{0,32},{32,0},{1,33},{33,1},{2,34},{34,2},{3,35},{35,3},{4,36},{36... | collective-permute-start | bytes 1572872 | tf_op jit(solution)/shard_map/ppermute | solution.py:133
  23.2 0.1 broadcast_bitcast_fusion
  23.3 0.0 collective-permute-done.2
  23.4 0.8 broadcast_in_dim.42
  24.2 15.5 %all-to-all-start = ((f32[32,16,256]{2,1,0:T(8,128)}), f32[32,16,256]{2,1,0:T(8,128)S(1)}, u32[]{:S(2)}, u32[]{:S(2)}) async-start(f32[32,16,256]{2,1,0:T(8,128)} %bitcast.8), calls=%async_computation | async-start | bytes 1048576 | tf_op jit(solution)/shard_map/all_to_all | solution.py:159
  39.7 0.1 fusion.1
  39.8 0.0 collective-permute-done.1
  39.8 0.1 broadcast_multiply_fusion
  39.9 0.1 broadcast_select_fusion
  40.1 6.8 %all-to-all-done = f32[32,16,256]{2,1,0:T(8,128)S(1)} async-done(((f32[32,16,256]{2,1,0:T(8,128)}), f32[32,16,256]{2,1,0:T(8,128)S(1)}, u32[]{:S(2)}, u32[]{:S(2)}) %all-to-all-start) | async-done | bytes 524320 | tf_op jit(solution)/shard_map/all_to_all | solution.py:159
  46.9 0.6 fusion.16
  47.5 1.9 %collective-permute-start.3 = (f32[8,32,256]{2,1,0:T(8,128)S(1)}, f32[8,32,256]{2,1,0:T(8,128)S(1)}, u32[]{:S(2)}, u32[]{:S(2)}) collective-permute-start(f32[8,32,256]{2,1,0:T(8,128)S(1)} %fusion.16), channel_id=1, source_target_pairs={{0,1},{1,0},{2,3},{3,2},{4,5},{5,4},{6,7},{7,6},{8,9},{9,8},{10,11... | collective-permute-start | bytes 786440 | tf_op jit(solution)/shard_map/ppermute | solution.py:170
  49.4 0.0 copy-done
  49.5 0.6 fusion.15
  50.1 6.8 %collective-permute-done.3 = f32[8,32,256]{2,1,0:T(8,128)S(1)} collective-permute-done((f32[8,32,256]{2,1,0:T(8,128)S(1)}, f32[8,32,256]{2,1,0:T(8,128)S(1)}, u32[]{:S(2)}, u32[]{:S(2)}) %collective-permute-start.3) | collective-permute-done | bytes 262176 | tf_op jit(solution)/shard_map/ppermute | solution.py:170
  56.8 0.7 add.78
  57.6 7.5 %all-to-all-start.1 = ((f32[8,32,256]{2,1,0:T(8,128)}), f32[8,32,256]{2,1,0:T(8,128)S(1)}, u32[]{:S(2)}, u32[]{:S(2)}) async-start(f32[8,32,256]{2,1,0:T(8,128)} %add.78), calls=%async_computation.1 | async-start | bytes 524288 | tf_op jit(solution)/shard_map/all_to_all | solution.py:179
  65.1 3.5 %collective-permute-start.5 = (f32[16,256]{1,0:T(8,128)S(1)}, f32[16,256]{1,0:T(8,128)S(1)}, u32[]{:S(2)}, u32[]{:S(2)}) collective-permute-start(f32[16,256]{1,0:T(8,128)S(1)} %get-tuple-element.23), channel_id=1, source_target_pairs={{0,32},{32,0},{1,33},{33,1},{2,34},{34,2},{3,35},{35,3},{4,36},{36... | collective-permute-start | bytes 49160 | tf_op jit(solution)/shard_map/ppermute | solution.py:121
  68.7 0.8 collective-permute-done.5
  69.5 13.3 %all-to-all-done.1 = f32[8,32,256]{2,1,0:T(8,128)S(1)} async-done(((f32[8,32,256]{2,1,0:T(8,128)}), f32[8,32,256]{2,1,0:T(8,128)S(1)}, u32[]{:S(2)}, u32[]{:S(2)}) %all-to-all-start.1) | async-done | bytes 262176 | tf_op jit(solution)/shard_map/all_to_all | solution.py:179
  82.8 0.4 fusion.2
  83.2 15.2 %all_to_all.25 = f32[32,8,128]{2,1,0:T(8,128)S(1)} all-to-all(f32[32,8,128]{2,1,0:T(8,128)S(1)} %bitcast.54), channel_id=1, replica_groups=mesh['yh'=2,'x'=4,'c'=2,'yl'=2,'zh'=8,'zl'=2] {'yh','x','yl','zl'}, dimensions={0} | all-to-all | bytes 262144 | tf_op jit(solution)/shard_map/all_to_all | solution.py:197
  98.4 15.3 %all_to_all.26 = f32[8,8,128]{2,1,0:T(8,128)S(1)} all-to-all(f32[8,8,128]{2,1,0:T(8,128)S(1)} %broadcast_in_dim.43), channel_id=1, replica_groups=mesh['yh'=2,'x'=4,'c'=2,'yl'=2,'zh'=8,'zl'=2] {'zh'}, dimensions={0} | all-to-all | bytes 65536 | tf_op jit(solution)/shard_map/all_to_all | solution.py:88
  113.7 0.7 broadcast_in_dim.44
  114.5 7.6 %all-to-all-start.4 = ((f32[64,8,128]{2,1,0:T(8,128)}), f32[64,8,128]{2,1,0:T(8,128)S(1)}, u32[]{:S(2)}, u32[]{:S(2)}) async-start(f32[64,8,128]{2,1,0:T(8,128)} %broadcast_in_dim.44), calls=%async_computation.4 | async-start | bytes 524288 | tf_op jit(solution)/shard_map/all_to_all | solution.py:88
  122.0 2.3 %collective-permute-start.4 = (f32[16,256]{1,0:T(8,128)S(1)}, f32[16,256]{1,0:T(8,128)S(1)}, u32[]{:S(2)}, u32[]{:S(2)}) collective-permute-start(f32[16,256]{1,0:T(8,128)S(1)} %get-tuple-element.25), channel_id=1, source_target_pairs={{0,32},{32,0},{1,33},{33,1},{2,34},{34,2},{3,35},{35,3},{4,36},{36... | collective-permute-start | bytes 49160 | tf_op jit(solution)/shard_map/ppermute | solution.py:182
  124.3 0.8 collective-permute-done.4
  125.1 0.6 fusion.6
  125.7 5.7 %all-to-all-done.4 = f32[64,8,128]{2,1,0:T(8,128)S(1)} async-done(((f32[64,8,128]{2,1,0:T(8,128)}), f32[64,8,128]{2,1,0:T(8,128)S(1)}, u32[]{:S(2)}, u32[]{:S(2)}) %all-to-all-start.4) | async-done | bytes 262176 | tf_op jit(solution)/shard_map/all_to_all | solution.py:88
  131.5 0.7 copy.48
  (21 shorter events, 0.3 us)
Async XLA Ops:
  0.6 48.8 %copy-start = (f32[4,128,128]{2,1,0:T(8,128)S(1)}, f32[4,128,128]{2,1,0:T(8,128)}, u32[]{:S(2)}) copy-start(f32[4,128,128]{2,1,0:T(8,128)} %param.12) | copy-start | bytes 786436
  0.7 5.2 %copy-start.1 = (f32[16,512]{1,0:T(8,128)S(1)}, f32[16,512]{1,0:T(8,128)}, u32[]{:S(2)}) copy-start(f32[16,512]{1,0:T(8,128)} %param.11) | copy-start | bytes 98308
  1.8 19.5 %collective-permute-start = (f32[256,256]{1,0:T(8,128)S(1)}, f32[256,256]{1,0:T(8,128)S(1)}, u32[]{:S(2)}, u32[]{:S(2)}) collective-permute-start(f32[256,256]{1,0:T(8,128)S(1)} %get-tuple-element.21), channel_id=1, source_target_pairs={{0,16},{16,0},{1,17},{17,1},{2,18},{18,2},{3,19},{19,3},{4,20},{20... | collective-permute-start | bytes 786440 | tf_op jit(solution)/shard_map/ppermute | solution.py:127
  5.8 17.5 %collective-permute-start.2 = (f32[16,512]{1,0:T(8,128)S(1)}, f32[16,512]{1,0:T(8,128)S(1)}, u32[]{:S(2)}, u32[]{:S(2)}) collective-permute-start(f32[16,512]{1,0:T(8,128)S(1)} %copy-done.1), channel_id=1, source_target_pairs={{0,384},{1,416},{2,400},{3,432},{4,144},{5,176},{6,192},{7,96},{8,... | collective-permute-start | bytes 98312 | tf_op jit(solution)/shard_map/ppermute | solution.py:114
  19.5 0.7 copy-start.2
  19.5 0.7 copy-start.3
  21.3 18.5 %collective-permute-start.1 = (f32[256,512]{1,0:T(8,128)S(1)}, f32[256,512]{1,0:T(8,128)S(1)}, u32[]{:S(2)}, u32[]{:S(2)}) collective-permute-start(f32[256,512]{1,0:T(8,128)S(1)} %maximum_select_fusion.1), channel_id=1, source_target_pairs={{0,32},{32,0},{1,33},{33,1},{2,34},{34,2},{3,35},{35,3},{4,36},{36... | collective-permute-start | bytes 1572872 | tf_op jit(solution)/shard_map/ppermute | solution.py:133
  24.2 22.6 %all-to-all-start = ((f32[32,16,256]{2,1,0:T(8,128)}), f32[32,16,256]{2,1,0:T(8,128)S(1)}, u32[]{:S(2)}, u32[]{:S(2)}) async-start(f32[32,16,256]{2,1,0:T(8,128)} %bitcast.8), calls=%async_computation | async-start | bytes 1048576 | tf_op jit(solution)/shard_map/all_to_all | solution.py:159
  47.5 9.4 %collective-permute-start.3 = (f32[8,32,256]{2,1,0:T(8,128)S(1)}, f32[8,32,256]{2,1,0:T(8,128)S(1)}, u32[]{:S(2)}, u32[]{:S(2)}) collective-permute-start(f32[8,32,256]{2,1,0:T(8,128)S(1)} %fusion.16), channel_id=1, source_target_pairs={{0,1},{1,0},{2,3},{3,2},{4,5},{5,4},{6,7},{7,6},{8,9},{9,8},{10,11... | collective-permute-start | bytes 786440 | tf_op jit(solution)/shard_map/ppermute | solution.py:170
  57.6 25.2 %all-to-all-start.1 = ((f32[8,32,256]{2,1,0:T(8,128)}), f32[8,32,256]{2,1,0:T(8,128)S(1)}, u32[]{:S(2)}, u32[]{:S(2)}) async-start(f32[8,32,256]{2,1,0:T(8,128)} %add.78), calls=%async_computation.1 | async-start | bytes 524288 | tf_op jit(solution)/shard_map/all_to_all | solution.py:179
  65.1 4.4 %collective-permute-start.5 = (f32[16,256]{1,0:T(8,128)S(1)}, f32[16,256]{1,0:T(8,128)S(1)}, u32[]{:S(2)}, u32[]{:S(2)}) collective-permute-start(f32[16,256]{1,0:T(8,128)S(1)} %get-tuple-element.23), channel_id=1, source_target_pairs={{0,32},{32,0},{1,33},{33,1},{2,34},{34,2},{3,35},{35,3},{4,36},{36... | collective-permute-start | bytes 49160 | tf_op jit(solution)/shard_map/ppermute | solution.py:121
  114.5 17.0 %all-to-all-start.4 = ((f32[64,8,128]{2,1,0:T(8,128)}), f32[64,8,128]{2,1,0:T(8,128)S(1)}, u32[]{:S(2)}, u32[]{:S(2)}) async-start(f32[64,8,128]{2,1,0:T(8,128)} %broadcast_in_dim.44), calls=%async_computation.4 | async-start | bytes 524288 | tf_op jit(solution)/shard_map/all_to_all | solution.py:88
  122.0 3.1 %collective-permute-start.4 = (f32[16,256]{1,0:T(8,128)S(1)}, f32[16,256]{1,0:T(8,128)S(1)}, u32[]{:S(2)}, u32[]{:S(2)}) collective-permute-start(f32[16,256]{1,0:T(8,128)S(1)} %get-tuple-element.25), channel_id=1, source_target_pairs={{0,32},{32,0},{1,33},{33,1},{2,34},{34,2},{3,35},{35,3},{4,36},{36... | collective-permute-start | bytes 49160 | tf_op jit(solution)/shard_map/ppermute | solution.py:182

commit v9 on v7

--- a/solution.py
+++ b/solution.py
@@ -111,12 +111,8 @@
 
     chunks = col_span // row_count
     pairs, groups = routes(chunks)
-    moved = lax.ppermute(active_own, ALL, pairs)
-
-    by_core = active_own.reshape(row_count, 2, half).transpose(1, 0, 2)
-    mine = jnp.where(core == 0, by_core[0], by_core[1])
-    theirs = jnp.where(core == 0, by_core[1], by_core[0])
-    active_pair = jnp.stack([mine, lax.ppermute(theirs, "c", SWAP)])
+
+    moved = lax.ppermute(panels, ALL, pairs)
 
     block_rows = row_span // BLK
     blocks = ancestor_inverse.reshape(block_rows, BLK, col_span)
@@ -153,6 +149,19 @@
         outgoing, ALL, 0, 0, tiled=True, axis_index_groups=groups
     ).reshape(2 * col_span, half)
 
+    needed, active_own = lax.optimization_barrier((needed, active_own))
+    by_core = active_own.reshape(row_count, 2, half).transpose(1, 0, 2)
+    mine = jnp.where(core == 0, by_core[0], by_core[1])
+    theirs = jnp.where(core == 0, by_core[1], by_core[0])
+    active_pair = jnp.stack([mine, lax.ppermute(theirs, "c", SWAP)])
+
+    here = lax.axis_index(DEPTH)
+    keep_here = lax.dynamic_slice(
+        active_blocks.reshape(YL, deep, S), (0, here, core * (S // CS)), (YL, 1, S // CS)
+    )
+    keep_here = jnp.repeat(keep_here, W, axis=2)
+    needed = (needed.reshape(YL, col_span, half) * keep_here).reshape(-1, half)
+
     def product(rows):
         value = jnp.dot(
             rows, needed, precision=lax.Precision.HIGHEST, preferred_element_type=jnp.float32
@@ -161,7 +170,9 @@
 
     leaving = product(leave)
     arrived = lax.ppermute(leaving, "zl", SWAP)
-    pair_sum = product(stay) + arrived
+    staying = product(stay)
+    staying, arrived = lax.optimization_barrier((staying, arrived))
+    pair_sum = staying + arrived
     part = S // 2 * W // lax.axis_size(SIDE)
     own_diag = lax.dynamic_slice_in_dim(
         diag_inverse.reshape(S * W, W), lax.axis_index(BACK) * part, part, 0

time: 135 us -> 133 us (0.985)
  waiting for transfers between devices: 36.6 us -> 34.7 us
    all_to_all x1, waiting for transfers between devices: 6.77 us -> 4.68 us  [body(): lax.all_to_all(outgoing, ALL, 0, 0, tiled=True, axis_index_groups=groups)]
where the time goes in v9:
time: 133 us
  starting transfers between devices  56.9 us (43%)
  waiting for transfers between devices  34.7 us (26%)
  blocking collectives  30.5 us (23%)
  local copies, waits for them, and re-layouts  4.74 us (4%)
  other arithmetic  3.23 us (2%)
  matrix products  1.57 us (1%)
    all_to_all x1, blocking collectives, spread(): return lax.all_to_all(copies, axis, 0, 0, tiled=True)  15.3 us
    all_to_all x1, blocking collectives, body(): lax.all_to_all(local_diag.reshape(peers, part, W), SIDE, 0, 0, tiled=True)  15.2 us
    all_to_all x1, waiting for transfers between devices, body(): parts = lax.all_to_all(pair_sum, 'zh', 0, 0, tiled=True)  13.3 us
    all_to_all x1, starting transfers between devices, body(): lax.all_to_all(outgoing, ALL, 0, 0, tiled=True, axis_index_groups=groups)  13 us
    all_to_all x1, starting transfers between devices, body(): parts = lax.all_to_all(pair_sum, 'zh', 0, 0, tiled=True)  12.6 us
    ppermute x1, starting transfers between devices, body(): moved = lax.ppermute(panels, ALL, pairs)  9.82 us
    all_to_all x1, starting transfers between devices, spread(): return lax.all_to_all(copies, axis, 0, 0, tiled=True)  7.56 us
    ppermute x1, waiting for transfers between devices, body(): arrived = lax.ppermute(leaving, 'zl', SWAP)  6.75 us
  transfers between devices with their start and end apart: 9, of which 7 were waited for; matrix products, arithmetic and copies ran while one was open for 3% of the time, Pallas kernels for 0%

profile of v9, /device:TPU:1, one launch (start us, length us, event | category | flops | bytes accessed | tf_op | source)
XLA Modules:
  0.0 132.5 jit_solution(9622558695591003439)
XLA Ops:
  0.6 0.0 copy-start
  0.7 0.0 copy-start.1
  0.7 1.1 slice_select_fusion.1
  1.8 4.0 %collective-permute-start = (f32[256,256]{1,0:T(8,128)S(1)}, f32[256,256]{1,0:T(8,128)S(1)}, u32[]{:S(2)}, u32[]{:S(2)}) collective-permute-start(f32[256,256]{1,0:T(8,128)S(1)} %get-tuple-element.19), channel_id=1, source_target_pairs={{0,16},{16,0},{1,17},{17,1},{2,18},{18,2},{3,19},{19,3},{4,20},{20... | collective-permute-start | bytes 786440 | tf_op jit(solution)/shard_map/ppermute | solution.py:121
  5.8 0.0 copy-done.1
  5.8 9.8 %collective-permute-start.2 = (f32[16,512]{1,0:T(8,128)S(1)}, f32[16,512]{1,0:T(8,128)S(1)}, u32[]{:S(2)}, u32[]{:S(2)}) collective-permute-start(f32[16,512]{1,0:T(8,128)S(1)} %copy-done.1), channel_id=1, source_target_pairs={{0,384},{1,416},{2,400},{3,432},{4,144},{5,176},{6,192},{7,96},{8,... | collective-permute-start | bytes 98312 | tf_op jit(solution)/shard_map/ppermute | solution.py:115
  15.7 0.8 fusion.16
  16.5 0.1 reshape.155
  16.5 0.0 copy-start.2
  16.5 0.0 copy-start.3
  16.5 0.1 reshape.156
  16.6 0.6 copy-done.2
  17.2 0.0 copy-done.3
  17.2 0.1 compare_reduce_fusion
  17.3 0.1 reshape.165
  17.4 0.1 constant_dynamic-slice_fusion.1
  17.5 0.1 copy.26
  17.6 0.1 broadcast_bitcast_fusion
  17.7 0.2 fusion.13
  17.9 0.1 broadcast_bitcast_fusion.2
  18.0 0.1 broadcast_bitcast_fusion.3
  18.0 0.2 dynamic-slice_reduce_fusion
  18.2 2.5 %collective-permute-done.2 = f32[16,512]{1,0:T(8,128)S(1)} collective-permute-done((f32[16,512]{1,0:T(8,128)S(1)}, f32[16,512]{1,0:T(8,128)S(1)}, u32[]{:S(2)}, u32[]{:S(2)}) %collective-permute-start.2) | collective-permute-done | bytes 32800 | tf_op jit(solution)/shard_map/ppermute | solution.py:115
  20.8 0.8 broadcast_in_dim.40
  21.6 13.0 %all-to-all-start = ((f32[32,16,256]{2,1,0:T(8,128)}), f32[32,16,256]{2,1,0:T(8,128)S(1)}, u32[]{:S(2)}, u32[]{:S(2)}) async-start(f32[32,16,256]{2,1,0:T(8,128)} %bitcast.6), calls=%async_computation | async-start | bytes 1048576 | tf_op jit(solution)/shard_map/all_to_all | solution.py:148
  34.6 0.0 collective-permute-done
  34.7 2.2 %collective-permute-start.1 = (f32[256,512]{1,0:T(8,128)S(1)}, f32[256,512]{1,0:T(8,128)S(1)}, u32[]{:S(2)}, u32[]{:S(2)}) collective-permute-start(f32[256,512]{1,0:T(8,128)S(1)} %maximum_select_fusion.1), channel_id=1, source_target_pairs={{0,32},{32,0},{1,33},{33,1},{2,34},{34,2},{3,35},{35,3},{4,36},{36... | collective-permute-start | bytes 1572872 | tf_op jit(solution)/shard_map/ppermute | solution.py:127
  36.9 0.1 broadcast_bitcast_fusion.1
  37.0 0.1 fusion.1
  37.1 4.7 %all-to-all-done = f32[32,16,256]{2,1,0:T(8,128)S(1)} async-done(((f32[32,16,256]{2,1,0:T(8,128)}), f32[32,16,256]{2,1,0:T(8,128)S(1)}, u32[]{:S(2)}, u32[]{:S(2)}) %all-to-all-start) | async-done | bytes 524320 | tf_op jit(solution)/shard_map/all_to_all | solution.py:148
  41.8 0.0 collective-permute-done.1
  41.8 0.1 broadcast_multiply_fusion
  41.9 0.1 broadcast_select_fusion
  42.1 0.6 fusion.2
  42.7 1.9 %collective-permute-start.3 = (f32[8,32,256]{2,1,0:T(8,128)S(1)}, f32[8,32,256]{2,1,0:T(8,128)S(1)}, u32[]{:S(2)}, u32[]{:S(2)}) collective-permute-start(f32[8,32,256]{2,1,0:T(8,128)S(1)} %fusion.2), channel_id=1, source_target_pairs={{0,1},{1,0},{2,3},{3,2},{4,5},{5,4},{6,7},{7,6},{8,9},{9,8},{10,11... | collective-permute-start | bytes 786440 | tf_op jit(solution)/shard_map/ppermute | solution.py:172
  44.6 0.0 copy-done
  44.7 0.6 fusion.4
  45.3 6.8 %collective-permute-done.3 = f32[8,32,256]{2,1,0:T(8,128)S(1)} collective-permute-done((f32[8,32,256]{2,1,0:T(8,128)S(1)}, f32[8,32,256]{2,1,0:T(8,128)S(1)}, u32[]{:S(2)}, u32[]{:S(2)}) %collective-permute-start.3) | collective-permute-done | bytes 262176 | tf_op jit(solution)/shard_map/ppermute | solution.py:172
  52.0 0.7 add.75
  52.8 12.6 %all-to-all-start.1 = ((f32[8,32,256]{2,1,0:T(8,128)}), f32[8,32,256]{2,1,0:T(8,128)S(1)}, u32[]{:S(2)}, u32[]{:S(2)}) async-start(f32[8,32,256]{2,1,0:T(8,128)} %add.75), calls=%async_computation.1 | async-start | bytes 524288 | tf_op jit(solution)/shard_map/all_to_all | solution.py:181
  65.4 3.5 %collective-permute-start.5 = (f32[16,256]{1,0:T(8,128)S(1)}, f32[16,256]{1,0:T(8,128)S(1)}, u32[]{:S(2)}, u32[]{:S(2)}) collective-permute-start(f32[16,256]{1,0:T(8,128)S(1)} %get-tuple-element.21), channel_id=1, source_target_pairs={{0,32},{32,0},{1,33},{33,1},{2,34},{34,2},{3,35},{35,3},{4,36},{36... | collective-permute-start | bytes 49160 | tf_op jit(solution)/shard_map/ppermute | solution.py:156
  69.0 0.8 collective-permute-done.5
  69.8 13.3 %all-to-all-done.1 = f32[8,32,256]{2,1,0:T(8,128)S(1)} async-done(((f32[8,32,256]{2,1,0:T(8,128)}), f32[8,32,256]{2,1,0:T(8,128)S(1)}, u32[]{:S(2)}, u32[]{:S(2)}) %all-to-all-start.1) | async-done | bytes 262176 | tf_op jit(solution)/shard_map/all_to_all | solution.py:181
  83.1 0.4 fusion.6
  83.5 15.2 %all_to_all.25 = f32[32,8,128]{2,1,0:T(8,128)S(1)} all-to-all(f32[32,8,128]{2,1,0:T(8,128)S(1)} %bitcast.61), channel_id=1, replica_groups=mesh['yh'=2,'x'=4,'c'=2,'yl'=2,'zh'=8,'zl'=2] {'yh','x','yl','zl'}, dimensions={0} | all-to-all | bytes 262144 | tf_op jit(solution)/shard_map/all_to_all | solution.py:199
  98.7 15.3 %all_to_all.26 = f32[8,8,128]{2,1,0:T(8,128)S(1)} all-to-all(f32[8,8,128]{2,1,0:T(8,128)S(1)} %broadcast_in_dim.43), channel_id=1, replica_groups=mesh['yh'=2,'x'=4,'c'=2,'yl'=2,'zh'=8,'zl'=2] {'zh'}, dimensions={0} | all-to-all | bytes 65536 | tf_op jit(solution)/shard_map/all_to_all | solution.py:88
  114.0 0.7 broadcast_in_dim.44
  114.8 7.6 %all-to-all-start.4 = ((f32[64,8,128]{2,1,0:T(8,128)}), f32[64,8,128]{2,1,0:T(8,128)S(1)}, u32[]{:S(2)}, u32[]{:S(2)}) async-start(f32[64,8,128]{2,1,0:T(8,128)} %broadcast_in_dim.44), calls=%async_computation.4 | async-start | bytes 524288 | tf_op jit(solution)/shard_map/all_to_all | solution.py:88
  122.4 2.3 %collective-permute-start.4 = (f32[16,256]{1,0:T(8,128)S(1)}, f32[16,256]{1,0:T(8,128)S(1)}, u32[]{:S(2)}, u32[]{:S(2)}) collective-permute-start(f32[16,256]{1,0:T(8,128)S(1)} %get-tuple-element.23), channel_id=1, source_target_pairs={{0,32},{32,0},{1,33},{33,1},{2,34},{34,2},{3,35},{35,3},{4,36},{36... | collective-permute-start | bytes 49160 | tf_op jit(solution)/shard_map/ppermute | solution.py:184
  124.6 0.8 collective-permute-done.4
  125.4 0.6 fusion.10
  126.1 5.7 %all-to-all-done.4 = f32[64,8,128]{2,1,0:T(8,128)S(1)} async-done(((f32[64,8,128]{2,1,0:T(8,128)}), f32[64,8,128]{2,1,0:T(8,128)S(1)}, u32[]{:S(2)}, u32[]{:S(2)}) %all-to-all-start.4) | async-done | bytes 262176 | tf_op jit(solution)/shard_map/all_to_all | solution.py:88
  131.8 0.7 copy.47
  (22 shorter events, 0.3 us)
Async XLA Ops:
  0.6 44.0 %copy-start = (f32[4,128,128]{2,1,0:T(8,128)S(1)}, f32[4,128,128]{2,1,0:T(8,128)}, u32[]{:S(2)}) copy-start(f32[4,128,128]{2,1,0:T(8,128)} %param.11) | copy-start | bytes 786436
  0.7 5.2 %copy-start.1 = (f32[16,512]{1,0:T(8,128)S(1)}, f32[16,512]{1,0:T(8,128)}, u32[]{:S(2)}) copy-start(f32[16,512]{1,0:T(8,128)} %param.10) | copy-start | bytes 98308
  1.8 32.8 %collective-permute-start = (f32[256,256]{1,0:T(8,128)S(1)}, f32[256,256]{1,0:T(8,128)S(1)}, u32[]{:S(2)}, u32[]{:S(2)}) collective-permute-start(f32[256,256]{1,0:T(8,128)S(1)} %get-tuple-element.19), channel_id=1, source_target_pairs={{0,16},{16,0},{1,17},{17,1},{2,18},{18,2},{3,19},{19,3},{4,20},{20... | collective-permute-start | bytes 786440 | tf_op jit(solution)/shard_map/ppermute | solution.py:121
  5.8 14.9 %collective-permute-start.2 = (f32[16,512]{1,0:T(8,128)S(1)}, f32[16,512]{1,0:T(8,128)S(1)}, u32[]{:S(2)}, u32[]{:S(2)}) collective-permute-start(f32[16,512]{1,0:T(8,128)S(1)} %copy-done.1), channel_id=1, source_target_pairs={{0,384},{1,416},{2,400},{3,432},{4,144},{5,176},{6,192},{7,96},{8,... | collective-permute-start | bytes 98312 | tf_op jit(solution)/shard_map/ppermute | solution.py:115
  16.5 0.7 copy-start.2
  16.5 0.7 copy-start.3
  21.6 20.1 %all-to-all-start = ((f32[32,16,256]{2,1,0:T(8,128)}), f32[32,16,256]{2,1,0:T(8,128)S(1)}, u32[]{:S(2)}, u32[]{:S(2)}) async-start(f32[32,16,256]{2,1,0:T(8,128)} %bitcast.6), calls=%async_computation | async-start | bytes 1048576 | tf_op jit(solution)/shard_map/all_to_all | solution.py:148
  34.7 7.1 %collective-permute-start.1 = (f32[256,512]{1,0:T(8,128)S(1)}, f32[256,512]{1,0:T(8,128)S(1)}, u32[]{:S(2)}, u32[]{:S(2)}) collective-permute-start(f32[256,512]{1,0:T(8,128)S(1)} %maximum_select_fusion.1), channel_id=1, source_target_pairs={{0,32},{32,0},{1,33},{33,1},{2,34},{34,2},{3,35},{35,3},{4,36},{36... | collective-permute-start | bytes 1572872 | tf_op jit(solution)/shard_map/ppermute | solution.py:127
  42.7 9.4 %collective-permute-start.3 = (f32[8,32,256]{2,1,0:T(8,128)S(1)}, f32[8,32,256]{2,1,0:T(8,128)S(1)}, u32[]{:S(2)}, u32[]{:S(2)}) collective-permute-start(f32[8,32,256]{2,1,0:T(8,128)S(1)} %fusion.2), channel_id=1, source_target_pairs={{0,1},{1,0},{2,3},{3,2},{4,5},{5,4},{6,7},{7,6},{8,9},{9,8},{10,11... | collective-permute-start | bytes 786440 | tf_op jit(solution)/shard_map/ppermute | solution.py:172
  52.8 30.3 %all-to-all-start.1 = ((f32[8,32,256]{2,1,0:T(8,128)}), f32[8,32,256]{2,1,0:T(8,128)S(1)}, u32[]{:S(2)}, u32[]{:S(2)}) async-start(f32[8,32,256]{2,1,0:T(8,128)} %add.75), calls=%async_computation.1 | async-start | bytes 524288 | tf_op jit(solution)/shard_map/all_to_all | solution.py:181
  65.4 4.4 %collective-permute-start.5 = (f32[16,256]{1,0:T(8,128)S(1)}, f32[16,256]{1,0:T(8,128)S(1)}, u32[]{:S(2)}, u32[]{:S(2)}) collective-permute-start(f32[16,256]{1,0:T(8,128)S(1)} %get-tuple-element.21), channel_id=1, source_target_pairs={{0,32},{32,0},{1,33},{33,1},{2,34},{34,2},{3,35},{35,3},{4,36},{36... | collective-permute-start | bytes 49160 | tf_op jit(solution)/shard_map/ppermute | solution.py:156
  114.8 17.0 %all-to-all-start.4 = ((f32[64,8,128]{2,1,0:T(8,128)}), f32[64,8,128]{2,1,0:T(8,128)S(1)}, u32[]{:S(2)}, u32[]{:S(2)}) async-start(f32[64,8,128]{2,1,0:T(8,128)} %broadcast_in_dim.44), calls=%async_computation.4 | async-start | bytes 524288 | tf_op jit(solution)/shard_map/all_to_all | solution.py:88
  122.4 3.1 %collective-permute-start.4 = (f32[16,256]{1,0:T(8,128)S(1)}, f32[16,256]{1,0:T(8,128)S(1)}, u32[]{:S(2)}, u32[]{:S(2)}) collective-permute-start(f32[16,256]{1,0:T(8,128)S(1)} %get-tuple-element.23), channel_id=1, source_target_pairs={{0,32},{32,0},{1,33},{33,1},{2,34},{34,2},{3,35},{35,3},{4,36},{36... | collective-permute-start | bytes 49160 | tf_op jit(solution)/shard_map/ppermute | solution.py:184

commit v10 on v9

--- a/solution.py
+++ b/solution.py
@@ -16,6 +16,7 @@
 BACK = ("c", "yh", "x", "yl", "zl")
 ALL = ("yh", "x", "c", "yl", "zh", "zl")
 SWAP = [(0, 1), (1, 0)]
+FAR_FIRST = [[(ZH // 2 + i) % ZH for i in range(ZH)]]
 
 
 def flat_of(yh, x, c, yl, zh, zl):
@@ -83,9 +84,9 @@
     return pairs, groups
 
 
-def spread(value, axis):
+def spread(value, axis, groups=None):
     copies = jnp.broadcast_to(value[None], (lax.axis_size(axis),) + value.shape)
-    return lax.all_to_all(copies, axis, 0, 0, tiled=True)
+    return lax.all_to_all(copies, axis, 0, 0, tiled=True, axis_index_groups=groups)
 
 
 def body(ancestor_inverse, block_mask, block_ids, row_lists, panels, diag_inverse):
@@ -124,6 +125,7 @@
         jnp.concatenate([kept, came], axis=1),
         jnp.concatenate([came, kept], axis=1),
     )
+    own_rows = lax.optimization_barrier(own_rows)
     other_rows = lax.ppermute(own_rows, "c", SWAP)
 
     def keep_cols(grid_row):
@@ -134,7 +136,8 @@
 
     def by_depth(rows, grid_row):
         rows = rows * keep_cols(grid_row)[None, :]
-        return rows.reshape(far, near, row_count, 2 * col_span)
+        rows = rows.reshape(far, near, row_count, 2 * col_span)
+        return jnp.roll(rows, -far // 2, axis=0)
 
     pieces = jnp.stack(
         [by_depth(own_rows, prow_index), by_depth(other_rows, prow_index ^ 1)], axis=2
@@ -178,7 +181,9 @@
         diag_inverse.reshape(S * W, W), lax.axis_index(BACK) * part, part, 0
     )
     pair_sum, own_diag = lax.optimization_barrier((pair_sum, own_diag))
-    parts = lax.all_to_all(pair_sum, "zh", 0, 0, tiled=True)
+    parts = lax.all_to_all(
+        pair_sum, "zh", 0, 0, tiled=True, axis_index_groups=FAR_FIRST
+    )
     summed = jnp.sum(parts, axis=0).reshape(2, row_count, half)
 
     back = lax.ppermute(summed[1], "c", SWAP)
@@ -198,7 +203,7 @@
     peers = lax.axis_size(SIDE)
     terms = lax.all_to_all(local_diag.reshape(peers, part, W), SIDE, 0, 0, tiled=True)
     terms = jnp.sum(terms, axis=0)
-    terms = own_diag + jnp.sum(spread(terms, "zh"), axis=0)
+    terms = own_diag + jnp.sum(spread(terms, "zh", FAR_FIRST), axis=0)
     diag_blocks = spread(terms, BACK).reshape(S, W, W)
     return (inverse_panels, diag_blocks)
 

time: 133 us -> 126 us (0.947)
  waiting for transfers between devices: 34.7 us -> 28.7 us
  blocking collectives: 30.5 us -> 26.3 us
  starting transfers between devices: 56.9 us -> 59.9 us
    all_to_all x2, waiting for transfers between devices: 19 us -> 13.2 us  [the longest x1 7.41 us: body(): lax.all_to_all(pair_sum, 'zh', 0, 0, tiled=True, axis_index_groups=FAR_FI...]
    all_to_all x2, starting transfers between devices: 20.2 us -> 23.1 us  [the longest x1 15.5 us: body(): lax.all_to_all(pair_sum, 'zh', 0, 0, tiled=True, axis_index_groups=FAR_FI...]
    all_to_all x1, blocking collectives: 15.2 us -> 13 us  [body(): lax.all_to_all(local_diag.reshape(peers, part, W), SIDE, 0, 0, tiled=True)]
    all_to_all x1, blocking collectives: 15.3 us -> 13.3 us  [spread(): lax.all_to_all(copies, axis, 0, 0, tiled=True, axis_index_groups=groups)]
  transfers between devices with their start and end apart: 9 -> 9, of which waited for: 7 -> 7; matrix products, arithmetic and copies ran while one was open for 3% -> 4% of each run, Pallas kernels for 0% -> 0%
where the time goes in v10:
time: 126 us
  starting transfers between devices  59.9 us (48%)
  waiting for transfers between devices  28.7 us (23%)
  blocking collectives  26.3 us (21%)
  local copies, waits for them, and re-layouts  4.81 us (4%)
  other arithmetic  3.3 us (3%)
  matrix products  1.57 us (1%)
    all_to_all x1, starting transfers between devices, body(): lax.all_to_all(pair_sum, 'zh', 0, 0, tiled=True, axis_index_groups=FAR_FI...  15.5 us
    all_to_all x1, blocking collectives, spread(): lax.all_to_all(copies, axis, 0, 0, tiled=True, axis_index_groups=groups)  13.3 us
    all_to_all x1, starting transfers between devices, body(): lax.all_to_all(outgoing, ALL, 0, 0, tiled=True, axis_index_groups=groups)  13.1 us
    all_to_all x1, blocking collectives, body(): lax.all_to_all(local_diag.reshape(peers, part, W), SIDE, 0, 0, tiled=True)  13 us
    ppermute x1, starting transfers between devices, body(): moved = lax.ppermute(panels, ALL, pairs)  9.82 us
    all_to_all x1, starting transfers between devices, spread(): lax.all_to_all(copies, axis, 0, 0, tiled=True, axis_index_groups=groups)  7.57 us
    all_to_all x1, waiting for transfers between devices, body(): lax.all_to_all(pair_sum, 'zh', 0, 0, tiled=True, axis_index_groups=FAR_FI...  7.41 us
    ppermute x1, waiting for transfers between devices, body(): arrived = lax.ppermute(leaving, 'zl', SWAP)  6.75 us
  transfers between devices with their start and end apart: 9, of which 7 were waited for; matrix products, arithmetic and copies ran while one was open for 4% of the time, Pallas kernels for 0%

profile of v10, /device:TPU:1, one launch (start us, length us, event | category | flops | bytes accessed | tf_op | source)
XLA Modules:
  0.0 125.5 jit_solution(11245778293097804786)
XLA Ops:
  0.6 0.0 copy-start
  0.7 0.0 copy-start.1
  0.7 1.1 slice_select_fusion.1
  1.8 4.0 %collective-permute-start = (f32[256,256]{1,0:T(8,128)S(1)}, f32[256,256]{1,0:T(8,128)S(1)}, u32[]{:S(2)}, u32[]{:S(2)}) collective-permute-start(f32[256,256]{1,0:T(8,128)S(1)} %get-tuple-element.23), channel_id=1, source_target_pairs={{0,16},{16,0},{1,17},{17,1},{2,18},{18,2},{3,19},{19,3},{4,20},{20... | collective-permute-start | bytes 786440 | tf_op jit(solution)/shard_map/ppermute | solution.py:122
  5.8 0.0 copy-done.1
  5.8 9.8 %collective-permute-start.2 = (f32[16,512]{1,0:T(8,128)S(1)}, f32[16,512]{1,0:T(8,128)S(1)}, u32[]{:S(2)}, u32[]{:S(2)}) collective-permute-start(f32[16,512]{1,0:T(8,128)S(1)} %copy-done.1), channel_id=1, source_target_pairs={{0,384},{1,416},{2,400},{3,432},{4,144},{5,176},{6,192},{7,96},{8,... | collective-permute-start | bytes 98312 | tf_op jit(solution)/shard_map/ppermute | solution.py:116
  15.7 0.8 fusion.15
  16.5 0.1 reshape.98
  16.6 0.0 copy-start.2
  16.6 0.0 copy-start.3
  16.6 0.1 reshape.99
  16.6 0.6 copy-done.2
  17.2 0.0 copy-done.3
  17.2 0.1 compare_reduce_fusion
  17.3 0.1 reshape.108
  17.4 0.2 dynamic-slice_reduce_fusion
  17.6 0.1 broadcast_bitcast_fusion.1
  17.7 0.1 constant_dynamic-slice_fusion.1
  17.8 0.1 copy.26
  17.9 0.1 broadcast_bitcast_fusion
  17.9 0.2 fusion.12
  18.2 0.1 broadcast_bitcast_fusion.2
  18.2 0.1 broadcast_bitcast_fusion.3
  18.3 2.4 %collective-permute-done.2 = f32[16,512]{1,0:T(8,128)S(1)} collective-permute-done((f32[16,512]{1,0:T(8,128)S(1)}, f32[16,512]{1,0:T(8,128)S(1)}, u32[]{:S(2)}, u32[]{:S(2)}) %collective-permute-start.2) | collective-permute-done | bytes 32800 | tf_op jit(solution)/shard_map/ppermute | solution.py:116
  20.8 0.8 broadcast_in_dim.40
  21.6 13.1 %all-to-all-start = ((f32[32,16,256]{2,1,0:T(8,128)}), f32[32,16,256]{2,1,0:T(8,128)S(1)}, u32[]{:S(2)}, u32[]{:S(2)}) async-start(f32[32,16,256]{2,1,0:T(8,128)} %bitcast.9), calls=%async_computation | async-start | bytes 1048576 | tf_op jit(solution)/shard_map/all_to_all | solution.py:151
  34.7 0.0 collective-permute-done
  34.8 2.2 %collective-permute-start.1 = (f32[256,512]{1,0:T(8,128)S(1)}, f32[256,512]{1,0:T(8,128)S(1)}, u32[]{:S(2)}, u32[]{:S(2)}) collective-permute-start(f32[256,512]{1,0:T(8,128)S(1)} %maximum_select_fusion), channel_id=1, source_target_pairs={{0,32},{32,0},{1,33},{33,1},{2,34},{34,2},{3,35},{35,3},{4,36},{36... | collective-permute-start | bytes 1572872 | tf_op jit(solution)/shard_map/ppermute | solution.py:129
  37.0 0.1 broadcast_multiply_fusion.1
  37.2 4.7 %all-to-all-done = f32[32,16,256]{2,1,0:T(8,128)S(1)} async-done(((f32[32,16,256]{2,1,0:T(8,128)}), f32[32,16,256]{2,1,0:T(8,128)S(1)}, u32[]{:S(2)}, u32[]{:S(2)}) %all-to-all-start) | async-done | bytes 524320 | tf_op jit(solution)/shard_map/all_to_all | solution.py:151
  41.9 0.0 collective-permute-done.1
  41.9 0.1 broadcast_multiply_fusion
  42.1 0.1 broadcast_select_fusion
  42.3 0.6 fusion.1
  42.9 1.9 %collective-permute-start.3 = (f32[8,32,256]{2,1,0:T(8,128)S(1)}, f32[8,32,256]{2,1,0:T(8,128)S(1)}, u32[]{:S(2)}, u32[]{:S(2)}) collective-permute-start(f32[8,32,256]{2,1,0:T(8,128)S(1)} %fusion.1), channel_id=1, source_target_pairs={{0,1},{1,0},{2,3},{3,2},{4,5},{5,4},{6,7},{7,6},{8,9},{9,8},{10,11... | collective-permute-start | bytes 786440 | tf_op jit(solution)/shard_map/ppermute | solution.py:175
  44.8 0.0 copy-done
  44.9 0.6 fusion.3
  45.5 6.8 %collective-permute-done.3 = f32[8,32,256]{2,1,0:T(8,128)S(1)} collective-permute-done((f32[8,32,256]{2,1,0:T(8,128)S(1)}, f32[8,32,256]{2,1,0:T(8,128)S(1)}, u32[]{:S(2)}, u32[]{:S(2)}) %collective-permute-start.3) | collective-permute-done | bytes 262176 | tf_op jit(solution)/shard_map/ppermute | solution.py:175
  52.2 0.7 add.75
  53.0 15.5 %all-to-all-start.1 = ((f32[8,32,256]{2,1,0:T(8,128)}), f32[8,32,256]{2,1,0:T(8,128)S(1)}, u32[]{:S(2)}, u32[]{:S(2)}) async-start(f32[8,32,256]{2,1,0:T(8,128)} %add.75), calls=%async_computation.1 | async-start | bytes 524288 | tf_op jit(solution)/shard_map/all_to_all | solution.py:184
  68.5 3.5 %collective-permute-start.5 = (f32[16,256]{1,0:T(8,128)S(1)}, f32[16,256]{1,0:T(8,128)S(1)}, u32[]{:S(2)}, u32[]{:S(2)}) collective-permute-start(f32[16,256]{1,0:T(8,128)S(1)} %get-tuple-element.25), channel_id=1, source_target_pairs={{0,32},{32,0},{1,33},{33,1},{2,34},{34,2},{3,35},{35,3},{4,36},{36... | collective-permute-start | bytes 49160 | tf_op jit(solution)/shard_map/ppermute | solution.py:159
  72.0 0.8 collective-permute-done.5
  72.8 7.4 %all-to-all-done.1 = f32[8,32,256]{2,1,0:T(8,128)S(1)} async-done(((f32[8,32,256]{2,1,0:T(8,128)}), f32[8,32,256]{2,1,0:T(8,128)S(1)}, u32[]{:S(2)}, u32[]{:S(2)}) %all-to-all-start.1) | async-done | bytes 262176 | tf_op jit(solution)/shard_map/all_to_all | solution.py:184
  80.3 0.4 fusion.5
  80.7 13.0 %all_to_all.25 = f32[32,8,128]{2,1,0:T(8,128)S(1)} all-to-all(f32[32,8,128]{2,1,0:T(8,128)S(1)} %bitcast.67), channel_id=1, replica_groups=mesh['yh'=2,'x'=4,'c'=2,'yl'=2,'zh'=8,'zl'=2] {'yh','x','yl','zl'}, dimensions={0} | all-to-all | bytes 262144 | tf_op jit(solution)/shard_map/all_to_all | solution.py:204
  93.7 13.3 %all_to_all.26 = f32[8,8,128]{2,1,0:T(8,128)S(1)} all-to-all(f32[8,8,128]{2,1,0:T(8,128)S(1)} %broadcast_in_dim.43), channel_id=1, replica_groups={{8,10,12,14,0,2,4,6},{9,11,13,15,1,3,5,7},{24,26,28,30,16,18,20,22},{25..., dimensions={0} | all-to-all | bytes 65536 | tf_op jit(solution)/shard_map/all_to_all | solution.py:89
  107.0 0.7 broadcast_in_dim.44
  107.7 7.6 %all-to-all-start.4 = ((f32[64,8,128]{2,1,0:T(8,128)}), f32[64,8,128]{2,1,0:T(8,128)S(1)}, u32[]{:S(2)}, u32[]{:S(2)}) async-start(f32[64,8,128]{2,1,0:T(8,128)} %broadcast_in_dim.44), calls=%async_computation.4 | async-start | bytes 524288 | tf_op jit(solution)/shard_map/all_to_all | solution.py:89
  115.3 2.3 %collective-permute-start.4 = (f32[16,256]{1,0:T(8,128)S(1)}, f32[16,256]{1,0:T(8,128)S(1)}, u32[]{:S(2)}, u32[]{:S(2)}) collective-permute-start(f32[16,256]{1,0:T(8,128)S(1)} %get-tuple-element.27), channel_id=1, source_target_pairs={{0,32},{32,0},{1,33},{33,1},{2,34},{34,2},{3,35},{35,3},{4,36},{36... | collective-permute-start | bytes 49160 | tf_op jit(solution)/shard_map/ppermute | solution.py:189
  117.6 0.8 collective-permute-done.4
  118.4 0.6 fusion.9
  119.0 5.7 %all-to-all-done.4 = f32[64,8,128]{2,1,0:T(8,128)S(1)} async-done(((f32[64,8,128]{2,1,0:T(8,128)}), f32[64,8,128]{2,1,0:T(8,128)S(1)}, u32[]{:S(2)}, u32[]{:S(2)}) %all-to-all-start.4) | async-done | bytes 262176 | tf_op jit(solution)/shard_map/all_to_all | solution.py:89
  124.8 0.7 copy.47
  (26 shorter events, 0.5 us)
Async XLA Ops:
  0.6 44.2 %copy-start = (f32[4,128,128]{2,1,0:T(8,128)S(1)}, f32[4,128,128]{2,1,0:T(8,128)}, u32[]{:S(2)}) copy-start(f32[4,128,128]{2,1,0:T(8,128)} %param.11) | copy-start | bytes 786436
  0.7 5.2 %copy-start.1 = (f32[16,512]{1,0:T(8,128)S(1)}, f32[16,512]{1,0:T(8,128)}, u32[]{:S(2)}) copy-start(f32[16,512]{1,0:T(8,128)} %param.10) | copy-start | bytes 98308
  1.8 33.0 %collective-permute-start = (f32[256,256]{1,0:T(8,128)S(1)}, f32[256,256]{1,0:T(8,128)S(1)}, u32[]{:S(2)}, u32[]{:S(2)}) collective-permute-start(f32[256,256]{1,0:T(8,128)S(1)} %get-tuple-element.23), channel_id=1, source_target_pairs={{0,16},{16,0},{1,17},{17,1},{2,18},{18,2},{3,19},{19,3},{4,20},{20... | collective-permute-start | bytes 786440 | tf_op jit(solution)/shard_map/ppermute | solution.py:122
  5.8 14.9 %collective-permute-start.2 = (f32[16,512]{1,0:T(8,128)S(1)}, f32[16,512]{1,0:T(8,128)S(1)}, u32[]{:S(2)}, u32[]{:S(2)}) collective-permute-start(f32[16,512]{1,0:T(8,128)S(1)} %copy-done.1), channel_id=1, source_target_pairs={{0,384},{1,416},{2,400},{3,432},{4,144},{5,176},{6,192},{7,96},{8,... | collective-permute-start | bytes 98312 | tf_op jit(solution)/shard_map/ppermute | solution.py:116
  16.6 0.7 copy-start.2
  16.6 0.7 copy-start.3
  21.6 20.2 %all-to-all-start = ((f32[32,16,256]{2,1,0:T(8,128)}), f32[32,16,256]{2,1,0:T(8,128)S(1)}, u32[]{:S(2)}, u32[]{:S(2)}) async-start(f32[32,16,256]{2,1,0:T(8,128)} %bitcast.9), calls=%async_computation | async-start | bytes 1048576 | tf_op jit(solution)/shard_map/all_to_all | solution.py:151
  34.8 7.1 %collective-permute-start.1 = (f32[256,512]{1,0:T(8,128)S(1)}, f32[256,512]{1,0:T(8,128)S(1)}, u32[]{:S(2)}, u32[]{:S(2)}) collective-permute-start(f32[256,512]{1,0:T(8,128)S(1)} %maximum_select_fusion), channel_id=1, source_target_pairs={{0,32},{32,0},{1,33},{33,1},{2,34},{34,2},{3,35},{35,3},{4,36},{36... | collective-permute-start | bytes 1572872 | tf_op jit(solution)/shard_map/ppermute | solution.py:129
  42.9 9.4 %collective-permute-start.3 = (f32[8,32,256]{2,1,0:T(8,128)S(1)}, f32[8,32,256]{2,1,0:T(8,128)S(1)}, u32[]{:S(2)}, u32[]{:S(2)}) collective-permute-start(f32[8,32,256]{2,1,0:T(8,128)S(1)} %fusion.1), channel_id=1, source_target_pairs={{0,1},{1,0},{2,3},{3,2},{4,5},{5,4},{6,7},{7,6},{8,9},{9,8},{10,11... | collective-permute-start | bytes 786440 | tf_op jit(solution)/shard_map/ppermute | solution.py:175
  53.0 27.3 %all-to-all-start.1 = ((f32[8,32,256]{2,1,0:T(8,128)}), f32[8,32,256]{2,1,0:T(8,128)S(1)}, u32[]{:S(2)}, u32[]{:S(2)}) async-start(f32[8,32,256]{2,1,0:T(8,128)} %add.75), calls=%async_computation.1 | async-start | bytes 524288 | tf_op jit(solution)/shard_map/all_to_all | solution.py:184
  68.5 4.3 %collective-permute-start.5 = (f32[16,256]{1,0:T(8,128)S(1)}, f32[16,256]{1,0:T(8,128)S(1)}, u32[]{:S(2)}, u32[]{:S(2)}) collective-permute-start(f32[16,256]{1,0:T(8,128)S(1)} %get-tuple-element.25), channel_id=1, source_target_pairs={{0,32},{32,0},{1,33},{33,1},{2,34},{34,2},{3,35},{35,3},{4,36},{36... | collective-permute-start | bytes 49160 | tf_op jit(solution)/shard_map/ppermute | solution.py:159
  107.7 17.1 %all-to-all-start.4 = ((f32[64,8,128]{2,1,0:T(8,128)}), f32[64,8,128]{2,1,0:T(8,128)S(1)}, u32[]{:S(2)}, u32[]{:S(2)}) async-start(f32[64,8,128]{2,1,0:T(8,128)} %broadcast_in_dim.44), calls=%async_computation.4 | async-start | bytes 524288 | tf_op jit(solution)/shard_map/all_to_all | solution.py:89
  115.3 3.1 %collective-permute-start.4 = (f32[16,256]{1,0:T(8,128)S(1)}, f32[16,256]{1,0:T(8,128)S(1)}, u32[]{:S(2)}, u32[]{:S(2)}) collective-permute-start(f32[16,256]{1,0:T(8,128)S(1)} %get-tuple-element.27), channel_id=1, source_target_pairs={{0,32},{32,0},{1,33},{33,1},{2,34},{34,2},{3,35},{35,3},{4,36},{36... | collective-permute-start | bytes 49160 | tf_op jit(solution)/shard_map/ppermute | solution.py:189

commit v11 on v10

--- a/solution.py
+++ b/solution.py
@@ -17,6 +17,20 @@
 ALL = ("yh", "x", "c", "yl", "zh", "zl")
 SWAP = [(0, 1), (1, 0)]
 FAR_FIRST = [[(ZH // 2 + i) % ZH for i in range(ZH)]]
+
+
+def side_order():
+    return [
+        ((((yh + YH // 2) % YH * XS + (x + XS // 2) % XS) * YL + yl) * ZL) + zl
+        for yh in range(YH)
+        for x in range(XS)
+        for yl in range(YL)
+        for zl in range(ZL)
+    ]
+
+
+SIDE_FIRST = [side_order()]
+BACK_FIRST = [[c * len(SIDE_FIRST[0]) + m for c in range(CS) for m in SIDE_FIRST[0]]]
 
 
 def flat_of(yh, x, c, yl, zh, zl):
@@ -177,9 +191,10 @@
     staying, arrived = lax.optimization_barrier((staying, arrived))
     pair_sum = staying + arrived
     part = S // 2 * W // lax.axis_size(SIDE)
-    own_diag = lax.dynamic_slice_in_dim(
-        diag_inverse.reshape(S * W, W), lax.axis_index(BACK) * part, part, 0
-    )
+    far_yh = (lax.axis_index("yh") + YH // 2) % YH
+    far_x = (lax.axis_index("x") + XS // 2) % XS
+    place = (((core * YH + far_yh) * XS + far_x) * YL + side) * ZL + odd
+    own_diag = lax.dynamic_slice_in_dim(diag_inverse.reshape(S * W, W), place * part, part, 0)
     pair_sum, own_diag = lax.optimization_barrier((pair_sum, own_diag))
     parts = lax.all_to_all(
         pair_sum, "zh", 0, 0, tiled=True, axis_index_groups=FAR_FIRST
@@ -201,10 +216,12 @@
         precision=lax.Precision.HIGHEST,
     )
     peers = lax.axis_size(SIDE)
-    terms = lax.all_to_all(local_diag.reshape(peers, part, W), SIDE, 0, 0, tiled=True)
+    terms = lax.all_to_all(
+        local_diag.reshape(peers, part, W), SIDE, 0, 0, tiled=True, axis_index_groups=SIDE_FIRST
+    )
     terms = jnp.sum(terms, axis=0)
     terms = own_diag + jnp.sum(spread(terms, "zh", FAR_FIRST), axis=0)
-    diag_blocks = spread(terms, BACK).reshape(S, W, W)
+    diag_blocks = spread(terms, BACK, BACK_FIRST).reshape(S, W, W)
     return (inverse_panels, diag_blocks)
 
 

time: 126 us -> 125 us (level)
  waiting for transfers between devices: 28.7 us -> 24.3 us
  starting transfers between devices: 59.9 us -> 64.1 us
    all_to_all x1, waiting for transfers between devices: 5.75 us -> 1.19 us  [spread(): lax.all_to_all(copies, axis, 0, 0, tiled=True, axis_index_groups=groups)]
    all_to_all x1, starting transfers between devices: 7.57 us -> 11.9 us  [spread(): lax.all_to_all(copies, axis, 0, 0, tiled=True, axis_index_groups=groups)]
where the time goes in v11:
time: 125 us; the launch traced here: 124 us
  starting transfers between devices  64.1 us (51%)
  blocking collectives  25.3 us (20%)
  waiting for transfers between devices  24.3 us (19%)
  local copies, waits for them, and re-layouts  4.81 us (4%)
  other arithmetic  3.3 us (3%)
  matrix products  1.57 us (1%)
    all_to_all x1, starting transfers between devices, body(): lax.all_to_all(pair_sum, 'zh', 0, 0, tiled=True, axis_index_groups=FAR_FI...  15.5 us
    all_to_all x1, blocking collectives, spread(): lax.all_to_all(copies, axis, 0, 0, tiled=True, axis_index_groups=groups)  13.5 us
    all_to_all x1, starting transfers between devices, body(): lax.all_to_all(outgoing, ALL, 0, 0, tiled=True, axis_index_groups=groups)  13.1 us
    all_to_all x1, starting transfers between devices, spread(): lax.all_to_all(copies, axis, 0, 0, tiled=True, axis_index_groups=groups)  11.9 us
    all_to_all x1, blocking collectives, body(): lax.all_to_all(local_diag.reshape(peers, part, W), SIDE, 0, 0, tiled=True...  11.8 us
    ppermute x1, starting transfers between devices, body(): moved = lax.ppermute(panels, ALL, pairs)  9.82 us
    all_to_all x1, waiting for transfers between devices, body(): lax.all_to_all(pair_sum, 'zh', 0, 0, tiled=True, axis_index_groups=FAR_FI...  7.41 us
    ppermute x1, waiting for transfers between devices, body(): arrived = lax.ppermute(leaving, 'zl', SWAP)  6.75 us
  transfers between devices with their start and end apart: 9, of which 7 were waited for; matrix products, arithmetic and copies ran while one was open for 4% of the time, Pallas kernels for 0%

profile of v11, /device:TPU:1, one launch (start us, length us, event | category | flops | bytes accessed | tf_op | source)
XLA Modules:
  0.0 124.3 jit_solution(3888305301552873963)
XLA Ops:
  0.6 0.0 copy-start
  0.7 0.0 copy-start.1
  0.7 1.1 slice_select_fusion.1
  1.8 4.0 %collective-permute-start = (f32[256,256]{1,0:T(8,128)S(1)}, f32[256,256]{1,0:T(8,128)S(1)}, u32[]{:S(2)}, u32[]{:S(2)}) collective-permute-start(f32[256,256]{1,0:T(8,128)S(1)} %get-tuple-element.23), channel_id=1, source_target_pairs={{0,16},{16,0},{1,17},{17,1},{2,18},{18,2},{3,19},{19,3},{4,20},{20... | collective-permute-start | bytes 786440 | tf_op jit(solution)/shard_map/ppermute | solution.py:136
  5.8 0.0 copy-done.1
  5.8 9.8 %collective-permute-start.2 = (f32[16,512]{1,0:T(8,128)S(1)}, f32[16,512]{1,0:T(8,128)S(1)}, u32[]{:S(2)}, u32[]{:S(2)}) collective-permute-start(f32[16,512]{1,0:T(8,128)S(1)} %copy-done.1), channel_id=1, source_target_pairs={{0,384},{1,416},{2,400},{3,432},{4,144},{5,176},{6,192},{7,96},{8,... | collective-permute-start | bytes 98312 | tf_op jit(solution)/shard_map/ppermute | solution.py:130
  15.7 0.8 fusion.15
  16.5 0.1 reshape.98
  16.6 0.0 copy-start.2
  16.6 0.0 copy-start.3
  16.6 0.1 reshape.99
  16.6 0.6 copy-done.2
  17.2 0.0 copy-done.3
  17.2 0.1 compare_reduce_fusion
  17.3 0.1 reshape.108
  17.4 0.2 dynamic-slice_reduce_fusion
  17.6 0.1 broadcast_bitcast_fusion.1
  17.7 0.1 constant_dynamic-slice_fusion.1
  17.8 0.1 copy.26
  17.9 0.1 broadcast_bitcast_fusion
  17.9 0.2 fusion.12
  18.2 0.1 broadcast_bitcast_fusion.2
  18.2 0.1 broadcast_bitcast_fusion.3
  18.3 2.4 %collective-permute-done.2 = f32[16,512]{1,0:T(8,128)S(1)} collective-permute-done((f32[16,512]{1,0:T(8,128)S(1)}, f32[16,512]{1,0:T(8,128)S(1)}, u32[]{:S(2)}, u32[]{:S(2)}) %collective-permute-start.2) | collective-permute-done | bytes 32800 | tf_op jit(solution)/shard_map/ppermute | solution.py:130
  20.8 0.8 broadcast_in_dim.40
  21.6 13.1 %all-to-all-start = ((f32[32,16,256]{2,1,0:T(8,128)}), f32[32,16,256]{2,1,0:T(8,128)S(1)}, u32[]{:S(2)}, u32[]{:S(2)}) async-start(f32[32,16,256]{2,1,0:T(8,128)} %bitcast.9), calls=%async_computation | async-start | bytes 1048576 | tf_op jit(solution)/shard_map/all_to_all | solution.py:165
  34.7 0.0 collective-permute-done
  34.8 2.2 %collective-permute-start.1 = (f32[256,512]{1,0:T(8,128)S(1)}, f32[256,512]{1,0:T(8,128)S(1)}, u32[]{:S(2)}, u32[]{:S(2)}) collective-permute-start(f32[256,512]{1,0:T(8,128)S(1)} %maximum_select_fusion), channel_id=1, source_target_pairs={{0,32},{32,0},{1,33},{33,1},{2,34},{34,2},{3,35},{35,3},{4,36},{36... | collective-permute-start | bytes 1572872 | tf_op jit(solution)/shard_map/ppermute | solution.py:143
  37.0 0.1 broadcast_multiply_fusion.1
  37.2 4.7 %all-to-all-done = f32[32,16,256]{2,1,0:T(8,128)S(1)} async-done(((f32[32,16,256]{2,1,0:T(8,128)}), f32[32,16,256]{2,1,0:T(8,128)S(1)}, u32[]{:S(2)}, u32[]{:S(2)}) %all-to-all-start) | async-done | bytes 524320 | tf_op jit(solution)/shard_map/all_to_all | solution.py:165
  41.9 0.0 collective-permute-done.1
  41.9 0.1 broadcast_multiply_fusion
  42.1 0.1 broadcast_select_fusion
  42.3 0.6 fusion.1
  42.9 1.9 %collective-permute-start.3 = (f32[8,32,256]{2,1,0:T(8,128)S(1)}, f32[8,32,256]{2,1,0:T(8,128)S(1)}, u32[]{:S(2)}, u32[]{:S(2)}) collective-permute-start(f32[8,32,256]{2,1,0:T(8,128)S(1)} %fusion.1), channel_id=1, source_target_pairs={{0,1},{1,0},{2,3},{3,2},{4,5},{5,4},{6,7},{7,6},{8,9},{9,8},{10,11... | collective-permute-start | bytes 786440 | tf_op jit(solution)/shard_map/ppermute | solution.py:189
  44.8 0.0 copy-done
  44.9 0.6 fusion.3
  45.5 6.7 %collective-permute-done.3 = f32[8,32,256]{2,1,0:T(8,128)S(1)} collective-permute-done((f32[8,32,256]{2,1,0:T(8,128)S(1)}, f32[8,32,256]{2,1,0:T(8,128)S(1)}, u32[]{:S(2)}, u32[]{:S(2)}) %collective-permute-start.3) | collective-permute-done | bytes 262176 | tf_op jit(solution)/shard_map/ppermute | solution.py:189
  52.2 0.7 add.88
  53.0 15.5 %all-to-all-start.1 = ((f32[8,32,256]{2,1,0:T(8,128)}), f32[8,32,256]{2,1,0:T(8,128)S(1)}, u32[]{:S(2)}, u32[]{:S(2)}) async-start(f32[8,32,256]{2,1,0:T(8,128)} %add.88), calls=%async_computation.1 | async-start | bytes 524288 | tf_op jit(solution)/shard_map/all_to_all | solution.py:199
  68.5 3.5 %collective-permute-start.5 = (f32[16,256]{1,0:T(8,128)S(1)}, f32[16,256]{1,0:T(8,128)S(1)}, u32[]{:S(2)}, u32[]{:S(2)}) collective-permute-start(f32[16,256]{1,0:T(8,128)S(1)} %get-tuple-element.25), channel_id=1, source_target_pairs={{0,32},{32,0},{1,33},{33,1},{2,34},{34,2},{3,35},{35,3},{4,36},{36... | collective-permute-start | bytes 49160 | tf_op jit(solution)/shard_map/ppermute | solution.py:173
  72.0 0.8 collective-permute-done.5
  72.8 7.4 %all-to-all-done.1 = f32[8,32,256]{2,1,0:T(8,128)S(1)} async-done(((f32[8,32,256]{2,1,0:T(8,128)}), f32[8,32,256]{2,1,0:T(8,128)S(1)}, u32[]{:S(2)}, u32[]{:S(2)}) %all-to-all-start.1) | async-done | bytes 262176 | tf_op jit(solution)/shard_map/all_to_all | solution.py:199
  80.3 0.4 fusion.5
  80.7 11.8 %all_to_all.25 = f32[32,8,128]{2,1,0:T(8,128)S(1)} all-to-all(f32[32,8,128]{2,1,0:T(8,128)S(1)} %bitcast.67), channel_id=1, replica_groups={{384,385,400,401,448,449,464,465,256,257,272,273,320,321,336,337,128,12..., dimensions={0} | all-to-all | bytes 262144 | tf_op jit(solution)/shard_map/all_to_all | solution.py:219
  92.5 13.5 %all_to_all.26 = f32[8,8,128]{2,1,0:T(8,128)S(1)} all-to-all(f32[8,8,128]{2,1,0:T(8,128)S(1)} %broadcast_in_dim.43), channel_id=1, replica_groups={{8,10,12,14,0,2,4,6},{9,11,13,15,1,3,5,7},{24,26,28,30,16,18,20,22},{25..., dimensions={0} | all-to-all | bytes 65536 | tf_op jit(solution)/shard_map/all_to_all | solution.py:103
  106.1 0.7 broadcast_in_dim.44
  106.8 11.9 %all-to-all-start.4 = ((f32[64,8,128]{2,1,0:T(8,128)}), f32[64,8,128]{2,1,0:T(8,128)S(1)}, u32[]{:S(2)}, u32[]{:S(2)}) async-start(f32[64,8,128]{2,1,0:T(8,128)} %broadcast_in_dim.44), calls=%async_computation.4 | async-start | bytes 524288 | tf_op jit(solution)/shard_map/all_to_all | solution.py:103
  118.7 2.1 %collective-permute-start.4 = (f32[16,256]{1,0:T(8,128)S(1)}, f32[16,256]{1,0:T(8,128)S(1)}, u32[]{:S(2)}, u32[]{:S(2)}) collective-permute-start(f32[16,256]{1,0:T(8,128)S(1)} %get-tuple-element.27), channel_id=1, source_target_pairs={{0,32},{32,0},{1,33},{33,1},{2,34},{34,2},{3,35},{35,3},{4,36},{36... | collective-permute-start | bytes 49160 | tf_op jit(solution)/shard_map/ppermute | solution.py:204
  120.8 1.0 collective-permute-done.4
  121.8 0.6 fusion.9
  122.4 1.2 all-to-all-done.4
  123.6 0.7 copy.47
  (26 shorter events, 0.5 us)
Async XLA Ops:
  0.6 44.2 %copy-start = (f32[4,128,128]{2,1,0:T(8,128)S(1)}, f32[4,128,128]{2,1,0:T(8,128)}, u32[]{:S(2)}) copy-start(f32[4,128,128]{2,1,0:T(8,128)} %param.11) | copy-start | bytes 786436
  0.7 5.2 %copy-start.1 = (f32[16,512]{1,0:T(8,128)S(1)}, f32[16,512]{1,0:T(8,128)}, u32[]{:S(2)}) copy-start(f32[16,512]{1,0:T(8,128)} %param.10) | copy-start | bytes 98308
  1.8 33.0 %collective-permute-start = (f32[256,256]{1,0:T(8,128)S(1)}, f32[256,256]{1,0:T(8,128)S(1)}, u32[]{:S(2)}, u32[]{:S(2)}) collective-permute-start(f32[256,256]{1,0:T(8,128)S(1)} %get-tuple-element.23), channel_id=1, source_target_pairs={{0,16},{16,0},{1,17},{17,1},{2,18},{18,2},{3,19},{19,3},{4,20},{20... | collective-permute-start | bytes 786440 | tf_op jit(solution)/shard_map/ppermute | solution.py:136
  5.8 14.9 %collective-permute-start.2 = (f32[16,512]{1,0:T(8,128)S(1)}, f32[16,512]{1,0:T(8,128)S(1)}, u32[]{:S(2)}, u32[]{:S(2)}) collective-permute-start(f32[16,512]{1,0:T(8,128)S(1)} %copy-done.1), channel_id=1, source_target_pairs={{0,384},{1,416},{2,400},{3,432},{4,144},{5,176},{6,192},{7,96},{8,... | collective-permute-start | bytes 98312 | tf_op jit(solution)/shard_map/ppermute | solution.py:130
  16.6 0.7 copy-start.2
  16.6 0.7 copy-start.3
  21.6 20.2 %all-to-all-start = ((f32[32,16,256]{2,1,0:T(8,128)}), f32[32,16,256]{2,1,0:T(8,128)S(1)}, u32[]{:S(2)}, u32[]{:S(2)}) async-start(f32[32,16,256]{2,1,0:T(8,128)} %bitcast.9), calls=%async_computation | async-start | bytes 1048576 | tf_op jit(solution)/shard_map/all_to_all | solution.py:165
  34.8 7.1 %collective-permute-start.1 = (f32[256,512]{1,0:T(8,128)S(1)}, f32[256,512]{1,0:T(8,128)S(1)}, u32[]{:S(2)}, u32[]{:S(2)}) collective-permute-start(f32[256,512]{1,0:T(8,128)S(1)} %maximum_select_fusion), channel_id=1, source_target_pairs={{0,32},{32,0},{1,33},{33,1},{2,34},{34,2},{3,35},{35,3},{4,36},{36... | collective-permute-start | bytes 1572872 | tf_op jit(solution)/shard_map/ppermute | solution.py:143
  42.9 9.4 %collective-permute-start.3 = (f32[8,32,256]{2,1,0:T(8,128)S(1)}, f32[8,32,256]{2,1,0:T(8,128)S(1)}, u32[]{:S(2)}, u32[]{:S(2)}) collective-permute-start(f32[8,32,256]{2,1,0:T(8,128)S(1)} %fusion.1), channel_id=1, source_target_pairs={{0,1},{1,0},{2,3},{3,2},{4,5},{5,4},{6,7},{7,6},{8,9},{9,8},{10,11... | collective-permute-start | bytes 786440 | tf_op jit(solution)/shard_map/ppermute | solution.py:189
  53.0 27.3 %all-to-all-start.1 = ((f32[8,32,256]{2,1,0:T(8,128)}), f32[8,32,256]{2,1,0:T(8,128)S(1)}, u32[]{:S(2)}, u32[]{:S(2)}) async-start(f32[8,32,256]{2,1,0:T(8,128)} %add.88), calls=%async_computation.1 | async-start | bytes 524288 | tf_op jit(solution)/shard_map/all_to_all | solution.py:199
  68.5 4.3 %collective-permute-start.5 = (f32[16,256]{1,0:T(8,128)S(1)}, f32[16,256]{1,0:T(8,128)S(1)}, u32[]{:S(2)}, u32[]{:S(2)}) collective-permute-start(f32[16,256]{1,0:T(8,128)S(1)} %get-tuple-element.25), channel_id=1, source_target_pairs={{0,32},{32,0},{1,33},{33,1},{2,34},{34,2},{3,35},{35,3},{4,36},{36... | collective-permute-start | bytes 49160 | tf_op jit(solution)/shard_map/ppermute | solution.py:173
  106.8 16.8 %all-to-all-start.4 = ((f32[64,8,128]{2,1,0:T(8,128)}), f32[64,8,128]{2,1,0:T(8,128)S(1)}, u32[]{:S(2)}, u32[]{:S(2)}) async-start(f32[64,8,128]{2,1,0:T(8,128)} %broadcast_in_dim.44), calls=%async_computation.4 | async-start | bytes 524288 | tf_op jit(solution)/shard_map/all_to_all | solution.py:103
  118.7 3.1 %collective-permute-start.4 = (f32[16,256]{1,0:T(8,128)S(1)}, f32[16,256]{1,0:T(8,128)S(1)}, u32[]{:S(2)}, u32[]{:S(2)}) collective-permute-start(f32[16,256]{1,0:T(8,128)S(1)} %get-tuple-element.27), channel_id=1, source_target_pairs={{0,32},{32,0},{1,33},{33,1},{2,34},{34,2},{3,35},{35,3},{4,36},{36... | collective-permute-start | bytes 49160 | tf_op jit(solution)/shard_map/ppermute | solution.py:204

commit v12 on v11

--- a/solution.py
+++ b/solution.py
@@ -159,7 +159,7 @@
     leave = jnp.where(odd == 0, pieces[:, 1], pieces[:, 0]).reshape(-1, 2 * col_span)
     stay = jnp.where(odd == 0, pieces[:, 0], pieces[:, 1]).reshape(-1, 2 * col_span)
 
-    halves = moved.reshape(row_count, CS, half).transpose(1, 0, 2)
+    halves = jnp.stack([moved[:, :half], moved[:, half:]])
     outgoing = jnp.broadcast_to(halves[None], (chunks * YL // CS, CS, row_count, half))
     outgoing = outgoing.reshape(chunks * YL, row_count, half)
     needed = lax.all_to_all(
@@ -170,7 +170,7 @@
     by_core = active_own.reshape(row_count, 2, half).transpose(1, 0, 2)
     mine = jnp.where(core == 0, by_core[0], by_core[1])
     theirs = jnp.where(core == 0, by_core[1], by_core[0])
-    active_pair = jnp.stack([mine, lax.ppermute(theirs, "c", SWAP)])
+    from_core = lax.ppermute(theirs, "c", SWAP)
 
     here = lax.axis_index(DEPTH)
     keep_here = lax.dynamic_slice(
@@ -188,7 +188,8 @@
     leaving = product(leave)
     arrived = lax.ppermute(leaving, "zl", SWAP)
     staying = product(stay)
-    staying, arrived = lax.optimization_barrier((staying, arrived))
+    active_pair = jnp.stack([mine, from_core])
+    staying, arrived, active_pair = lax.optimization_barrier((staying, arrived, active_pair))
     pair_sum = staying + arrived
     part = S // 2 * W // lax.axis_size(SIDE)
     far_yh = (lax.axis_index("yh") + YH // 2) % YH

time: 125 us -> 128 us (1.024)
  waiting for transfers between devices: 24.3 us -> 28.6 us
    all_to_all x1, waiting for transfers between devices: 7.41 us -> 12.3 us  [body(): lax.all_to_all(pair_sum, 'zh', 0, 0, tiled=True, axis_index_groups=FAR_FI...]
  transfers between devices with their start and end apart: 9 -> 9, of which waited for: 7 -> 6; matrix products, arithmetic and copies ran while one was open for 4% -> 4% of each run, Pallas kernels for 0% -> 0%
where the time goes in v12:
time: 128 us; the launch traced here: 127 us
  starting transfers between devices  63.1 us (49%)
  waiting for transfers between devices  28.6 us (22%)
  blocking collectives  24.7 us (19%)
  local copies, waits for them, and re-layouts  4.8 us (4%)
  other arithmetic  3.3 us (3%)
  matrix products  1.57 us (1%)
    all_to_all x1, starting transfers between devices, body(): lax.all_to_all(pair_sum, 'zh', 0, 0, tiled=True, axis_index_groups=FAR_FI...  15.6 us
    all_to_all x1, blocking collectives, spread(): lax.all_to_all(copies, axis, 0, 0, tiled=True, axis_index_groups=groups)  13.5 us
    all_to_all x1, starting transfers between devices, body(): lax.all_to_all(outgoing, ALL, 0, 0, tiled=True, axis_index_groups=groups)  13.1 us
    all_to_all x1, waiting for transfers between devices, body(): lax.all_to_all(pair_sum, 'zh', 0, 0, tiled=True, axis_index_groups=FAR_FI...  12.3 us
    all_to_all x1, starting transfers between devices, spread(): lax.all_to_all(copies, axis, 0, 0, tiled=True, axis_index_groups=groups)  12 us
    all_to_all x1, blocking collectives, body(): lax.all_to_all(local_diag.reshape(peers, part, W), SIDE, 0, 0, tiled=True...  11.2 us
    ppermute x1, starting transfers between devices, body(): moved = lax.ppermute(panels, ALL, pairs)  9.82 us
    ppermute x1, waiting for transfers between devices, body(): arrived = lax.ppermute(leaving, 'zl', SWAP)  7.04 us
  transfers between devices with their start and end apart: 9, of which 6 were waited for; matrix products, arithmetic and copies ran while one was open for 4% of the time, Pallas kernels for 0%

profile of v12, /device:TPU:1, one launch (start us, length us, event | category | flops | bytes accessed | tf_op | source)
XLA Modules:
  0.0 127.0 jit_solution(5617688098936149569)
XLA Ops:
  0.6 0.0 copy-start
  0.7 0.0 copy-start.1
  0.7 1.1 slice_select_fusion.1
  1.8 4.0 %collective-permute-start = (f32[256,256]{1,0:T(8,128)S(1)}, f32[256,256]{1,0:T(8,128)S(1)}, u32[]{:S(2)}, u32[]{:S(2)}) collective-permute-start(f32[256,256]{1,0:T(8,128)S(1)} %get-tuple-element.25), channel_id=1, source_target_pairs={{0,16},{16,0},{1,17},{17,1},{2,18},{18,2},{3,19},{19,3},{4,20},{20... | collective-permute-start | bytes 786440 | tf_op jit(solution)/shard_map/ppermute | solution.py:136
  5.8 0.0 copy-done.1
  5.8 9.8 %collective-permute-start.2 = (f32[16,512]{1,0:T(8,128)S(1)}, f32[16,512]{1,0:T(8,128)S(1)}, u32[]{:S(2)}, u32[]{:S(2)}) collective-permute-start(f32[16,512]{1,0:T(8,128)S(1)} %copy-done.1), channel_id=1, source_target_pairs={{0,384},{1,416},{2,400},{3,432},{4,144},{5,176},{6,192},{7,96},{8,... | collective-permute-start | bytes 98312 | tf_op jit(solution)/shard_map/ppermute | solution.py:130
  15.7 0.8 fusion.15
  16.5 0.1 reshape.95
  16.6 0.1 reshape.96
  16.6 0.2 fusion.12
  16.9 0.1 broadcast_bitcast_fusion.2
  16.9 0.0 copy-start.2
  16.9 0.0 copy-start.3
  16.9 0.1 broadcast_bitcast_fusion.3
  17.0 0.6 copy-done.2
  17.6 0.0 copy-done.3
  17.6 0.1 compare_reduce_fusion
  17.7 0.1 reshape.104
  17.8 0.2 dynamic-slice_reduce_fusion
  18.0 0.1 broadcast_bitcast_fusion.1
  18.1 0.1 constant_dynamic-slice_fusion.1
  18.2 0.1 copy.23
  18.3 0.1 broadcast_bitcast_fusion
  18.3 0.0 copy-done
  18.4 2.4 %collective-permute-done.2 = f32[16,512]{1,0:T(8,128)S(1)} collective-permute-done((f32[16,512]{1,0:T(8,128)S(1)}, f32[16,512]{1,0:T(8,128)S(1)}, u32[]{:S(2)}, u32[]{:S(2)}) %collective-permute-start.2) | collective-permute-done | bytes 32800 | tf_op jit(solution)/shard_map/ppermute | solution.py:130
  20.8 0.9 broadcast_in_dim.40
  21.6 13.1 %all-to-all-start = ((f32[32,16,256]{2,1,0:T(8,128)}), f32[32,16,256]{2,1,0:T(8,128)S(1)}, u32[]{:S(2)}, u32[]{:S(2)}) async-start(f32[32,16,256]{2,1,0:T(8,128)} %bitcast.10), calls=%async_computation | async-start | bytes 1048576 | tf_op jit(solution)/shard_map/all_to_all | solution.py:165
  34.8 0.0 collective-permute-done
  34.8 2.2 %collective-permute-start.1 = (f32[256,512]{1,0:T(8,128)S(1)}, f32[256,512]{1,0:T(8,128)S(1)}, u32[]{:S(2)}, u32[]{:S(2)}) collective-permute-start(f32[256,512]{1,0:T(8,128)S(1)} %maximum_select_fusion), channel_id=1, source_target_pairs={{0,32},{32,0},{1,33},{33,1},{2,34},{34,2},{3,35},{35,3},{4,36},{36... | collective-permute-start | bytes 1572872 | tf_op jit(solution)/shard_map/ppermute | solution.py:143
  37.0 0.1 broadcast_multiply_fusion.1
  37.2 4.7 %all-to-all-done = f32[32,16,256]{2,1,0:T(8,128)S(1)} async-done(((f32[32,16,256]{2,1,0:T(8,128)}), f32[32,16,256]{2,1,0:T(8,128)S(1)}, u32[]{:S(2)}, u32[]{:S(2)}) %all-to-all-start) | async-done | bytes 524320 | tf_op jit(solution)/shard_map/all_to_all | solution.py:165
  41.9 2.3 %collective-permute-start.4 = (f32[16,256]{1,0:T(8,128)S(1)}, f32[16,256]{1,0:T(8,128)S(1)}, u32[]{:S(2)}, u32[]{:S(2)}) collective-permute-start(f32[16,256]{1,0:T(8,128)S(1)} %get-tuple-element.29), channel_id=1, source_target_pairs={{0,32},{32,0},{1,33},{33,1},{2,34},{34,2},{3,35},{35,3},{4,36},{36... | collective-permute-start | bytes 49160 | tf_op jit(solution)/shard_map/ppermute | solution.py:173
  44.3 0.0 collective-permute-done.1
  44.3 0.1 broadcast_multiply_fusion
  44.4 0.1 broadcast_select_fusion
  44.6 0.6 fusion.1
  45.2 1.9 %collective-permute-start.3 = (f32[8,32,256]{2,1,0:T(8,128)S(1)}, f32[8,32,256]{2,1,0:T(8,128)S(1)}, u32[]{:S(2)}, u32[]{:S(2)}) collective-permute-start(f32[8,32,256]{2,1,0:T(8,128)S(1)} %fusion.1), channel_id=1, source_target_pairs={{0,1},{1,0},{2,3},{3,2},{4,5},{5,4},{6,7},{7,6},{8,9},{9,8},{10,11... | collective-permute-start | bytes 786440 | tf_op jit(solution)/shard_map/ppermute | solution.py:189
  47.2 0.0 collective-permute-done.4
  47.2 0.6 fusion.3
  47.8 7.0 %collective-permute-done.3 = f32[8,32,256]{2,1,0:T(8,128)S(1)} collective-permute-done((f32[8,32,256]{2,1,0:T(8,128)S(1)}, f32[8,32,256]{2,1,0:T(8,128)S(1)}, u32[]{:S(2)}, u32[]{:S(2)}) %collective-permute-start.3) | collective-permute-done | bytes 262176 | tf_op jit(solution)/shard_map/ppermute | solution.py:189
  54.9 0.7 add.88
  55.6 15.6 %all-to-all-start.1 = ((f32[8,32,256]{2,1,0:T(8,128)}), f32[8,32,256]{2,1,0:T(8,128)S(1)}, u32[]{:S(2)}, u32[]{:S(2)}) async-start(f32[8,32,256]{2,1,0:T(8,128)} %add.88), calls=%async_computation.1 | async-start | bytes 524288 | tf_op jit(solution)/shard_map/all_to_all | solution.py:200
  71.3 12.3 %all-to-all-done.1 = f32[8,32,256]{2,1,0:T(8,128)S(1)} async-done(((f32[8,32,256]{2,1,0:T(8,128)}), f32[8,32,256]{2,1,0:T(8,128)S(1)}, u32[]{:S(2)}, u32[]{:S(2)}) %all-to-all-start.1) | async-done | bytes 262176 | tf_op jit(solution)/shard_map/all_to_all | solution.py:200
  83.5 0.4 fusion.5
  83.9 11.2 %all_to_all.25 = f32[32,8,128]{2,1,0:T(8,128)S(1)} all-to-all(f32[32,8,128]{2,1,0:T(8,128)S(1)} %bitcast.70), channel_id=1, replica_groups={{384,385,400,401,448,449,464,465,256,257,272,273,320,321,336,337,128,12..., dimensions={0} | all-to-all | bytes 262144 | tf_op jit(solution)/shard_map/all_to_all | solution.py:220
  95.2 13.5 %all_to_all.26 = f32[8,8,128]{2,1,0:T(8,128)S(1)} all-to-all(f32[8,8,128]{2,1,0:T(8,128)S(1)} %broadcast_in_dim.43), channel_id=1, replica_groups={{8,10,12,14,0,2,4,6},{9,11,13,15,1,3,5,7},{24,26,28,30,16,18,20,22},{25..., dimensions={0} | all-to-all | bytes 65536 | tf_op jit(solution)/shard_map/all_to_all | solution.py:103
  108.7 0.7 broadcast_in_dim.44
  109.4 12.0 %all-to-all-start.4 = ((f32[64,8,128]{2,1,0:T(8,128)}), f32[64,8,128]{2,1,0:T(8,128)S(1)}, u32[]{:S(2)}, u32[]{:S(2)}) async-start(f32[64,8,128]{2,1,0:T(8,128)} %broadcast_in_dim.44), calls=%async_computation.4 | async-start | bytes 524288 | tf_op jit(solution)/shard_map/all_to_all | solution.py:103
  121.4 2.1 %collective-permute-start.5 = (f32[16,256]{1,0:T(8,128)S(1)}, f32[16,256]{1,0:T(8,128)S(1)}, u32[]{:S(2)}, u32[]{:S(2)}) collective-permute-start(f32[16,256]{1,0:T(8,128)S(1)} %get-tuple-element.27), channel_id=1, source_target_pairs={{0,32},{32,0},{1,33},{33,1},{2,34},{34,2},{3,35},{35,3},{4,36},{36... | collective-permute-start | bytes 49160 | tf_op jit(solution)/shard_map/ppermute | solution.py:205
  123.5 1.0 collective-permute-done.5
  124.4 0.6 fusion.9
  125.1 1.2 all-to-all-done.4
  126.3 0.7 copy.44
  (26 shorter events, 0.5 us)
Async XLA Ops:
  0.6 17.7 %copy-start = (f32[4,128,128]{2,1,0:T(8,128)S(1)}, f32[4,128,128]{2,1,0:T(8,128)}, u32[]{:S(2)}) copy-start(f32[4,128,128]{2,1,0:T(8,128)} %param.11) | copy-start | bytes 786436
  0.7 5.2 %copy-start.1 = (f32[16,512]{1,0:T(8,128)S(1)}, f32[16,512]{1,0:T(8,128)}, u32[]{:S(2)}) copy-start(f32[16,512]{1,0:T(8,128)} %param.10) | copy-start | bytes 98308
  1.8 33.0 %collective-permute-start = (f32[256,256]{1,0:T(8,128)S(1)}, f32[256,256]{1,0:T(8,128)S(1)}, u32[]{:S(2)}, u32[]{:S(2)}) collective-permute-start(f32[256,256]{1,0:T(8,128)S(1)} %get-tuple-element.25), channel_id=1, source_target_pairs={{0,16},{16,0},{1,17},{17,1},{2,18},{18,2},{3,19},{19,3},{4,20},{20... | collective-permute-start | bytes 786440 | tf_op jit(solution)/shard_map/ppermute | solution.py:136
  5.8 14.9 %collective-permute-start.2 = (f32[16,512]{1,0:T(8,128)S(1)}, f32[16,512]{1,0:T(8,128)S(1)}, u32[]{:S(2)}, u32[]{:S(2)}) collective-permute-start(f32[16,512]{1,0:T(8,128)S(1)} %copy-done.1), channel_id=1, source_target_pairs={{0,384},{1,416},{2,400},{3,432},{4,144},{5,176},{6,192},{7,96},{8,... | collective-permute-start | bytes 98312 | tf_op jit(solution)/shard_map/ppermute | solution.py:130
  16.9 0.7 copy-start.2
  16.9 0.7 copy-start.3
  21.6 20.3 %all-to-all-start = ((f32[32,16,256]{2,1,0:T(8,128)}), f32[32,16,256]{2,1,0:T(8,128)S(1)}, u32[]{:S(2)}, u32[]{:S(2)}) async-start(f32[32,16,256]{2,1,0:T(8,128)} %bitcast.10), calls=%async_computation | async-start | bytes 1048576 | tf_op jit(solution)/shard_map/all_to_all | solution.py:165
  34.8 9.4 %collective-permute-start.1 = (f32[256,512]{1,0:T(8,128)S(1)}, f32[256,512]{1,0:T(8,128)S(1)}, u32[]{:S(2)}, u32[]{:S(2)}) collective-permute-start(f32[256,512]{1,0:T(8,128)S(1)} %maximum_select_fusion), channel_id=1, source_target_pairs={{0,32},{32,0},{1,33},{33,1},{2,34},{34,2},{3,35},{35,3},{4,36},{36... | collective-permute-start | bytes 1572872 | tf_op jit(solution)/shard_map/ppermute | solution.py:143
  41.9 5.3 %collective-permute-start.4 = (f32[16,256]{1,0:T(8,128)S(1)}, f32[16,256]{1,0:T(8,128)S(1)}, u32[]{:S(2)}, u32[]{:S(2)}) collective-permute-start(f32[16,256]{1,0:T(8,128)S(1)} %get-tuple-element.29), channel_id=1, source_target_pairs={{0,32},{32,0},{1,33},{33,1},{2,34},{34,2},{3,35},{35,3},{4,36},{36... | collective-permute-start | bytes 49160 | tf_op jit(solution)/shard_map/ppermute | solution.py:173
  45.2 9.6 %collective-permute-start.3 = (f32[8,32,256]{2,1,0:T(8,128)S(1)}, f32[8,32,256]{2,1,0:T(8,128)S(1)}, u32[]{:S(2)}, u32[]{:S(2)}) collective-permute-start(f32[8,32,256]{2,1,0:T(8,128)S(1)} %fusion.1), channel_id=1, source_target_pairs={{0,1},{1,0},{2,3},{3,2},{4,5},{5,4},{6,7},{7,6},{8,9},{9,8},{10,11... | collective-permute-start | bytes 786440 | tf_op jit(solution)/shard_map/ppermute | solution.py:189
  55.6 27.9 %all-to-all-start.1 = ((f32[8,32,256]{2,1,0:T(8,128)}), f32[8,32,256]{2,1,0:T(8,128)S(1)}, u32[]{:S(2)}, u32[]{:S(2)}) async-start(f32[8,32,256]{2,1,0:T(8,128)} %add.88), calls=%async_computation.1 | async-start | bytes 524288 | tf_op jit(solution)/shard_map/all_to_all | solution.py:200
  109.4 16.9 %all-to-all-start.4 = ((f32[64,8,128]{2,1,0:T(8,128)}), f32[64,8,128]{2,1,0:T(8,128)S(1)}, u32[]{:S(2)}, u32[]{:S(2)}) async-start(f32[64,8,128]{2,1,0:T(8,128)} %broadcast_in_dim.44), calls=%async_computation.4 | async-start | bytes 524288 | tf_op jit(solution)/shard_map/all_to_all | solution.py:103
  121.4 3.1 %collective-permute-start.5 = (f32[16,256]{1,0:T(8,128)S(1)}, f32[16,256]{1,0:T(8,128)S(1)}, u32[]{:S(2)}, u32[]{:S(2)}) collective-permute-start(f32[16,256]{1,0:T(8,128)S(1)} %get-tuple-element.27), channel_id=1, source_target_pairs={{0,32},{32,0},{1,33},{33,1},{2,34},{34,2},{3,35},{35,3},{4,36},{36... | collective-permute-start | bytes 49160 | tf_op jit(solution)/shard_map/ppermute | solution.py:205

commit v13 on v12

--- a/solution.py
+++ b/solution.py
@@ -92,7 +92,7 @@
                 for yl in range(YL)
             ]
             where.update(assign(sources, targets))
-        order = [q * chunks + j for q in blocks for j in range(chunks)]
+        order = [q * chunks + j for q in reversed(blocks) for j in range(chunks)]
         pairs += [(source, where[source]) for source in order]
         groups.append([where[source] for source in order])
     return pairs, groups
@@ -136,8 +136,8 @@
     came = lax.ppermute(sent, "yl", SWAP)
     own_rows = jnp.where(
         side == 0,
+        jnp.concatenate([came, kept], axis=1),
         jnp.concatenate([kept, came], axis=1),
-        jnp.concatenate([came, kept], axis=1),
     )
     own_rows = lax.optimization_barrier(own_rows)
     other_rows = lax.ppermute(own_rows, "c", SWAP)
@@ -146,7 +146,8 @@
         marks = lax.dynamic_slice(block_mask, (grid_row * block_rows + side, 0), (1, cols))
         marks = marks.reshape(cols // deep, deep)
         marks = lax.dynamic_slice(marks, (0, lax.axis_index(DEPTH)), (cols // deep, 1))
-        return jnp.repeat(marks.reshape(cols // deep).astype(jnp.float32), col_span)
+        marks = jnp.flip(marks.reshape(cols // deep).astype(jnp.float32))
+        return jnp.repeat(marks, col_span)
 
     def by_depth(rows, grid_row):
         rows = rows * keep_cols(grid_row)[None, :]
@@ -176,7 +177,7 @@
     keep_here = lax.dynamic_slice(
         active_blocks.reshape(YL, deep, S), (0, here, core * (S // CS)), (YL, 1, S // CS)
     )
-    keep_here = jnp.repeat(keep_here, W, axis=2)
+    keep_here = jnp.repeat(jnp.flip(keep_here, 0), W, axis=2)
     needed = (needed.reshape(YL, col_span, half) * keep_here).reshape(-1, half)
 
     def product(rows):

time: 128 us -> 128 us (level)
  waiting for transfers between devices: 28.6 us -> 30 us
    all_to_all x1, waiting for transfers between devices: 4.69 us -> 6.9 us  [body(): lax.all_to_all(outgoing, ALL, 0, 0, tiled=True, axis_index_groups=groups)]
where the time goes in v13:
time: 128 us
  starting transfers between devices  62.4 us (49%)
  waiting for transfers between devices  30 us (23%)
  blocking collectives  24.6 us (19%)
  local copies, waits for them, and re-layouts  5 us (4%)
  other arithmetic  3.3 us (3%)
  matrix products  1.57 us (1%)
    all_to_all x1, starting transfers between devices, body(): lax.all_to_all(pair_sum, 'zh', 0, 0, tiled=True, axis_index_groups=FAR_FI...  15.5 us
    all_to_all x1, blocking collectives, spread(): lax.all_to_all(copies, axis, 0, 0, tiled=True, axis_index_groups=groups)  13.5 us
    all_to_all x1, waiting for transfers between devices, body(): lax.all_to_all(pair_sum, 'zh', 0, 0, tiled=True, axis_index_groups=FAR_FI...  12.3 us
    all_to_all x1, starting transfers between devices, spread(): lax.all_to_all(copies, axis, 0, 0, tiled=True, axis_index_groups=groups)  12 us
    all_to_all x1, starting transfers between devices, body(): lax.all_to_all(outgoing, ALL, 0, 0, tiled=True, axis_index_groups=groups)  11.9 us
    all_to_all x1, blocking collectives, body(): lax.all_to_all(local_diag.reshape(peers, part, W), SIDE, 0, 0, tiled=True...  11.1 us
    ppermute x1, starting transfers between devices, body(): moved = lax.ppermute(panels, ALL, pairs)  9.82 us
    all_to_all x1, waiting for transfers between devices, body(): lax.all_to_all(outgoing, ALL, 0, 0, tiled=True, axis_index_groups=groups)  6.9 us
  transfers between devices with their start and end apart: 9, of which 6 were waited for; matrix products, arithmetic and copies ran while one was open for 4% of the time, Pallas kernels for 0%

profile of v13, /device:TPU:1, one launch (start us, length us, event | category | flops | bytes accessed | tf_op | source)
XLA Modules:
  0.0 127.8 jit_solution(18025714663450398057)
XLA Ops:
  0.6 0.0 copy-start
  0.7 0.0 copy-start.1
  0.7 1.1 slice_select_fusion.1
  1.8 4.0 %collective-permute-start = (f32[256,256]{1,0:T(8,128)S(1)}, f32[256,256]{1,0:T(8,128)S(1)}, u32[]{:S(2)}, u32[]{:S(2)}) collective-permute-start(f32[256,256]{1,0:T(8,128)S(1)} %get-tuple-element.24), channel_id=1, source_target_pairs={{0,16},{16,0},{1,17},{17,1},{2,18},{18,2},{3,19},{19,3},{4,20},{20... | collective-permute-start | bytes 786440 | tf_op jit(solution)/shard_map/ppermute | solution.py:136
  5.8 0.0 copy-done.1
  5.8 9.8 %collective-permute-start.2 = (f32[16,512]{1,0:T(8,128)S(1)}, f32[16,512]{1,0:T(8,128)S(1)}, u32[]{:S(2)}, u32[]{:S(2)}) collective-permute-start(f32[16,512]{1,0:T(8,128)S(1)} %copy-done.1), channel_id=1, source_target_pairs={{256,336},{257,240},{258,208},{259,112},{260,80},{261,32},{262,448... | collective-permute-start | bytes 98312 | tf_op jit(solution)/shard_map/ppermute | solution.py:130
  15.7 0.8 fusion.15
  16.5 0.1 reshape.95
  16.6 0.1 reshape.96
  16.6 0.2 fusion.12
  16.9 0.1 rev.14
  17.0 0.1 broadcast_bitcast_fusion.2
  17.0 0.0 copy-start.2
  17.0 0.1 rev.13
  17.1 0.0 copy-start.3
  17.1 0.1 broadcast_bitcast_fusion.3
  17.2 0.5 copy-done.2
  17.7 0.1 copy-done.3
  17.8 0.1 compare_reduce_fusion
  17.9 0.1 reshape.104
  18.0 0.2 dynamic-slice_reduce_fusion
  18.2 0.1 broadcast_bitcast_fusion.1
  18.3 0.1 constant_dynamic-slice_fusion.1
  18.4 0.1 copy.23
  18.5 0.1 broadcast_bitcast_fusion
  18.5 0.0 copy-done
  18.6 2.2 %collective-permute-done.2 = f32[16,512]{1,0:T(8,128)S(1)} collective-permute-done((f32[16,512]{1,0:T(8,128)S(1)}, f32[16,512]{1,0:T(8,128)S(1)}, u32[]{:S(2)}, u32[]{:S(2)}) %collective-permute-start.2) | collective-permute-done | bytes 32800 | tf_op jit(solution)/shard_map/ppermute | solution.py:130
  20.8 0.9 broadcast_in_dim.40
  21.6 11.9 %all-to-all-start = ((f32[32,16,256]{2,1,0:T(8,128)}), f32[32,16,256]{2,1,0:T(8,128)S(1)}, u32[]{:S(2)}, u32[]{:S(2)}) async-start(f32[32,16,256]{2,1,0:T(8,128)} %bitcast.10), calls=%async_computation | async-start | bytes 1048576 | tf_op jit(solution)/shard_map/all_to_all | solution.py:166
  33.5 0.0 collective-permute-done
  33.6 2.3 %collective-permute-start.1 = (f32[256,512]{1,0:T(8,128)S(1)}, f32[256,512]{1,0:T(8,128)S(1)}, u32[]{:S(2)}, u32[]{:S(2)}) collective-permute-start(f32[256,512]{1,0:T(8,128)S(1)} %maximum_select_fusion), channel_id=1, source_target_pairs={{0,32},{32,0},{1,33},{33,1},{2,34},{34,2},{3,35},{35,3},{4,36},{36... | collective-permute-start | bytes 1572872 | tf_op jit(solution)/shard_map/ppermute | solution.py:143
  35.9 0.1 broadcast_multiply_fusion.1
  36.1 6.9 %all-to-all-done = f32[32,16,256]{2,1,0:T(8,128)S(1)} async-done(((f32[32,16,256]{2,1,0:T(8,128)}), f32[32,16,256]{2,1,0:T(8,128)S(1)}, u32[]{:S(2)}, u32[]{:S(2)}) %all-to-all-start) | async-done | bytes 524320 | tf_op jit(solution)/shard_map/all_to_all | solution.py:166
  43.0 2.3 %collective-permute-start.4 = (f32[16,256]{1,0:T(8,128)S(1)}, f32[16,256]{1,0:T(8,128)S(1)}, u32[]{:S(2)}, u32[]{:S(2)}) collective-permute-start(f32[16,256]{1,0:T(8,128)S(1)} %get-tuple-element.29), channel_id=1, source_target_pairs={{0,32},{32,0},{1,33},{33,1},{2,34},{34,2},{3,35},{35,3},{4,36},{36... | collective-permute-start | bytes 49160 | tf_op jit(solution)/shard_map/ppermute | solution.py:174
  45.4 0.0 collective-permute-done.1
  45.4 0.1 broadcast_multiply_fusion
  45.5 0.1 broadcast_select_fusion
  45.7 0.6 fusion.1
  46.3 2.5 %collective-permute-start.3 = (f32[8,32,256]{2,1,0:T(8,128)S(1)}, f32[8,32,256]{2,1,0:T(8,128)S(1)}, u32[]{:S(2)}, u32[]{:S(2)}) collective-permute-start(f32[8,32,256]{2,1,0:T(8,128)S(1)} %fusion.1), channel_id=1, source_target_pairs={{0,1},{1,0},{2,3},{3,2},{4,5},{5,4},{6,7},{7,6},{8,9},{9,8},{10,11... | collective-permute-start | bytes 786440 | tf_op jit(solution)/shard_map/ppermute | solution.py:190
  48.9 0.0 collective-permute-done.4
  49.0 0.6 fusion.3
  49.6 6.4 %collective-permute-done.3 = f32[8,32,256]{2,1,0:T(8,128)S(1)} collective-permute-done((f32[8,32,256]{2,1,0:T(8,128)S(1)}, f32[8,32,256]{2,1,0:T(8,128)S(1)}, u32[]{:S(2)}, u32[]{:S(2)}) %collective-permute-start.3) | collective-permute-done | bytes 262176 | tf_op jit(solution)/shard_map/ppermute | solution.py:190
  56.0 0.7 add.88
  56.7 15.5 %all-to-all-start.1 = ((f32[8,32,256]{2,1,0:T(8,128)}), f32[8,32,256]{2,1,0:T(8,128)S(1)}, u32[]{:S(2)}, u32[]{:S(2)}) async-start(f32[8,32,256]{2,1,0:T(8,128)} %add.88), calls=%async_computation.1 | async-start | bytes 524288 | tf_op jit(solution)/shard_map/all_to_all | solution.py:201
  72.2 12.3 %all-to-all-done.1 = f32[8,32,256]{2,1,0:T(8,128)S(1)} async-done(((f32[8,32,256]{2,1,0:T(8,128)}), f32[8,32,256]{2,1,0:T(8,128)S(1)}, u32[]{:S(2)}, u32[]{:S(2)}) %all-to-all-start.1) | async-done | bytes 262176 | tf_op jit(solution)/shard_map/all_to_all | solution.py:201
  84.5 0.4 fusion.5
  84.9 11.1 %all_to_all.25 = f32[32,8,128]{2,1,0:T(8,128)S(1)} all-to-all(f32[32,8,128]{2,1,0:T(8,128)S(1)} %bitcast.70), channel_id=1, replica_groups={{384,385,400,401,448,449,464,465,256,257,272,273,320,321,336,337,128,12..., dimensions={0} | all-to-all | bytes 262144 | tf_op jit(solution)/shard_map/all_to_all | solution.py:221
  96.0 13.5 %all_to_all.26 = f32[8,8,128]{2,1,0:T(8,128)S(1)} all-to-all(f32[8,8,128]{2,1,0:T(8,128)S(1)} %broadcast_in_dim.43), channel_id=1, replica_groups={{8,10,12,14,0,2,4,6},{9,11,13,15,1,3,5,7},{24,26,28,30,16,18,20,22},{25..., dimensions={0} | all-to-all | bytes 65536 | tf_op jit(solution)/shard_map/all_to_all | solution.py:103
  109.5 0.7 broadcast_in_dim.44
  110.2 12.0 %all-to-all-start.4 = ((f32[64,8,128]{2,1,0:T(8,128)}), f32[64,8,128]{2,1,0:T(8,128)S(1)}, u32[]{:S(2)}, u32[]{:S(2)}) async-start(f32[64,8,128]{2,1,0:T(8,128)} %broadcast_in_dim.44), calls=%async_computation.4 | async-start | bytes 524288 | tf_op jit(solution)/shard_map/all_to_all | solution.py:103
  122.2 2.1 %collective-permute-start.5 = (f32[16,256]{1,0:T(8,128)S(1)}, f32[16,256]{1,0:T(8,128)S(1)}, u32[]{:S(2)}, u32[]{:S(2)}) collective-permute-start(f32[16,256]{1,0:T(8,128)S(1)} %get-tuple-element.27), channel_id=1, source_target_pairs={{0,32},{32,0},{1,33},{33,1},{2,34},{34,2},{3,35},{35,3},{4,36},{36... | collective-permute-start | bytes 49160 | tf_op jit(solution)/shard_map/ppermute | solution.py:206
  124.3 1.0 collective-permute-done.5
  125.3 0.6 fusion.9
  125.9 1.2 all-to-all-done.4
  127.1 0.7 copy.44
  (27 shorter events, 0.5 us)
Async XLA Ops:
  0.6 17.9 %copy-start = (f32[4,128,128]{2,1,0:T(8,128)S(1)}, f32[4,128,128]{2,1,0:T(8,128)}, u32[]{:S(2)}) copy-start(f32[4,128,128]{2,1,0:T(8,128)} %param.11) | copy-start | bytes 786436
  0.7 5.2 %copy-start.1 = (f32[16,512]{1,0:T(8,128)S(1)}, f32[16,512]{1,0:T(8,128)}, u32[]{:S(2)}) copy-start(f32[16,512]{1,0:T(8,128)} %param.10) | copy-start | bytes 98308
  1.8 31.8 %collective-permute-start = (f32[256,256]{1,0:T(8,128)S(1)}, f32[256,256]{1,0:T(8,128)S(1)}, u32[]{:S(2)}, u32[]{:S(2)}) collective-permute-start(f32[256,256]{1,0:T(8,128)S(1)} %get-tuple-element.24), channel_id=1, source_target_pairs={{0,16},{16,0},{1,17},{17,1},{2,18},{18,2},{3,19},{19,3},{4,20},{20... | collective-permute-start | bytes 786440 | tf_op jit(solution)/shard_map/ppermute | solution.py:136
  5.8 14.9 %collective-permute-start.2 = (f32[16,512]{1,0:T(8,128)S(1)}, f32[16,512]{1,0:T(8,128)S(1)}, u32[]{:S(2)}, u32[]{:S(2)}) collective-permute-start(f32[16,512]{1,0:T(8,128)S(1)} %copy-done.1), channel_id=1, source_target_pairs={{256,336},{257,240},{258,208},{259,112},{260,80},{261,32},{262,448... | collective-permute-start | bytes 98312 | tf_op jit(solution)/shard_map/ppermute | solution.py:130
  17.0 0.7 copy-start.2
  17.1 0.7 copy-start.3
  21.6 21.4 %all-to-all-start = ((f32[32,16,256]{2,1,0:T(8,128)}), f32[32,16,256]{2,1,0:T(8,128)S(1)}, u32[]{:S(2)}, u32[]{:S(2)}) async-start(f32[32,16,256]{2,1,0:T(8,128)} %bitcast.10), calls=%async_computation | async-start | bytes 1048576 | tf_op jit(solution)/shard_map/all_to_all | solution.py:166
  33.6 11.8 %collective-permute-start.1 = (f32[256,512]{1,0:T(8,128)S(1)}, f32[256,512]{1,0:T(8,128)S(1)}, u32[]{:S(2)}, u32[]{:S(2)}) collective-permute-start(f32[256,512]{1,0:T(8,128)S(1)} %maximum_select_fusion), channel_id=1, source_target_pairs={{0,32},{32,0},{1,33},{33,1},{2,34},{34,2},{3,35},{35,3},{4,36},{36... | collective-permute-start | bytes 1572872 | tf_op jit(solution)/shard_map/ppermute | solution.py:143
  43.0 5.9 %collective-permute-start.4 = (f32[16,256]{1,0:T(8,128)S(1)}, f32[16,256]{1,0:T(8,128)S(1)}, u32[]{:S(2)}, u32[]{:S(2)}) collective-permute-start(f32[16,256]{1,0:T(8,128)S(1)} %get-tuple-element.29), channel_id=1, source_target_pairs={{0,32},{32,0},{1,33},{33,1},{2,34},{34,2},{3,35},{35,3},{4,36},{36... | collective-permute-start | bytes 49160 | tf_op jit(solution)/shard_map/ppermute | solution.py:174
  46.3 9.6 %collective-permute-start.3 = (f32[8,32,256]{2,1,0:T(8,128)S(1)}, f32[8,32,256]{2,1,0:T(8,128)S(1)}, u32[]{:S(2)}, u32[]{:S(2)}) collective-permute-start(f32[8,32,256]{2,1,0:T(8,128)S(1)} %fusion.1), channel_id=1, source_target_pairs={{0,1},{1,0},{2,3},{3,2},{4,5},{5,4},{6,7},{7,6},{8,9},{9,8},{10,11... | collective-permute-start | bytes 786440 | tf_op jit(solution)/shard_map/ppermute | solution.py:190
  56.7 27.7 %all-to-all-start.1 = ((f32[8,32,256]{2,1,0:T(8,128)}), f32[8,32,256]{2,1,0:T(8,128)S(1)}, u32[]{:S(2)}, u32[]{:S(2)}) async-start(f32[8,32,256]{2,1,0:T(8,128)} %add.88), calls=%async_computation.1 | async-start | bytes 524288 | tf_op jit(solution)/shard_map/all_to_all | solution.py:201
  110.2 16.9 %all-to-all-start.4 = ((f32[64,8,128]{2,1,0:T(8,128)}), f32[64,8,128]{2,1,0:T(8,128)S(1)}, u32[]{:S(2)}, u32[]{:S(2)}) async-start(f32[64,8,128]{2,1,0:T(8,128)} %broadcast_in_dim.44), calls=%async_computation.4 | async-start | bytes 524288 | tf_op jit(solution)/shard_map/all_to_all | solution.py:103
  122.2 3.1 %collective-permute-start.5 = (f32[16,256]{1,0:T(8,128)S(1)}, f32[16,256]{1,0:T(8,128)S(1)}, u32[]{:S(2)}, u32[]{:S(2)}) collective-permute-start(f32[16,256]{1,0:T(8,128)S(1)} %get-tuple-element.27), channel_id=1, source_target_pairs={{0,32},{32,0},{1,33},{33,1},{2,34},{34,2},{3,35},{35,3},{4,36},{36... | collective-permute-start | bytes 49160 | tf_op jit(solution)/shard_map/ppermute | solution.py:206
